TPU v7x, 512 devices: a whole 4x8x8 slice. The times are simulated.
512 devices in a mesh: ctx: 32 (over z, y_hi, core), head: 16 (over x, y_lo).
Axes of the slice: x: 4, y: 8 (y_hi: 2, y_lo: 4; y = y_hi * 4 + y_lo), z: 8, core: 2. Of those that a mesh axis runs over, the one named last changes fastest.
Arguments:
- features: bfloat16 [16384, 5376], P('ctx', 'head'), may hold values from -30 to 30
- query_weight: bfloat16 [5376, 4096], P('ctx', 'head'), as said below
- key_weight: bfloat16 [5376, 2048], P('ctx', 'head'), as said below
- value_weight: bfloat16 [5376, 2048], P('ctx', 'head'), may hold values from -0.078125 to 0.078125
- doc_lengths: int32 [8], replicated, may hold values from 1 to 8192, 16384 in all
- out_grad: bfloat16 [16384, 4096], P('ctx', 'head'), may hold values from -6 to 6
Outputs:
- attention: bfloat16 [16384, 4096], P('ctx', 'head')
- key_weight_grad: bfloat16 [5376, 2048], P('ctx', 'head')
- value_weight_grad: bfloat16 [5376, 2048], P('ctx', 'head')
Inputs may be any that keep to these rules, and one draw needn't show every extreme that they name: `doc_lengths`: the lengths sum to 16384; the longest document holds half of them. `query_weight`: projection entries. `key_weight`: projection entries.
All inputs are finite; a program needn't handle non-finite values.
Results may differ from a plain program's by a relative error of at most 0.029.
Values may be sent and summed in bfloat16 or wider, within the bound.
No kernel may reach another device: no remote copies, remote signals or barrier semaphores. Data moves between devices by JAX's collectives and lax.ppermute only.
A program may use at most 64 MiB of HBM per device.

v0:
```python
import functools

import jax
import jax.numpy as jnp
from jax import lax
from jax.experimental import pallas as pl
from jax.experimental.pallas import tpu as pltpu
from jax.sharding import Mesh
from jax.sharding import PartitionSpec as P


HEADS_Q = 32
HEAD_DIM = 128
WINDOW = 1024
SPAN = 2
CORES = 2
CTX = ("z", "far", "core")
HEAD = ("x", "y")
ROPE_BASE = 10000.0


def cycled(value, axis, step):
    count = lax.axis_size(axis)
    return lax.ppermute(value, axis, [(i, (i + step) % count) for i in range(count)])


def passed_along(block, distance):
    devices = range(lax.axis_size(CTX))
    route = [(i - distance, i) for i in devices if i - distance in devices]
    return lax.ppermute(block, CTX, route)


def rope_tables(offsets):
    middle = HEAD_DIM // 2
    inverse = ROPE_BASE ** (-(jnp.arange(middle).astype(jnp.float32) * 2.0 / HEAD_DIM))
    angles = offsets.astype(jnp.float32)[:, None] * inverse[None, :]
    cosine = jnp.cos(angles)
    sine = jnp.sin(angles)
    return (
        jnp.concatenate([cosine, cosine], axis=-1),
        jnp.concatenate([-sine, sine], axis=-1),
    )


def start_of(positions, starts):
    candidates = jnp.where(starts[None, :] <= positions[:, None], starts[None, :], -1)
    return jnp.max(candidates, axis=1)


def spread_features(own):
    arrays, pieces = [], []

    def add(array, entries):
        for at, (x_step, y_step, half) in enumerate(entries):
            pieces.append((len(arrays), at, x_step, y_step, half))
        arrays.append(array)

    def across(batch, y_steps, x_steps):
        halves = [(y_step, half) for y_step in y_steps for half in range(2)]
        add(batch, [(0, *entry) for entry in halves])
        for x_step in x_steps:
            moved = cycled(batch, "x", -x_step)
            add(moved, [(x_step, *entry) for entry in halves])

    above = cycled(own, "y", 1)
    below = cycled(own, "y", -1)
    across(own, (0,), (1, 3, 2))
    sides = jnp.concatenate([above, below])
    across(sides, (3, 1), (1, 3, 2))
    own, sides = lax.optimization_barrier((own, sides))
    opposite = cycled(own, "y", 2)
    across(opposite, (2,), (1, 3, 2))
    return arrays, pieces, sides


CONTRACT_ROWS = (((0,), (0,)), ((), ()))
CONTRACT_COLS = (((1,), (1,)), ((), ()))
BLOCK = 256


def turned(values, cosine, sine_signed):
    return values * cosine + pltpu.roll(values, HEAD_DIM // 2, 1) * sine_signed


def unturned(values, cosine, sine_signed):
    return values * cosine - pltpu.roll(values, HEAD_DIM // 2, 1) * sine_signed


def accumulated(pieces, columns, place_ref, weights_ref, arrays, total):
    first, last = columns
    for number, (array, at, x_step, y_step, half) in enumerate(pieces):
        place = place_ref[x_step * 4 + y_step]
        weight = weights_ref[(place // 2) * CORES + half, place % 2, :, first:last]
        term = lax.dot_general(
            arrays[array][at], weight, CONTRACT_ROWS, preferred_element_type=jnp.float32
        )
        total[...] = term if number == 0 else total[...] + term


def key_value_kernel(pieces, columns, place_ref, weights_ref, cos_ref, sin_ref, *refs):
    *arrays, out_ref, total = refs
    accumulated(pieces, columns, place_ref, weights_ref, arrays, total)
    keys = turned(total[:, :HEAD_DIM], cos_ref[...], sin_ref[...])
    out_ref[0] = keys.astype(jnp.bfloat16)
    out_ref[1] = total[:, HEAD_DIM:].astype(jnp.bfloat16)


def query_kernel(pieces, columns, place_ref, weights_ref, cos_ref, sin_ref, *refs, scale):
    *arrays, out_ref, total = refs
    accumulated(pieces, columns, place_ref, weights_ref, arrays, total)
    for head in range((columns[1] - columns[0]) // HEAD_DIM):
        part = total[:, head * HEAD_DIM : (head + 1) * HEAD_DIM]
        queries = turned(part, cos_ref[...], sin_ref[...]) * scale
        out_ref[:, head * HEAD_DIM : (head + 1) * HEAD_DIM] = queries.astype(jnp.bfloat16)


def attention_kernel(low_ref, q_ref, far_ref, near_ref, own_ref, grad_ref, att_ref, *refs):
    far_out, near_out, own_out, keys, values, acc = refs
    tokens, width = q_ref.shape
    for number, ref in enumerate((far_ref, near_ref, own_ref)):
        keys[number * tokens : (number + 1) * tokens] = ref[0]
        values[number * tokens : (number + 1) * tokens] = ref[1]
    acc[...] = jnp.zeros_like(acc)
    span = 2 * tokens + BLOCK
    heads = width // HEAD_DIM
    for head in range(heads):
        cols = slice(head * HEAD_DIM, (head + 1) * HEAD_DIM)
        for at in range(0, tokens, BLOCK):
            rows = slice(at, at + BLOCK)
            window = slice(at, at + span)
            low = low_ref[:, rows]
            key_at = lax.broadcasted_iota(jnp.int32, (span, BLOCK), 0) + at
            query_at = lax.broadcasted_iota(jnp.int32, (span, BLOCK), 1) + (2 * tokens + at)
            allowed = (key_at >= low) & (key_at <= query_at)
            query = q_ref[rows, cols]
            grad = grad_ref[rows, cols]
            scores = lax.dot_general(
                keys[window], query, CONTRACT_COLS, preferred_element_type=jnp.float32
            )
            scores = jnp.where(allowed, scores, -jnp.inf)
            raw = jnp.exp(scores - jnp.max(scores, axis=0, keepdims=True))
            probs = raw * (1.0 / jnp.sum(raw, axis=0, keepdims=True))
            low_probs = probs.astype(jnp.bfloat16)
            attended = lax.dot_general(
                values[window], low_probs, CONTRACT_ROWS, preferred_element_type=jnp.float32
            )
            attended = attended.T.astype(jnp.bfloat16)
            att_ref[rows, cols] = attended
            product = grad.astype(jnp.float32) * attended.astype(jnp.float32)
            out_dot = jnp.sum(product.T, axis=0, keepdims=True)
            acc[1, window] += jnp.dot(low_probs, grad, preferred_element_type=jnp.float32)
            prob_grad = lax.dot_general(
                values[window], grad, CONTRACT_COLS, preferred_element_type=jnp.float32
            )
            score_grad = (probs * (prob_grad - out_dot)).astype(jnp.bfloat16)
            acc[0, window] += jnp.dot(score_grad, query, preferred_element_type=jnp.float32)
    far_out[...] = acc[:, :tokens].astype(jnp.bfloat16)
    near_out[...] = acc[:, tokens : 2 * tokens].astype(jnp.bfloat16)
    own_out[...] = acc[:, 2 * tokens :]


def attention_call(low, queries, far, near, own, grads):
    tokens, width = queries.shape
    vmem = pl.BlockSpec(memory_space=pltpu.VMEM)
    block = jax.ShapeDtypeStruct(own.shape, jnp.bfloat16)
    pairs = tokens * (2 * tokens + BLOCK) * (width // HEAD_DIM)
    return pl.pallas_call(
        attention_kernel,
        out_shape=(
            jax.ShapeDtypeStruct((tokens, width), jnp.bfloat16),
            block,
            block,
            jax.ShapeDtypeStruct(own.shape, jnp.float32),
        ),
        in_specs=[vmem] * 6,
        out_specs=(vmem,) * 4,
        scratch_shapes=[
            pltpu.VMEM((3 * tokens, HEAD_DIM), jnp.bfloat16),
            pltpu.VMEM((3 * tokens, HEAD_DIM), jnp.bfloat16),
            pltpu.VMEM((2, 3 * tokens, HEAD_DIM), jnp.float32),
        ],
        compiler_params=pltpu.CompilerParams(vmem_limit_bytes=10 << 20),
        cost_estimate=pl.CostEstimate(
            flops=10 * pairs * HEAD_DIM,
            bytes_accessed=4 * tokens * width * 4,
            transcendentals=pairs,
        ),
        name="attention",
    )(low, queries, far, near, own, grads)


def project(kernel, out_shape, arrays, pieces, columns, place, weights, tables):
    tokens = arrays[0].shape[2]
    width = columns[1] - columns[0]
    depth = len(pieces) * arrays[0].shape[1]
    vmem = pl.BlockSpec(memory_space=pltpu.VMEM)
    return pl.pallas_call(
        functools.partial(kernel, pieces, columns),
        out_shape=out_shape,
        in_specs=[pl.BlockSpec(memory_space=pltpu.SMEM)] + [vmem] * (3 + len(arrays)),
        out_specs=vmem,
        scratch_shapes=[pltpu.VMEM((tokens, width), jnp.float32)],
        compiler_params=pltpu.CompilerParams(vmem_limit_bytes=10 << 20),
        cost_estimate=pl.CostEstimate(
            flops=2 * tokens * depth * width,
            bytes_accessed=2 * depth * (tokens + width) + 4 * tokens * width,
            transcendentals=0,
        ),
        name="project",
    )(place, weights, *tables, *arrays)


def weight_grad_kernel(
    pieces, partner, place_ref, own_ref, near_ref, far_ref, cos_ref, sin_ref, *refs
):
    *arrays, out_ref, grads = refs
    core = place_ref[16]
    wanted = 1 - core if partner else core
    sums = [
        own_ref[i] + near_ref[i].astype(jnp.float32) + far_ref[i].astype(jnp.float32)
        for i in range(2)
    ]
    grads[:, :HEAD_DIM] = unturned(sums[0], cos_ref[...], sin_ref[...]).astype(jnp.bfloat16)
    grads[:, HEAD_DIM:] = sums[1].astype(jnp.bfloat16)
    for array, at, x_step, y_step, half in pieces:
        if half == 0:
            term = jnp.dot(
                arrays[array][at + wanted], grads[...], preferred_element_type=jnp.float32
            )
            out_ref[place_ref[x_step * 4 + y_step]] = term.astype(jnp.bfloat16)


def weight_grad(arrays, pieces, place, own, near, far, tables, partner):
    rows, tokens = arrays[0].shape[1:]
    width = 2 * HEAD_DIM
    vmem = pl.BlockSpec(memory_space=pltpu.VMEM)
    depth = len(pieces) * rows // 2
    return pl.pallas_call(
        functools.partial(weight_grad_kernel, pieces, partner),
        out_shape=jax.ShapeDtypeStruct((16, rows, width), jnp.bfloat16),
        in_specs=[pl.BlockSpec(memory_space=pltpu.SMEM)] + [vmem] * (5 + len(arrays)),
        out_specs=vmem,
        scratch_shapes=[pltpu.VMEM((tokens, width), jnp.bfloat16)],
        compiler_params=pltpu.CompilerParams(vmem_limit_bytes=10 << 20),
        cost_estimate=pl.CostEstimate(
            flops=2 * tokens * depth * width,
            bytes_accessed=2 * depth * (tokens + width) + 2 * tokens * width,
            transcendentals=0,
        ),
        name="weight_grad",
    )(place, own, near, far, *tables, *arrays)


def scattered_sum(kept, sent):
    chip = kept.astype(jnp.float32) + cycled(sent, "core", 1).astype(jnp.float32)
    chip = chip.astype(jnp.bfloat16)
    landed = lax.all_to_all(chip, ("z", "far"), 0, 0, tiled=True)
    return jnp.sum(landed.astype(jnp.float32), axis=0)


def spread_weights(query_weight, key_weight, value_weight):
    own = jnp.concatenate([query_weight, key_weight, value_weight], axis=1)
    other = cycled(own, "far", 1)
    far = lax.axis_index("far")
    both = jnp.where(far == 0, jnp.stack([own, other]), jnp.stack([other, own]))
    return lax.all_gather(both, ("z", "core"), axis=0, tiled=False)


def shards(features, query_weight, key_weight, value_weight, doc_lengths, out_grad):
    tok_rows, slab_rows = features.shape
    query_cols = query_weight.shape[1]
    value_cols = key_weight.shape[1]
    query_scale = (slab_rows * 16 / HEADS_Q) ** (-0.5)
    ctx_index = lax.axis_index(CTX)

    arrays, pieces, _ = spread_features(features.T.reshape(2, slab_rows // 2, tok_rows))
    weights = spread_weights(query_weight, key_weight, value_weight)
    step = jnp.arange(4, dtype=jnp.int32)
    x_at, y_at = lax.axis_index("x"), lax.axis_index("y")
    place = ((x_at + step) % 4)[:, None] * 4 + ((y_at + step) % 4)[None, :]
    place = jnp.concatenate([place.reshape(16), jnp.stack([lax.axis_index("core"), y_at])])
    place = place.astype(jnp.int32)

    starts = jnp.cumsum(doc_lengths) - doc_lengths
    query_index = ctx_index * tok_rows + jnp.arange(tok_rows, dtype=jnp.int32)
    query_start = start_of(query_index, starts)
    tables = rope_tables(query_index - query_start)
    low = jnp.maximum(query_start, query_index - (WINDOW - 1)) - (ctx_index - SPAN) * tok_rows
    low = low.astype(jnp.int32)[None]

    key_value = project(
        key_value_kernel,
        jax.ShapeDtypeStruct((2, tok_rows, HEAD_DIM), jnp.bfloat16),
        arrays,
        pieces,
        (query_cols, query_cols + 2 * value_cols),
        place,
        weights,
        tables,
    )
    far, near = passed_along(key_value, 2), passed_along(key_value, 1)
    queries = project(
        functools.partial(query_kernel, scale=query_scale),
        jax.ShapeDtypeStruct((tok_rows, query_cols), jnp.bfloat16),
        arrays,
        pieces,
        (0, query_cols),
        place,
        weights,
        tables,
    )
    attention, far_part, near_part, own_part = attention_call(
        low, queries, far, near, key_value, out_grad
    )
    far_back, near_back = passed_along(far_part, -2), passed_along(near_part, -1)
    sent, kept = (
        weight_grad(arrays, pieces, place, own_part, near_back, far_back, tables, partner)
        for partner in (True, False)
    )
    weight_grads = scattered_sum(kept, sent).astype(jnp.bfloat16)
    return attention, weight_grads[:, :value_cols], weight_grads[:, value_cols:]


def solution(mesh):
    sizes = (mesh.shape["ctx"] // 4, 2, 2, 4, 4)
    torus = Mesh(mesh.devices.reshape(sizes), CTX + HEAD)
    placed = (P(CTX, HEAD), P(CTX, HEAD), P(CTX, HEAD), P(CTX, HEAD), P(), P(CTX, HEAD))
    return jax.shard_map(
        shards,
        mesh=torus,
        in_specs=placed,
        out_specs=(P(CTX, HEAD), P(CTX, HEAD), P(CTX, HEAD)),
        check_vma=False,
    )
```

profile of v0, /device:TPU:56, one launch (start us, length us, event | category | flops | bytes accessed | tf_op | source)
XLA Modules:
  0.0 247.6 jit_solution(10512757669405818826)
XLA Ops:
  7.2 0.0 all-gather.2.cloned.1.call-start
  7.2 0.9 constant_dynamic-update-slice_fusion.2
  8.2 0.8 constant_dynamic-update-slice_fusion.1
  9.0 0.8 constant_dynamic-update-slice_fusion
  9.8 4.7 %collective-permute-start = (bf16[168,512]{1,0:T(8,128)(2,1)S(1)}, bf16[168,512]{1,0:T(8,128)(2,1)S(1)}, u32[]{:S(2)}, u32[]{:S(2)}) collective-permute-start(bf16[168,512]{1,0:T(8,128)(2,1)S(1)} %constant_dynamic-update-slice_fusion), channel_id=1, source_target_pairs={{0,32},{32,0},{1,33},{33,1},{2,34},{34,2},{3,35},{35,3},{4,36},{36... | collective-permute-start | bytes 516104 | tf_op jit(solution)/shard_map/ppermute | solution.py:24
  14.5 10.9 %collective-permute-done = bf16[168,512]{1,0:T(8,128)(2,1)S(1)} collective-permute-done((bf16[168,512]{1,0:T(8,128)(2,1)S(1)}, bf16[168,512]{1,0:T(8,128)(2,1)S(1)}, u32[]{:S(2)}, u32[]{:S(2)}) %collective-permute-start) | collective-permute-done | bytes 172064 | tf_op jit(solution)/shard_map/ppermute | solution.py:24
  25.4 0.8 maximum_select_fusion
  26.2 4.7 %collective-permute-start.1 = (bf16[2,168,512]{2,1,0:T(8,128)(2,1)S(1)}, bf16[2,168,512]{2,1,0:T(8,128)(2,1)S(1)}, u32[]{:S(2)}, u32[]{:S(2)}) collective-permute-start(bf16[2,168,512]{2,1,0:T(8,128)(2,1)S(1)} %bitcast.11), channel_id=1, source_target_pairs={{0,12},{4,0},{8,4},{12,8},{1,13},{5,1},{9,5},{13,9},{2,14},{6,2},{... | collective-permute-start | bytes 1032200 | tf_op jit(solution)/shard_map/ppermute | solution.py:24
  30.9 1.9 collective-permute-start.2
  32.8 4.2 %collective-permute-start.3 = (bf16[2,168,512]{2,1,0:T(8,128)(2,1)S(1)}, bf16[2,168,512]{2,1,0:T(8,128)(2,1)S(1)}, u32[]{:S(2)}, u32[]{:S(2)}) collective-permute-start(bf16[2,168,512]{2,1,0:T(8,128)(2,1)S(1)} %bitcast.13), channel_id=1, source_target_pairs={{0,8},{4,12},{8,0},{12,4},{1,9},{5,13},{9,1},{13,5},{2,10},{6,14},... | collective-permute-start | bytes 1032200 | tf_op jit(solution)/shard_map/ppermute | solution.py:24
  37.0 4.8 %collective-permute-start.4 = (bf16[2,168,512]{2,1,0:T(8,128)(2,1)S(1)}, bf16[2,168,512]{2,1,0:T(8,128)(2,1)S(1)}, u32[]{:S(2)}, u32[]{:S(2)}) collective-permute-start(bf16[2,168,512]{2,1,0:T(8,128)(2,1)S(1)} %bitcast.14), channel_id=1, source_target_pairs={{0,1},{1,2},{2,3},{3,0},{4,5},{5,6},{6,7},{7,4},{8,9},{9,10},{10,1... | collective-permute-start | bytes 1032200 | tf_op jit(solution)/shard_map/ppermute | solution.py:24
  41.8 1.9 collective-permute-start.5
  43.7 0.2 reduce-window.9
  43.9 0.1 select_reduce_fusion
  44.0 6.1 %collective-permute-done.4 = bf16[2,168,512]{2,1,0:T(8,128)(2,1)S(1)} collective-permute-done((bf16[2,168,512]{2,1,0:T(8,128)(2,1)S(1)}, bf16[2,168,512]{2,1,0:T(8,128)(2,1)S(1)}, u32[]{:S(2)}, u32[]{:S(2)}) %collective-permute-start.4) | collective-permute-done | bytes 344096 | tf_op jit(solution)/shard_map/ppermute | solution.py:24
  50.2 5.3 %collective-permute-done.5 = bf16[2,168,512]{2,1,0:T(8,128)(2,1)S(1)} collective-permute-done((bf16[2,168,512]{2,1,0:T(8,128)(2,1)S(1)}, bf16[2,168,512]{2,1,0:T(8,128)(2,1)S(1)}, u32[]{:S(2)}, u32[]{:S(2)}) %collective-permute-start.5) | collective-permute-done | bytes 344096 | tf_op jit(solution)/shard_map/ppermute | solution.py:24
  55.4 3.1 %collective-permute-start.6 = (bf16[4,168,512]{2,1,0:T(8,128)(2,1)S(1)}, bf16[4,168,512]{2,1,0:T(8,128)(2,1)S(1)}, u32[]{:S(2)}, u32[]{:S(2)}) collective-permute-start(bf16[4,168,512]{2,1,0:T(8,128)(2,1)S(1)} %constant_dynamic-update-slice_fusion.3.refs_4_), channel_id=1, source_target_pairs={{0,12},{4,0},{8,4},{12,8},{1,13},{5,1},{9,5},{13,9},{2,14},{6,2},{... | collective-permute-start | bytes 2064392 | tf_op jit(solution)/shard_map/ppermute | solution.py:24
  58.6 0.1 broadcast_add_fusion
  58.7 3.4 %collective-permute-start.9 = (bf16[2,168,512]{2,1,0:T(8,128)(2,1)S(1)}, bf16[2,168,512]{2,1,0:T(8,128)(2,1)}, u32[]{:S(2)}, u32[]{:S(2)}) collective-permute-start(bf16[2,168,512]{2,1,0:T(8,128)(2,1)S(1)} %bitcast.16), channel_id=1, source_target_pairs={{0,2},{1,3},{2,0},{3,1},{4,6},{5,7},{6,4},{7,5},{8,10},{9,11},{10,... | collective-permute-start | bytes 1032200 | tf_op jit(solution)/shard_map/ppermute | solution.py:24
  62.1 0.1 add.112
  62.2 0.7 copy-done.5
  62.9 2.1 collective-permute-start.7
  65.1 0.7 copy-done.8
  65.8 4.3 %collective-permute-start.8 = (bf16[4,168,512]{2,1,0:T(8,128)(2,1)S(1)}, bf16[4,168,512]{2,1,0:T(8,128)(2,1)S(1)}, u32[]{:S(2)}, u32[]{:S(2)}) collective-permute-start(bf16[4,168,512]{2,1,0:T(8,128)(2,1)S(1)} %constant_dynamic-update-slice_fusion.3.refs_4_), channel_id=1, source_target_pairs={{0,8},{4,12},{8,0},{12,4},{1,9},{5,13},{9,1},{13,5},{2,10},{6,14},... | collective-permute-start | bytes 2064392 | tf_op jit(solution)/shard_map/ppermute | solution.py:24
  70.1 0.1 pad_add_fusion.place_ref
  70.1 6.9 %collective-permute-done.9.refs_8_ = bf16[2,168,512]{2,1,0:T(8,128)(2,1)} collective-permute-done((bf16[2,168,512]{2,1,0:T(8,128)(2,1)S(1)}, bf16[2,168,512]{2,1,0:T(8,128)(2,1)}, u32[]{:S(2)}, u32[]{:S(2)}) %collective-permute-start.9) | collective-permute-done | bytes 344096 | tf_op jit(solution)/shard_map/ppermute | solution.py:24
  77.1 3.5 %collective-permute-start.10 = (bf16[2,168,512]{2,1,0:T(8,128)(2,1)}, bf16[2,168,512]{2,1,0:T(8,128)(2,1)S(1)}, u32[]{:S(2)}, u32[]{:S(2)}) collective-permute-start(bf16[2,168,512]{2,1,0:T(8,128)(2,1)} %collective-permute-done.9.refs_8_), channel_id=1, source_target_pairs={{0,12},{4,0},{8,4},{12,8},{1,13},{5,1},{9,5},{13,9},{2,14},{6,2},{... | collective-permute-start | bytes 1032200 | tf_op jit(solution)/shard_map/ppermute | solution.py:24
  80.6 2.4 collective-permute-start.11
  83.0 6.6 %collective-permute-start.12 = (bf16[2,168,512]{2,1,0:T(8,128)(2,1)}, bf16[2,168,512]{2,1,0:T(8,128)(2,1)S(1)}, u32[]{:S(2)}, u32[]{:S(2)}) collective-permute-start(bf16[2,168,512]{2,1,0:T(8,128)(2,1)} %collective-permute-done.9.refs_8_), channel_id=1, source_target_pairs={{0,8},{4,12},{8,0},{12,4},{1,9},{5,13},{9,1},{13,5},{2,10},{6,14},... | collective-permute-start | bytes 1032200 | tf_op jit(solution)/shard_map/ppermute | solution.py:24
  89.5 1.0 fusion
  90.5 0.2 pad_maximum_fusion
  90.8 5.2 %collective-permute-done.7.refs_6_ = bf16[4,168,512]{2,1,0:T(8,128)(2,1)S(1)} collective-permute-done((bf16[4,168,512]{2,1,0:T(8,128)(2,1)S(1)}, bf16[4,168,512]{2,1,0:T(8,128)(2,1)S(1)}, u32[]{:S(2)}, u32[]{:S(2)}) %collective-permute-start.7) | collective-permute-done | bytes 688160 | tf_op jit(solution)/shard_map/ppermute | solution.py:24
  96.0 2.5 %collective-permute-done.8.refs_7_ = bf16[4,168,512]{2,1,0:T(8,128)(2,1)S(1)} collective-permute-done((bf16[4,168,512]{2,1,0:T(8,128)(2,1)S(1)}, bf16[4,168,512]{2,1,0:T(8,128)(2,1)S(1)}, u32[]{:S(2)}, u32[]{:S(2)}) %collective-permute-start.8) | collective-permute-done | bytes 688160 | tf_op jit(solution)/shard_map/ppermute | solution.py:24
  98.5 0.7 copy-done.14
  99.2 12.7 %collective-permute-done.11.refs_10_ = bf16[2,168,512]{2,1,0:T(8,128)(2,1)S(1)} collective-permute-done((bf16[2,168,512]{2,1,0:T(8,128)(2,1)}, bf16[2,168,512]{2,1,0:T(8,128)(2,1)S(1)}, u32[]{:S(2)}, u32[]{:S(2)}) %collective-permute-start.11) | collective-permute-done | bytes 344096 | tf_op jit(solution)/shard_map/ppermute | solution.py:24
  111.9 0.8 copy-done.16
  112.7 0.8 copy-done.18
  113.5 2.6 %copy-done = bf16[16,2,168,512]{3,2,1,0:T(8,128)(2,1)S(1)} copy-done((bf16[16,2,168,512]{3,2,1,0:T(8,128)(2,1)S(1)}, bf16[16,2,168,512]{3,2,1,0:T(8,128)(2,1)}, u32[]{:S(2)}) %copy-start) | copy-done | bytes 5505048
  116.0 1.0 copy-done.3
  117.0 1.0 copy-done.6
  118.0 1.0 copy-done.9
  119.0 1.0 copy-done.12
  119.9 1.0 copy-done.15
  120.9 1.0 copy-done.17
  121.9 1.0 copy-done.19
  122.9 3.6 %project.3.own_ref = bf16[2,512,128]{2,1,0:T(8,128)(2,1)S(1)} custom-call(s32[18]{0:T(128)S(1)} %pad_add_fusion.place_ref, bf16[16,2,168,512]{3,2,1,0:T(8,128)(2,1)S(1)} %copy-done, f32[512,128]{1,0:T(8,128)S(1)} %get-tuple-element.20.cos_ref, f32[512,128]{1,0:T(8,128)S(1)} %get-tuple-element.21.sin_ref, bf16[2,168,512]{2,1,0:T(8,128)(2,1)S(1)} %bitcast.17, ...), custom_call_target="tpu_custom_call" | custom-call | flops 1409286144 | bytes 8781824 | tf_op jit(solution)/shard_map/project/pallas_call | solution.py:197
  126.5 3.3 %collective-permute-start.13 = (bf16[2,512,128]{2,1,0:T(8,128)(2,1)S(1)}, bf16[2,512,128]{2,1,0:T(8,128)(2,1)S(1)}, u32[]{:S(2)}, u32[]{:S(2)}) collective-permute-start(bf16[2,512,128]{2,1,0:T(8,128)(2,1)S(1)} %project.3.own_ref), channel_id=1, source_target_pairs={{0,32},{16,48},{32,64},{48,80},{64,96},{80,112},{96,128},{112,144}... | collective-permute-start | bytes 786440 | tf_op jit(solution)/shard_map/ppermute | solution.py:30
  129.8 2.1 collective-permute-start.14
  132.0 3.5 %project.2.q_ref = bf16[512,256]{1,0:T(8,128)(2,1)S(1)} custom-call(s32[18]{0:T(128)S(1)} %pad_add_fusion.place_ref, bf16[16,2,168,512]{3,2,1,0:T(8,128)(2,1)S(1)} %copy-done.1, f32[512,128]{1,0:T(8,128)S(1)} %get-tuple-element.20.cos_ref, f32[512,128]{1,0:T(8,128)S(1)} %get-tuple-element.21.sin_ref, bf16[2,168,512]{2,1,0:T(8,128)(2,1)S(1)} %bitcast.18, ...), custom_call_target="tpu_custom_call" | custom-call | flops 1409286144 | bytes 8781824 | tf_op jit(solution)/shard_map/project/pallas_call | solution.py:197
  135.6 8.8 %collective-permute-done.13.far_ref = bf16[2,512,128]{2,1,0:T(8,128)(2,1)S(1)} collective-permute-done((bf16[2,512,128]{2,1,0:T(8,128)(2,1)S(1)}, bf16[2,512,128]{2,1,0:T(8,128)(2,1)S(1)}, u32[]{:S(2)}, u32[]{:S(2)}) %collective-permute-start.13) | collective-permute-done | bytes 262176 | tf_op jit(solution)/shard_map/ppermute | solution.py:30
  144.4 0.7 collective-permute-done.14.near_ref
  145.1 5.7 %attention.1 = (bf16[512,256]{1,0:T(8,128)(2,1)}, bf16[2,512,128]{2,1,0:T(8,128)(2,1)S(1)}, bf16[2,512,128]{2,1,0:T(8,128)(2,1)S(1)}, f32[2,512,128]{2,1,0:T(8,128)S(1)}) custom-call(s32[1,512]{1,0:T(1,128)S(1)} %maximum_subtract_fusion.low_ref, bf16[512,256]{1,0:T(8,128)(2,1)S(1)} %project.2.q_ref, ...), custom_call_target="tpu_custom_call" | custom-call | flops 1677721600 | bytes 2097152 | tf_op jit(solution)/shard_map/attention/pallas_call | solution.py:167
  150.8 1.9 collective-permute-start.15
  152.7 1.9 collective-permute-start.16
  154.7 3.0 %collective-permute-done.15.near_ref = bf16[2,512,128]{2,1,0:T(8,128)(2,1)S(1)} collective-permute-done((bf16[2,512,128]{2,1,0:T(8,128)(2,1)S(1)}, bf16[2,512,128]{2,1,0:T(8,128)(2,1)S(1)}, u32[]{:S(2)}, u32[]{:S(2)}) %collective-permute-start.15) | collective-permute-done | bytes 262176 | tf_op jit(solution)/shard_map/ppermute | solution.py:30
  157.7 15.7 %collective-permute-done.16.far_ref = bf16[2,512,128]{2,1,0:T(8,128)(2,1)S(1)} collective-permute-done((bf16[2,512,128]{2,1,0:T(8,128)(2,1)S(1)}, bf16[2,512,128]{2,1,0:T(8,128)(2,1)S(1)}, u32[]{:S(2)}, u32[]{:S(2)}) %collective-permute-start.16) | collective-permute-done | bytes 262176 | tf_op jit(solution)/shard_map/ppermute | solution.py:30
  173.4 2.0 weight_grad.3
  175.5 1.9 collective-permute-start.17
  177.4 2.0 weight_grad.2
  179.4 1.1 collective-permute-done.17
  180.5 0.4 add_convert_fusion
  180.9 59.0 %all_to_all.5 = bf16[16,168,256]{2,1,0:T(8,128)(2,1)S(1)} all-to-all(bf16[16,168,256]{2,1,0:T(8,128)(2,1)S(1)} %add_convert_fusion), channel_id=1, replica_groups=mesh['z'=8,'far'=2,'core'=2,'x'=4,'y'=4] {'z','far'}, dimensions={0} | all-to-all | bytes 2752512 | tf_op jit(solution)/shard_map/all_to_all | solution.py:257
  239.9 0.2 reduce_sum.12
  240.1 0.6 fusion.4
  (47 shorter events, 0.2 us)
Async XLA Ops:
  7.2 19.0 %copy-start.2 = (bf16[512,336]{0,1:T(8,128)(2,1)S(1)}, bf16[512,336]{0,1:T(8,128)(2,1)}, u32[]{:S(2)}) copy-start(bf16[512,336]{0,1:T(8,128)(2,1)} %param.6) | copy-start | bytes 1032196
  7.2 36.5 %copy-start.21 = (s32[8]{0:T(128)S(1)}, s32[8]{0:T(128)}, u32[]{:S(2)}) copy-start(s32[8]{0:T(128)} %param.10) | copy-start | bytes 100
  7.2 106.3 %all-gather.2.cloned.1.call-start = ((), (), s32[]{:S(2)}) async-start(), calls=%async_computation.1 | async-start | bytes 5849088 | tf_op jit(solution)/shard_map/all_gather | solution.py:266
  9.8 15.6 %collective-permute-start = (bf16[168,512]{1,0:T(8,128)(2,1)S(1)}, bf16[168,512]{1,0:T(8,128)(2,1)S(1)}, u32[]{:S(2)}, u32[]{:S(2)}) collective-permute-start(bf16[168,512]{1,0:T(8,128)(2,1)S(1)} %constant_dynamic-update-slice_fusion), channel_id=1, source_target_pairs={{0,32},{32,0},{1,33},{33,1},{2,34},{34,2},{3,35},{35,3},{4,36},{36... | collective-permute-start | bytes 516104 | tf_op jit(solution)/shard_map/ppermute | solution.py:24
  26.2 36.0 %collective-permute-start.1 = (bf16[2,168,512]{2,1,0:T(8,128)(2,1)S(1)}, bf16[2,168,512]{2,1,0:T(8,128)(2,1)S(1)}, u32[]{:S(2)}, u32[]{:S(2)}) collective-permute-start(bf16[2,168,512]{2,1,0:T(8,128)(2,1)S(1)} %bitcast.11), channel_id=1, source_target_pairs={{0,12},{4,0},{8,4},{12,8},{1,13},{5,1},{9,5},{13,9},{2,14},{6,2},{... | collective-permute-start | bytes 1032200 | tf_op jit(solution)/shard_map/ppermute | solution.py:24
  30.9 34.2 %collective-permute-start.2 = (bf16[2,168,512]{2,1,0:T(8,128)(2,1)S(1)}, bf16[2,168,512]{2,1,0:T(8,128)(2,1)S(1)}, u32[]{:S(2)}, u32[]{:S(2)}) collective-permute-start(bf16[2,168,512]{2,1,0:T(8,128)(2,1)S(1)} %bitcast.12), channel_id=1, source_target_pairs={{0,4},{4,8},{8,12},{12,0},{1,5},{5,9},{9,13},{13,1},{2,6},{6,10},{... | collective-permute-start | bytes 1032200 | tf_op jit(solution)/shard_map/ppermute | solution.py:24
  32.8 47.8 %collective-permute-start.3 = (bf16[2,168,512]{2,1,0:T(8,128)(2,1)S(1)}, bf16[2,168,512]{2,1,0:T(8,128)(2,1)S(1)}, u32[]{:S(2)}, u32[]{:S(2)}) collective-permute-start(bf16[2,168,512]{2,1,0:T(8,128)(2,1)S(1)} %bitcast.13), channel_id=1, source_target_pairs={{0,8},{4,12},{8,0},{12,4},{1,9},{5,13},{9,1},{13,5},{2,10},{6,14},... | collective-permute-start | bytes 1032200 | tf_op jit(solution)/shard_map/ppermute | solution.py:24
  37.0 13.1 %collective-permute-start.4 = (bf16[2,168,512]{2,1,0:T(8,128)(2,1)S(1)}, bf16[2,168,512]{2,1,0:T(8,128)(2,1)S(1)}, u32[]{:S(2)}, u32[]{:S(2)}) collective-permute-start(bf16[2,168,512]{2,1,0:T(8,128)(2,1)S(1)} %bitcast.14), channel_id=1, source_target_pairs={{0,1},{1,2},{2,3},{3,0},{4,5},{5,6},{6,7},{7,4},{8,9},{9,10},{10,1... | collective-permute-start | bytes 1032200 | tf_op jit(solution)/shard_map/ppermute | solution.py:24
  41.8 13.6 %collective-permute-start.5 = (bf16[2,168,512]{2,1,0:T(8,128)(2,1)S(1)}, bf16[2,168,512]{2,1,0:T(8,128)(2,1)S(1)}, u32[]{:S(2)}, u32[]{:S(2)}) collective-permute-start(bf16[2,168,512]{2,1,0:T(8,128)(2,1)S(1)} %bitcast.15), channel_id=1, source_target_pairs={{0,3},{1,0},{2,1},{3,2},{4,7},{5,4},{6,5},{7,6},{8,11},{9,8},{10,9... | collective-permute-start | bytes 1032200 | tf_op jit(solution)/shard_map/ppermute | solution.py:24
  55.4 27.5 %collective-permute-start.6 = (bf16[4,168,512]{2,1,0:T(8,128)(2,1)S(1)}, bf16[4,168,512]{2,1,0:T(8,128)(2,1)S(1)}, u32[]{:S(2)}, u32[]{:S(2)}) collective-permute-start(bf16[4,168,512]{2,1,0:T(8,128)(2,1)S(1)} %constant_dynamic-update-slice_fusion.3.refs_4_), channel_id=1, source_target_pairs={{0,12},{4,0},{8,4},{12,8},{1,13},{5,1},{9,5},{13,9},{2,14},{6,2},{... | collective-permute-start | bytes 2064392 | tf_op jit(solution)/shard_map/ppermute | solution.py:24
  58.7 18.4 %collective-permute-start.9 = (bf16[2,168,512]{2,1,0:T(8,128)(2,1)S(1)}, bf16[2,168,512]{2,1,0:T(8,128)(2,1)}, u32[]{:S(2)}, u32[]{:S(2)}) collective-permute-start(bf16[2,168,512]{2,1,0:T(8,128)(2,1)S(1)} %bitcast.16), channel_id=1, source_target_pairs={{0,2},{1,3},{2,0},{3,1},{4,6},{5,7},{6,4},{7,5},{8,10},{9,11},{10,... | collective-permute-start | bytes 1032200 | tf_op jit(solution)/shard_map/ppermute | solution.py:24
  62.2 0.7 copy-start.5
  62.9 33.1 %collective-permute-start.7 = (bf16[4,168,512]{2,1,0:T(8,128)(2,1)S(1)}, bf16[4,168,512]{2,1,0:T(8,128)(2,1)S(1)}, u32[]{:S(2)}, u32[]{:S(2)}) collective-permute-start(bf16[4,168,512]{2,1,0:T(8,128)(2,1)S(1)} %constant_dynamic-update-slice_fusion.3.refs_4_), channel_id=1, source_target_pairs={{0,4},{4,8},{8,12},{12,0},{1,5},{5,9},{9,13},{13,1},{2,6},{6,10},{... | collective-permute-start | bytes 2064392 | tf_op jit(solution)/shard_map/ppermute | solution.py:24
  65.1 0.7 copy-start.8
  65.8 32.7 %collective-permute-start.8 = (bf16[4,168,512]{2,1,0:T(8,128)(2,1)S(1)}, bf16[4,168,512]{2,1,0:T(8,128)(2,1)S(1)}, u32[]{:S(2)}, u32[]{:S(2)}) collective-permute-start(bf16[4,168,512]{2,1,0:T(8,128)(2,1)S(1)} %constant_dynamic-update-slice_fusion.3.refs_4_), channel_id=1, source_target_pairs={{0,8},{4,12},{8,0},{12,4},{1,9},{5,13},{9,1},{13,5},{2,10},{6,14},... | collective-permute-start | bytes 2064392 | tf_op jit(solution)/shard_map/ppermute | solution.py:24
  77.1 21.4 %collective-permute-start.10 = (bf16[2,168,512]{2,1,0:T(8,128)(2,1)}, bf16[2,168,512]{2,1,0:T(8,128)(2,1)S(1)}, u32[]{:S(2)}, u32[]{:S(2)}) collective-permute-start(bf16[2,168,512]{2,1,0:T(8,128)(2,1)} %collective-permute-done.9.refs_8_), channel_id=1, source_target_pairs={{0,12},{4,0},{8,4},{12,8},{1,13},{5,1},{9,5},{13,9},{2,14},{6,2},{... | collective-permute-start | bytes 1032200 | tf_op jit(solution)/shard_map/ppermute | solution.py:24
  80.6 9.9 %copy-start.11 = (bf16[2,168,512]{2,1,0:T(8,128)(2,1)}, bf16[2,168,512]{2,1,0:T(8,128)(2,1)S(1)}, u32[]{:S(2)}) copy-start(bf16[2,168,512]{2,1,0:T(8,128)(2,1)S(1)} %collective-permute-done.3.refs_3_) | copy-start | bytes 1032196
  80.6 31.3 %collective-permute-start.11 = (bf16[2,168,512]{2,1,0:T(8,128)(2,1)}, bf16[2,168,512]{2,1,0:T(8,128)(2,1)S(1)}, u32[]{:S(2)}, u32[]{:S(2)}) collective-permute-start(bf16[2,168,512]{2,1,0:T(8,128)(2,1)} %collective-permute-done.9.refs_8_), channel_id=1, source_target_pairs={{0,4},{4,8},{8,12},{12,0},{1,5},{5,9},{9,13},{13,1},{2,6},{6,10},{... | collective-permute-start | bytes 1032200 | tf_op jit(solution)/shard_map/ppermute | solution.py:24
  83.0 29.7 %collective-permute-start.12 = (bf16[2,168,512]{2,1,0:T(8,128)(2,1)}, bf16[2,168,512]{2,1,0:T(8,128)(2,1)S(1)}, u32[]{:S(2)}, u32[]{:S(2)}) collective-permute-start(bf16[2,168,512]{2,1,0:T(8,128)(2,1)} %collective-permute-done.9.refs_8_), channel_id=1, source_target_pairs={{0,8},{4,12},{8,0},{12,4},{1,9},{5,13},{9,1},{13,5},{2,10},{6,14},... | collective-permute-start | bytes 1032200 | tf_op jit(solution)/shard_map/ppermute | solution.py:24
  98.5 0.7 copy-start.14
  111.9 0.8 copy-start.16
  112.7 0.8 copy-start.18
  113.5 2.6 %copy-start = (bf16[16,2,168,512]{3,2,1,0:T(8,128)(2,1)S(1)}, bf16[16,2,168,512]{3,2,1,0:T(8,128)(2,1)}, u32[]{:S(2)}) copy-start(bf16[16,2,168,512]{3,2,1,0:T(8,128)(2,1)} %all-gather.2.cloned.1.call-done.weights_ref) | copy-start | bytes 16515076
  116.0 1.0 copy-start.3
  117.0 1.0 copy-start.6
  118.0 1.0 copy-start.9
  119.0 1.0 copy-start.12
  119.9 1.0 copy-start.15
  120.9 1.0 copy-start.17
  121.9 1.0 copy-start.19
  122.9 9.1 %copy-start.1 = (bf16[16,2,168,512]{3,2,1,0:T(8,128)(2,1)S(1)}, bf16[16,2,168,512]{3,2,1,0:T(8,128)(2,1)}, u32[]{:S(2)}) copy-start(bf16[16,2,168,512]{3,2,1,0:T(8,128)(2,1)} %all-gather.2.cloned.1.call-done.weights_ref) | copy-start | bytes 16515076
  126.5 17.9 %collective-permute-start.13 = (bf16[2,512,128]{2,1,0:T(8,128)(2,1)S(1)}, bf16[2,512,128]{2,1,0:T(8,128)(2,1)S(1)}, u32[]{:S(2)}, u32[]{:S(2)}) collective-permute-start(bf16[2,512,128]{2,1,0:T(8,128)(2,1)S(1)} %project.3.own_ref), channel_id=1, source_target_pairs={{0,32},{16,48},{32,64},{48,80},{64,96},{80,112},{96,128},{112,144}... | collective-permute-start | bytes 786440 | tf_op jit(solution)/shard_map/ppermute | solution.py:30
  129.8 15.2 %collective-permute-start.14 = (bf16[2,512,128]{2,1,0:T(8,128)(2,1)S(1)}, bf16[2,512,128]{2,1,0:T(8,128)(2,1)S(1)}, u32[]{:S(2)}, u32[]{:S(2)}) collective-permute-start(bf16[2,512,128]{2,1,0:T(8,128)(2,1)S(1)} %project.3.own_ref), channel_id=1, source_target_pairs={{0,16},{16,32},{32,48},{48,64},{64,80},{80,96},{96,112},{112,128},... | collective-permute-start | bytes 786440 | tf_op jit(solution)/shard_map/ppermute | solution.py:30
  132.0 13.1 %copy-start.20 = (bf16[512,256]{1,0:T(8,128)(2,1)S(1)}, bf16[512,256]{1,0:T(8,128)(2,1)}, u32[]{:S(2)}) copy-start(bf16[512,256]{1,0:T(8,128)(2,1)} %grad_ref.1) | copy-start | bytes 786436
  135.5 37.9 %copy-start.4 = (bf16[512,336]{0,1:T(8,128)(2,1)S(1)}, bf16[512,336]{0,1:T(8,128)(2,1)}, u32[]{:S(2)}) copy-start(bf16[512,336]{0,1:T(8,128)(2,1)} %param.6) | copy-start | bytes 1032196
  135.6 37.9 %copy-start.7 = (bf16[2,168,512]{2,1,0:T(8,128)(2,1)S(1)}, bf16[2,168,512]{2,1,0:T(8,128)(2,1)}, u32[]{:S(2)}) copy-start(bf16[2,168,512]{2,1,0:T(8,128)(2,1)} %copy-done.5) | copy-start | bytes 1032196
  135.6 37.8 %copy-start.10 = (bf16[2,168,512]{2,1,0:T(8,128)(2,1)S(1)}, bf16[2,168,512]{2,1,0:T(8,128)(2,1)}, u32[]{:S(2)}) copy-start(bf16[2,168,512]{2,1,0:T(8,128)(2,1)} %copy-done.8) | copy-start | bytes 1032196
  135.6 37.8 %copy-start.13 = (bf16[2,168,512]{2,1,0:T(8,128)(2,1)S(1)}, bf16[2,168,512]{2,1,0:T(8,128)(2,1)}, u32[]{:S(2)}) copy-start(bf16[2,168,512]{2,1,0:T(8,128)(2,1)} %copy-done.11) | copy-start | bytes 1032196
  150.8 6.9 %collective-permute-start.15 = (bf16[2,512,128]{2,1,0:T(8,128)(2,1)S(1)}, bf16[2,512,128]{2,1,0:T(8,128)(2,1)S(1)}, u32[]{:S(2)}, u32[]{:S(2)}) collective-permute-start(bf16[2,512,128]{2,1,0:T(8,128)(2,1)S(1)} %get-tuple-element.11), channel_id=1, source_target_pairs={{16,0},{32,16},{48,32},{64,48},{80,64},{96,80},{112,96},{128,112},... | collective-permute-start | bytes 786440 | tf_op jit(solution)/shard_map/ppermute | solution.py:30
  152.7 20.7 %collective-permute-start.16 = (bf16[2,512,128]{2,1,0:T(8,128)(2,1)S(1)}, bf16[2,512,128]{2,1,0:T(8,128)(2,1)S(1)}, u32[]{:S(2)}, u32[]{:S(2)}) collective-permute-start(bf16[2,512,128]{2,1,0:T(8,128)(2,1)S(1)} %get-tuple-element.12), channel_id=1, source_target_pairs={{32,0},{48,16},{64,32},{80,48},{96,64},{112,80},{128,96},{144,112}... | collective-permute-start | bytes 786440 | tf_op jit(solution)/shard_map/ppermute | solution.py:30
  175.5 5.0 %collective-permute-start.17 = (bf16[16,168,256]{2,1,0:T(8,128)(2,1)S(1)}, bf16[16,168,256]{2,1,0:T(8,128)(2,1)S(1)}, u32[]{:S(2)}, u32[]{:S(2)}) collective-permute-start(bf16[16,168,256]{2,1,0:T(8,128)(2,1)S(1)} %weight_grad.3), channel_id=1, source_target_pairs={{0,16},{16,0},{1,17},{17,1},{2,18},{18,2},{3,19},{19,3},{4,20},{20... | collective-permute-start | bytes 4128776 | tf_op jit(solution)/shard_map/ppermute | solution.py:24
Sparse Core Ops, SparseCore 0:
  26.3 51.1 all-gather.1
where the time goes:
time: 249 us; the launch traced here: 248 us
  waiting for transfers between devices  79 us (32%)
  blocking collectives  59 us (24%)
  starting transfers between devices  58.7 us (24%)
  Pallas kernels  16.9 us (7%)
  local copies, waits for them, and re-layouts  16.5 us (7%)
  between operations  14.4 us (6%)
  other arithmetic  3 us (1%)
    all_to_all x1, blocking collectives, scattered_sum(): landed = lax.all_to_all(chip, ('z', 'far'), 0, 0, tiled=True)  59 us
    ppermute x14, waiting for transfers between devices, cycled(): lax.ppermute(value, axis, [(i, (i + step) % count) for i in range(count)])  50.7 us
    ppermute x14, starting transfers between devices, cycled(): lax.ppermute(value, axis, [(i, (i + step) % count) for i in range(count)])  49.4 us
    ppermute x4, waiting for transfers between devices, passed_along(): return lax.ppermute(block, CTX, route)  28.2 us
    unnamed x47, local copies, waits for them, and re-layouts  15 us
    ppermute x4, starting transfers between devices, passed_along(): return lax.ppermute(block, CTX, route)  9.27 us
    pallas_call x2, Pallas kernels, project(): pl.pallas_call(functools.partial(kernel, pieces, columns), out_shape=out_...  7.17 us
    pallas_call x1, Pallas kernels, attention_call(): pl.pallas_call(attention_kernel, out_shape=(jax.ShapeDtypeStruct((tokens,...  5.73 us
  transfers between devices with their start and end apart: 19, of which 12 were waited for; matrix products, arithmetic and copies ran while one was open for 1% of the time, Pallas kernels for 2%

commit v1 on v0

--- a/solution.py
+++ b/solution.py
@@ -66,11 +66,15 @@
     below = cycled(own, "y", -1)
     across(own, (0,), (1, 3, 2))
     sides = jnp.concatenate([above, below])
-    across(sides, (3, 1), (1, 3, 2))
-    own, sides = lax.optimization_barrier((own, sides))
+    across(sides, (3, 1), (1, 3))
+    early = len(arrays)
     opposite = cycled(own, "y", 2)
     across(opposite, (2,), (1, 3, 2))
-    return arrays, pieces, sides
+    right, left = arrays[early - 2 : early]
+    for moved, x_shift, y_step in ((left[:2], 1, 3), (right[2:], -1, 1)):
+        moved = cycled(moved, "x", x_shift)
+        add(moved, [(2, y_step, 0), (2, y_step, 1)])
+    return arrays, pieces, early
 
 
 CONTRACT_ROWS = (((0,), (0,)), ((), ()))
@@ -86,7 +90,7 @@
     return values * cosine - pltpu.roll(values, HEAD_DIM // 2, 1) * sine_signed
 
 
-def accumulated(pieces, columns, place_ref, weights_ref, arrays, total):
+def accumulated(pieces, columns, place_ref, weights_ref, arrays, total, begun=None):
     first, last = columns
     for number, (array, at, x_step, y_step, half) in enumerate(pieces):
         place = place_ref[x_step * 4 + y_step]
@@ -94,12 +98,21 @@
         term = lax.dot_general(
             arrays[array][at], weight, CONTRACT_ROWS, preferred_element_type=jnp.float32
         )
-        total[...] = term if number == 0 else total[...] + term
-
-
-def key_value_kernel(pieces, columns, place_ref, weights_ref, cos_ref, sin_ref, *refs):
+        if number == 0:
+            total[...] = term if begun is None else begun[...] + term
+        else:
+            total[...] += term
+
+
+def partial_kernel(pieces, columns, place_ref, weights_ref, cos_ref, sin_ref, *refs):
     *arrays, out_ref, total = refs
     accumulated(pieces, columns, place_ref, weights_ref, arrays, total)
+    out_ref[...] = total[...]
+
+
+def key_value_kernel(pieces, columns, place_ref, weights_ref, cos_ref, sin_ref, *refs):
+    *arrays, begun, out_ref, total = refs
+    accumulated(pieces, columns, place_ref, weights_ref, arrays, total, begun)
     keys = turned(total[:, :HEAD_DIM], cos_ref[...], sin_ref[...])
     out_ref[0] = keys.astype(jnp.bfloat16)
     out_ref[1] = total[:, HEAD_DIM:].astype(jnp.bfloat16)
@@ -189,7 +202,7 @@
     )(low, queries, far, near, own, grads)
 
 
-def project(kernel, out_shape, arrays, pieces, columns, place, weights, tables):
+def project(kernel, out_shape, arrays, pieces, columns, place, weights, tables, begun=()):
     tokens = arrays[0].shape[2]
     width = columns[1] - columns[0]
     depth = len(pieces) * arrays[0].shape[1]
@@ -197,7 +210,7 @@
     return pl.pallas_call(
         functools.partial(kernel, pieces, columns),
         out_shape=out_shape,
-        in_specs=[pl.BlockSpec(memory_space=pltpu.SMEM)] + [vmem] * (3 + len(arrays)),
+        in_specs=[pl.BlockSpec(memory_space=pltpu.SMEM)] + [vmem] * (3 + len(arrays) + len(begun)),
         out_specs=vmem,
         scratch_shapes=[pltpu.VMEM((tokens, width), jnp.float32)],
         compiler_params=pltpu.CompilerParams(vmem_limit_bytes=10 << 20),
@@ -207,7 +220,7 @@
             transcendentals=0,
         ),
         name="project",
-    )(place, weights, *tables, *arrays)
+    )(place, weights, *tables, *arrays, *begun)
 
 
 def weight_grad_kernel(
@@ -273,7 +286,7 @@
     query_scale = (slab_rows * 16 / HEADS_Q) ** (-0.5)
     ctx_index = lax.axis_index(CTX)
 
-    arrays, pieces, _ = spread_features(features.T.reshape(2, slab_rows // 2, tok_rows))
+    arrays, pieces, early = spread_features(features.T.reshape(2, slab_rows // 2, tok_rows))
     weights = spread_weights(query_weight, key_weight, value_weight)
     step = jnp.arange(4, dtype=jnp.int32)
     x_at, y_at = lax.axis_index("x"), lax.axis_index("y")
@@ -288,15 +301,27 @@
     low = jnp.maximum(query_start, query_index - (WINDOW - 1)) - (ctx_index - SPAN) * tok_rows
     low = low.astype(jnp.int32)[None]
 
+    columns = (query_cols, query_cols + 2 * value_cols)
+    begun = project(
+        partial_kernel,
+        jax.ShapeDtypeStruct((tok_rows, 2 * value_cols), jnp.float32),
+        arrays[:early],
+        [piece for piece in pieces if piece[0] < early],
+        columns,
+        place,
+        weights,
+        tables,
+    )
     key_value = project(
         key_value_kernel,
         jax.ShapeDtypeStruct((2, tok_rows, HEAD_DIM), jnp.bfloat16),
-        arrays,
-        pieces,
-        (query_cols, query_cols + 2 * value_cols),
+        arrays[early:],
+        [(piece[0] - early, *piece[1:]) for piece in pieces if piece[0] >= early],
+        columns,
         place,
         weights,
         tables,
+        (begun,),
     )
     far, near = passed_along(key_value, 2), passed_along(key_value, 1)
     queries = project(

time: 249 us -> 239 us (0.960)
  the two profiles are of different devices: /device:TPU:56 before, /device:TPU:22 now
where the time goes in v1:
time: 239 us; the launch traced here: 238 us
  blocking collectives  64.9 us (27%)
  waiting for transfers between devices  62.3 us (26%)
  starting transfers between devices  60.7 us (25%)
  Pallas kernels  20.2 us (8%)
  between operations  14.5 us (6%)
  local copies, waits for them, and re-layouts  10.9 us (5%)
  other arithmetic  5 us (2%)
    all_to_all x1, blocking collectives, scattered_sum(): landed = lax.all_to_all(chip, ('z', 'far'), 0, 0, tiled=True)  64.9 us
    ppermute x15, starting transfers between devices, cycled(): lax.ppermute(value, axis, [(i, (i + step) % count) for i in range(count)])  47 us
    ppermute x15, waiting for transfers between devices, cycled(): lax.ppermute(value, axis, [(i, (i + step) % count) for i in range(count)])  39.8 us
    ppermute x4, waiting for transfers between devices, passed_along(): return lax.ppermute(block, CTX, route)  22.5 us
    ppermute x4, starting transfers between devices, passed_along(): return lax.ppermute(block, CTX, route)  13.7 us
    pallas_call x3, Pallas kernels, project(): pl.pallas_call(functools.partial(kernel, pieces, columns), out_shape=out_...  9.34 us
    unnamed x25, local copies, waits for them, and re-layouts  7.79 us
    pallas_call x1, Pallas kernels, attention_call(): pl.pallas_call(attention_kernel, out_shape=(jax.ShapeDtypeStruct((tokens,...  5.73 us
  transfers between devices with their start and end apart: 20, of which 9 were waited for; matrix products, arithmetic and copies ran while one was open for 2% of the time, Pallas kernels for 4%

profile of v1, /device:TPU:22, one launch (start us, length us, event | category | flops | bytes accessed | tf_op | source)
XLA Modules:
  0.0 238.4 jit_solution(11221882746019039792)
XLA Ops:
  7.2 0.0 all-gather.2.cloned.1.call-start
  7.2 0.9 constant_dynamic-update-slice_fusion.2
  8.2 0.8 constant_dynamic-update-slice_fusion.1
  9.0 0.8 constant_dynamic-update-slice_fusion
  9.8 5.9 %collective-permute-start = (bf16[168,512]{1,0:T(8,128)(2,1)S(1)}, bf16[168,512]{1,0:T(8,128)(2,1)S(1)}, u32[]{:S(2)}, u32[]{:S(2)}) collective-permute-start(bf16[168,512]{1,0:T(8,128)(2,1)S(1)} %constant_dynamic-update-slice_fusion), channel_id=1, source_target_pairs={{0,32},{32,0},{1,33},{33,1},{2,34},{34,2},{3,35},{35,3},{4,36},{36... | collective-permute-start | bytes 516104 | tf_op jit(solution)/shard_map/ppermute | solution.py:24
  15.7 9.6 %collective-permute-done = bf16[168,512]{1,0:T(8,128)(2,1)S(1)} collective-permute-done((bf16[168,512]{1,0:T(8,128)(2,1)S(1)}, bf16[168,512]{1,0:T(8,128)(2,1)S(1)}, u32[]{:S(2)}, u32[]{:S(2)}) %collective-permute-start) | collective-permute-done | bytes 172064 | tf_op jit(solution)/shard_map/ppermute | solution.py:24
  25.3 0.8 maximum_select_fusion
  26.1 0.0 all-gather.2.cloned.1.call-update
  26.2 1.9 collective-permute-start.8
  28.1 3.8 %collective-permute-start.5 = (bf16[2,168,512]{2,1,0:T(8,128)(2,1)S(1)}, bf16[2,168,512]{2,1,0:T(8,128)(2,1)S(1)}, u32[]{:S(2)}, u32[]{:S(2)}) collective-permute-start(bf16[2,168,512]{2,1,0:T(8,128)(2,1)S(1)} %bitcast.12), channel_id=1, source_target_pairs={{0,3},{1,0},{2,1},{3,2},{4,7},{5,4},{6,5},{7,6},{8,11},{9,8},{10,9... | collective-permute-start | bytes 1032200 | tf_op jit(solution)/shard_map/ppermute | solution.py:24
  31.9 2.1 collective-permute-start.4
  34.0 3.3 %collective-permute-start.3 = (bf16[2,168,512]{2,1,0:T(8,128)(2,1)S(1)}, bf16[2,168,512]{2,1,0:T(8,128)(2,1)S(1)}, u32[]{:S(2)}, u32[]{:S(2)}) collective-permute-start(bf16[2,168,512]{2,1,0:T(8,128)(2,1)S(1)} %bitcast.14), channel_id=1, source_target_pairs={{0,8},{4,12},{8,0},{12,4},{1,9},{5,13},{9,1},{13,5},{2,10},{6,14},... | collective-permute-start | bytes 1032200 | tf_op jit(solution)/shard_map/ppermute | solution.py:24
  37.3 4.3 %collective-permute-start.2 = (bf16[2,168,512]{2,1,0:T(8,128)(2,1)S(1)}, bf16[2,168,512]{2,1,0:T(8,128)(2,1)}, u32[]{:S(2)}, u32[]{:S(2)}) collective-permute-start(bf16[2,168,512]{2,1,0:T(8,128)(2,1)S(1)} %bitcast.15), channel_id=1, source_target_pairs={{0,4},{4,8},{8,12},{12,0},{1,5},{5,9},{9,13},{13,1},{2,6},{6,10},{... | collective-permute-start | bytes 1032200 | tf_op jit(solution)/shard_map/ppermute | solution.py:24
  41.6 0.2 reduce-window.9
  41.8 0.1 select_reduce_fusion
  41.9 15.7 %collective-permute-done.4 = bf16[2,168,512]{2,1,0:T(8,128)(2,1)S(1)} collective-permute-done((bf16[2,168,512]{2,1,0:T(8,128)(2,1)S(1)}, bf16[2,168,512]{2,1,0:T(8,128)(2,1)S(1)}, u32[]{:S(2)}, u32[]{:S(2)}) %collective-permute-start.4) | collective-permute-done | bytes 344096 | tf_op jit(solution)/shard_map/ppermute | solution.py:24
  57.7 2.4 %collective-permute-start.7 = (bf16[4,168,512]{2,1,0:T(8,128)(2,1)S(1)}, bf16[4,168,512]{2,1,0:T(8,128)(2,1)S(1)}, u32[]{:S(2)}, u32[]{:S(2)}) collective-permute-start(bf16[4,168,512]{2,1,0:T(8,128)(2,1)S(1)} %constant_dynamic-update-slice_fusion.3.refs_4_), channel_id=1, source_target_pairs={{0,4},{4,8},{8,12},{12,0},{1,5},{5,9},{9,13},{13,1},{2,6},{6,10},{... | collective-permute-start | bytes 2064392 | tf_op jit(solution)/shard_map/ppermute | solution.py:24
  60.1 3.5 %collective-permute-start.6 = (bf16[4,168,512]{2,1,0:T(8,128)(2,1)S(1)}, bf16[4,168,512]{2,1,0:T(8,128)(2,1)S(1)}, u32[]{:S(2)}, u32[]{:S(2)}) collective-permute-start(bf16[4,168,512]{2,1,0:T(8,128)(2,1)S(1)} %constant_dynamic-update-slice_fusion.3.refs_4_), channel_id=1, source_target_pairs={{0,12},{4,0},{8,4},{12,8},{1,13},{5,1},{9,5},{13,9},{2,14},{6,2},{... | collective-permute-start | bytes 2064392 | tf_op jit(solution)/shard_map/ppermute | solution.py:24
  63.6 2.7 %collective-permute-start.1 = (bf16[2,168,512]{2,1,0:T(8,128)(2,1)S(1)}, bf16[2,168,512]{2,1,0:T(8,128)(2,1)S(1)}, u32[]{:S(2)}, u32[]{:S(2)}) collective-permute-start(bf16[2,168,512]{2,1,0:T(8,128)(2,1)S(1)} %bitcast.16), channel_id=1, source_target_pairs={{0,12},{4,0},{8,4},{12,8},{1,13},{5,1},{9,5},{13,9},{2,14},{6,2},{... | collective-permute-start | bytes 1032200 | tf_op jit(solution)/shard_map/ppermute | solution.py:24
  66.3 1.8 fusion
  68.2 8.2 %collective-permute-done.7.refs_6_ = bf16[4,168,512]{2,1,0:T(8,128)(2,1)S(1)} collective-permute-done((bf16[4,168,512]{2,1,0:T(8,128)(2,1)S(1)}, bf16[4,168,512]{2,1,0:T(8,128)(2,1)S(1)}, u32[]{:S(2)}, u32[]{:S(2)}) %collective-permute-start.7) | collective-permute-done | bytes 688160 | tf_op jit(solution)/shard_map/ppermute | solution.py:24
  76.3 3.3 %collective-permute-start.11 = (bf16[2,168,512]{2,1,0:T(8,128)(2,1)S(1)}, bf16[2,168,512]{2,1,0:T(8,128)(2,1)}, u32[]{:S(2)}, u32[]{:S(2)}) collective-permute-start(bf16[2,168,512]{2,1,0:T(8,128)(2,1)S(1)} %collective-permute-done.8.refs_7_.refs_0_), channel_id=1, source_target_pairs={{0,8},{4,12},{8,0},{12,4},{1,9},{5,13},{9,1},{13,5},{2,10},{6,14},... | collective-permute-start | bytes 1032200 | tf_op jit(solution)/shard_map/ppermute | solution.py:24
  79.7 0.8 slice.16
  80.4 1.1 collective-permute-done.6.refs_5_
  81.5 2.9 %collective-permute-start.10 = (bf16[2,168,512]{2,1,0:T(8,128)(2,1)S(1)}, bf16[2,168,512]{2,1,0:T(8,128)(2,1)}, u32[]{:S(2)}, u32[]{:S(2)}) collective-permute-start(bf16[2,168,512]{2,1,0:T(8,128)(2,1)S(1)} %collective-permute-done.8.refs_7_.refs_0_), channel_id=1, source_target_pairs={{0,4},{4,8},{8,12},{12,0},{1,5},{5,9},{9,13},{13,1},{2,6},{6,10},{... | collective-permute-start | bytes 1032200 | tf_op jit(solution)/shard_map/ppermute | solution.py:24
  84.4 0.8 slice.17
  85.2 0.0 collective-permute-done.3.refs_3_
  85.2 0.8 copy-done.3
  86.0 2.9 %collective-permute-start.9 = (bf16[2,168,512]{2,1,0:T(8,128)(2,1)S(1)}, bf16[2,168,512]{2,1,0:T(8,128)(2,1)}, u32[]{:S(2)}, u32[]{:S(2)}) collective-permute-start(bf16[2,168,512]{2,1,0:T(8,128)(2,1)S(1)} %collective-permute-done.8.refs_7_.refs_0_), channel_id=1, source_target_pairs={{0,12},{4,0},{8,4},{12,8},{1,13},{5,1},{9,5},{13,9},{2,14},{6,2},{... | collective-permute-start | bytes 1032200 | tf_op jit(solution)/shard_map/ppermute | solution.py:24
  88.9 0.0 collective-permute-done.2.refs_2_
  88.9 4.2 %collective-permute-start.12 = (bf16[2,168,512]{2,1,0:T(8,128)(2,1)}, bf16[2,168,512]{2,1,0:T(8,128)(2,1)}, u32[]{:S(2)}, u32[]{:S(2)}) collective-permute-start(bf16[2,168,512]{2,1,0:T(8,128)(2,1)} %slice.16), channel_id=1, source_target_pairs={{0,4},{4,8},{8,12},{12,0},{1,5},{5,9},{9,13},{13,1},{2,6},{6,10},{... | collective-permute-start | bytes 1032200 | tf_op jit(solution)/shard_map/ppermute | solution.py:24
  93.1 0.0 collective-permute-done.1.refs_1_
  93.1 0.7 copy-done.6
  93.8 1.9 collective-permute-start.13
  95.7 0.1 broadcast_add_fusion
  95.8 0.1 add.112
  95.9 0.1 pad_add_fusion.place_ref
  96.0 1.3 pad_maximum_fusion
  97.3 0.0 all-gather.2.cloned.1.call-done.weights_ref
  97.3 2.6 %copy-done = bf16[16,2,168,512]{3,2,1,0:T(8,128)(2,1)S(1)} copy-done((bf16[16,2,168,512]{3,2,1,0:T(8,128)(2,1)S(1)}, bf16[16,2,168,512]{3,2,1,0:T(8,128)(2,1)}, u32[]{:S(2)}) %copy-start) | copy-done | bytes 5505048
  99.9 1.0 copy-done.4
  100.9 1.0 copy-done.7
  101.9 2.6 %project.4.refs_6_ = f32[512,256]{1,0:T(8,128)S(1)} custom-call(s32[18]{0:T(128)S(1)} %pad_add_fusion.place_ref, bf16[16,2,168,512]{3,2,1,0:T(8,128)(2,1)S(1)} %copy-done, f32[512,128]{1,0:T(8,128)S(1)} %get-tuple-element.18.cos_ref, f32[512,128]{1,0:T(8,128)S(1)} %get-tuple-element.19.sin_ref, bf16[2,168,512]{2,1,0:T(8,128)(2,1)S(1)} %bitcast.17, ...), custom_call_target="tpu_custom_call" | custom-call | flops 880803840 | bytes 5685248 | tf_op jit(solution)/shard_map/project/pallas_call | solution.py:210
  104.5 0.0 collective-permute-done.10.refs_9_.refs_2_
  104.5 4.6 %collective-permute-done.13.refs_12_.refs_5_ = bf16[2,168,512]{2,1,0:T(8,128)(2,1)} collective-permute-done((bf16[2,168,512]{2,1,0:T(8,128)(2,1)}, bf16[2,168,512]{2,1,0:T(8,128)(2,1)}, u32[]{:S(2)}, u32[]{:S(2)}) %collective-permute-start.13) | collective-permute-done | bytes 344096 | tf_op jit(solution)/shard_map/ppermute | solution.py:24
  109.1 2.7 %project.5.own_ref = bf16[2,512,128]{2,1,0:T(8,128)(2,1)S(1)} custom-call(s32[18]{0:T(128)S(1)} %pad_add_fusion.place_ref, bf16[16,2,168,512]{3,2,1,0:T(8,128)(2,1)S(1)} %copy-done, f32[512,128]{1,0:T(8,128)S(1)} %get-tuple-element.18.cos_ref, f32[512,128]{1,0:T(8,128)S(1)} %get-tuple-element.19.sin_ref, ...), custom_call_target="tpu_custom_call" | custom-call | flops 528482304 | bytes 3620864 | tf_op jit(solution)/shard_map/project/pallas_call | solution.py:210
  111.8 1.9 collective-permute-start.15
  113.7 9.2 %collective-permute-start.14 = (bf16[2,512,128]{2,1,0:T(8,128)(2,1)S(1)}, bf16[2,512,128]{2,1,0:T(8,128)(2,1)S(1)}, u32[]{:S(2)}, u32[]{:S(2)}) collective-permute-start(bf16[2,512,128]{2,1,0:T(8,128)(2,1)S(1)} %project.5.own_ref), channel_id=1, source_target_pairs={{0,32},{16,48},{32,64},{48,80},{64,96},{80,112},{96,128},{112,144}... | collective-permute-start | bytes 786440 | tf_op jit(solution)/shard_map/ppermute | solution.py:30
  122.9 0.0 copy-start.9
  122.9 4.1 %project.3.q_ref = bf16[512,256]{1,0:T(8,128)(2,1)S(1)} custom-call(s32[18]{0:T(128)S(1)} %pad_add_fusion.place_ref, bf16[16,2,168,512]{3,2,1,0:T(8,128)(2,1)S(1)} %copy-done.1, f32[512,128]{1,0:T(8,128)S(1)} %get-tuple-element.18.cos_ref, f32[512,128]{1,0:T(8,128)S(1)} %get-tuple-element.19.sin_ref, bf16[2,168,512]{2,1,0:T(8,128)(2,1)S(1)} %bitcast.18, ...), custom_call_target="tpu_custom_call" | custom-call | flops 1409286144 | bytes 8781824 | tf_op jit(solution)/shard_map/project/pallas_call | solution.py:210
  127.0 3.8 %collective-permute-done.14.far_ref = bf16[2,512,128]{2,1,0:T(8,128)(2,1)S(1)} collective-permute-done((bf16[2,512,128]{2,1,0:T(8,128)(2,1)S(1)}, bf16[2,512,128]{2,1,0:T(8,128)(2,1)S(1)}, u32[]{:S(2)}, u32[]{:S(2)}) %collective-permute-start.14) | collective-permute-done | bytes 262176 | tf_op jit(solution)/shard_map/ppermute | solution.py:30
  130.8 5.7 %attention.1 = (bf16[512,256]{1,0:T(8,128)(2,1)}, bf16[2,512,128]{2,1,0:T(8,128)(2,1)S(1)}, bf16[2,512,128]{2,1,0:T(8,128)(2,1)S(1)}, f32[2,512,128]{2,1,0:T(8,128)S(1)}) custom-call(s32[1,512]{1,0:T(1,128)S(1)} %maximum_subtract_fusion.low_ref, bf16[512,256]{1,0:T(8,128)(2,1)S(1)} %project.3.q_ref, ...), custom_call_target="tpu_custom_call" | custom-call | flops 1677721600 | bytes 2097152 | tf_op jit(solution)/shard_map/attention/pallas_call | solution.py:180
  136.6 1.3 collective-permute-start.16
  137.9 1.3 collective-permute-start.17
  139.2 2.0 collective-permute-done.16.near_ref
  141.2 16.7 %collective-permute-done.17.far_ref = bf16[2,512,128]{2,1,0:T(8,128)(2,1)S(1)} collective-permute-done((bf16[2,512,128]{2,1,0:T(8,128)(2,1)S(1)}, bf16[2,512,128]{2,1,0:T(8,128)(2,1)S(1)}, u32[]{:S(2)}, u32[]{:S(2)}) %collective-permute-start.17) | collective-permute-done | bytes 262176 | tf_op jit(solution)/shard_map/ppermute | solution.py:30
  157.9 2.5 %weight_grad.3 = bf16[16,168,256]{2,1,0:T(8,128)(2,1)S(1)} custom-call(s32[18]{0:T(128)S(1)} %pad_add_fusion.place_ref, f32[2,512,128]{2,1,0:T(8,128)S(1)} %get-tuple-element.8.own_ref, bf16[2,512,128]{2,1,0:T(8,128)(2,1)S(1)} %collective-permute-done.16.near_ref, bf16[2,512,128]{2,1,0:T(8,128)(2,1)S(1)} %collective-permute-done.17.far_ref, ...), custom_call_target="tpu_custom_call" | custom-call | flops 704643072 | bytes 4390912 | tf_op jit(solution)/shard_map/weight_grad/pallas_call | solution.py:251
  160.4 1.9 collective-permute-start.18
  162.3 2.5 %weight_grad.2 = bf16[16,168,256]{2,1,0:T(8,128)(2,1)S(1)} custom-call(s32[18]{0:T(128)S(1)} %pad_add_fusion.place_ref, f32[2,512,128]{2,1,0:T(8,128)S(1)} %get-tuple-element.8.own_ref, bf16[2,512,128]{2,1,0:T(8,128)(2,1)S(1)} %collective-permute-done.16.near_ref, bf16[2,512,128]{2,1,0:T(8,128)(2,1)S(1)} %collective-permute-done.17.far_ref, ...), custom_call_target="tpu_custom_call" | custom-call | flops 704643072 | bytes 4390912 | tf_op jit(solution)/shard_map/weight_grad/pallas_call | solution.py:251
  164.9 0.5 collective-permute-done.18
  165.4 0.4 add_convert_fusion
  165.9 64.9 %all_to_all.5 = bf16[16,168,256]{2,1,0:T(8,128)(2,1)S(1)} all-to-all(bf16[16,168,256]{2,1,0:T(8,128)(2,1)S(1)} %add_convert_fusion), channel_id=1, replica_groups=mesh['z'=8,'far'=2,'core'=2,'x'=4,'y'=4] {'z','far'}, dimensions={0} | all-to-all | bytes 2752512 | tf_op jit(solution)/shard_map/all_to_all | solution.py:270
  230.7 0.2 reduce_sum.12
  230.9 0.6 fusion.4
  (30 shorter events, 0.1 us)
Async XLA Ops:
  7.2 19.0 %copy-start.2 = (bf16[512,336]{0,1:T(8,128)(2,1)S(1)}, bf16[512,336]{0,1:T(8,128)(2,1)}, u32[]{:S(2)}) copy-start(bf16[512,336]{0,1:T(8,128)(2,1)} %param.6) | copy-start | bytes 1032196
  7.2 34.4 %copy-start.10 = (s32[8]{0:T(128)S(1)}, s32[8]{0:T(128)}, u32[]{:S(2)}) copy-start(s32[8]{0:T(128)} %param.10) | copy-start | bytes 100
  7.2 90.1 %all-gather.2.cloned.1.call-start = ((), (), s32[]{:S(2)}) async-start(), calls=%async_computation.1 | async-start | bytes 5849088 | tf_op jit(solution)/shard_map/all_gather | solution.py:279
  9.8 15.6 %collective-permute-start = (bf16[168,512]{1,0:T(8,128)(2,1)S(1)}, bf16[168,512]{1,0:T(8,128)(2,1)S(1)}, u32[]{:S(2)}, u32[]{:S(2)}) collective-permute-start(bf16[168,512]{1,0:T(8,128)(2,1)S(1)} %constant_dynamic-update-slice_fusion), channel_id=1, source_target_pairs={{0,32},{32,0},{1,33},{33,1},{2,34},{34,2},{3,35},{35,3},{4,36},{36... | collective-permute-start | bytes 516104 | tf_op jit(solution)/shard_map/ppermute | solution.py:24
  26.2 37.4 %collective-permute-start.8 = (bf16[2,168,512]{2,1,0:T(8,128)(2,1)S(1)}, bf16[2,168,512]{2,1,0:T(8,128)(2,1)S(1)}, u32[]{:S(2)}, u32[]{:S(2)}) collective-permute-start(bf16[2,168,512]{2,1,0:T(8,128)(2,1)S(1)} %bitcast.11), channel_id=1, source_target_pairs={{0,2},{1,3},{2,0},{3,1},{4,6},{5,7},{6,4},{7,5},{8,10},{9,11},{10,... | collective-permute-start | bytes 1032200 | tf_op jit(solution)/shard_map/ppermute | solution.py:24
  28.1 29.6 %collective-permute-start.5 = (bf16[2,168,512]{2,1,0:T(8,128)(2,1)S(1)}, bf16[2,168,512]{2,1,0:T(8,128)(2,1)S(1)}, u32[]{:S(2)}, u32[]{:S(2)}) collective-permute-start(bf16[2,168,512]{2,1,0:T(8,128)(2,1)S(1)} %bitcast.12), channel_id=1, source_target_pairs={{0,3},{1,0},{2,1},{3,2},{4,7},{5,4},{6,5},{7,6},{8,11},{9,8},{10,9... | collective-permute-start | bytes 1032200 | tf_op jit(solution)/shard_map/ppermute | solution.py:24
  31.9 25.7 %collective-permute-start.4 = (bf16[2,168,512]{2,1,0:T(8,128)(2,1)S(1)}, bf16[2,168,512]{2,1,0:T(8,128)(2,1)S(1)}, u32[]{:S(2)}, u32[]{:S(2)}) collective-permute-start(bf16[2,168,512]{2,1,0:T(8,128)(2,1)S(1)} %bitcast.13), channel_id=1, source_target_pairs={{0,1},{1,2},{2,3},{3,0},{4,5},{5,6},{6,7},{7,4},{8,9},{9,10},{10,1... | collective-permute-start | bytes 1032200 | tf_op jit(solution)/shard_map/ppermute | solution.py:24
  34.0 51.3 %collective-permute-start.3 = (bf16[2,168,512]{2,1,0:T(8,128)(2,1)S(1)}, bf16[2,168,512]{2,1,0:T(8,128)(2,1)S(1)}, u32[]{:S(2)}, u32[]{:S(2)}) collective-permute-start(bf16[2,168,512]{2,1,0:T(8,128)(2,1)S(1)} %bitcast.14), channel_id=1, source_target_pairs={{0,8},{4,12},{8,0},{12,4},{1,9},{5,13},{9,1},{13,5},{2,10},{6,14},... | collective-permute-start | bytes 1032200 | tf_op jit(solution)/shard_map/ppermute | solution.py:24
  37.3 51.6 %collective-permute-start.2 = (bf16[2,168,512]{2,1,0:T(8,128)(2,1)S(1)}, bf16[2,168,512]{2,1,0:T(8,128)(2,1)}, u32[]{:S(2)}, u32[]{:S(2)}) collective-permute-start(bf16[2,168,512]{2,1,0:T(8,128)(2,1)S(1)} %bitcast.15), channel_id=1, source_target_pairs={{0,4},{4,8},{8,12},{12,0},{1,5},{5,9},{9,13},{13,1},{2,6},{6,10},{... | collective-permute-start | bytes 1032200 | tf_op jit(solution)/shard_map/ppermute | solution.py:24
  57.7 18.7 %collective-permute-start.7 = (bf16[4,168,512]{2,1,0:T(8,128)(2,1)S(1)}, bf16[4,168,512]{2,1,0:T(8,128)(2,1)S(1)}, u32[]{:S(2)}, u32[]{:S(2)}) collective-permute-start(bf16[4,168,512]{2,1,0:T(8,128)(2,1)S(1)} %constant_dynamic-update-slice_fusion.3.refs_4_), channel_id=1, source_target_pairs={{0,4},{4,8},{8,12},{12,0},{1,5},{5,9},{9,13},{13,1},{2,6},{6,10},{... | collective-permute-start | bytes 2064392 | tf_op jit(solution)/shard_map/ppermute | solution.py:24
  60.1 21.4 %collective-permute-start.6 = (bf16[4,168,512]{2,1,0:T(8,128)(2,1)S(1)}, bf16[4,168,512]{2,1,0:T(8,128)(2,1)S(1)}, u32[]{:S(2)}, u32[]{:S(2)}) collective-permute-start(bf16[4,168,512]{2,1,0:T(8,128)(2,1)S(1)} %constant_dynamic-update-slice_fusion.3.refs_4_), channel_id=1, source_target_pairs={{0,12},{4,0},{8,4},{12,8},{1,13},{5,1},{9,5},{13,9},{2,14},{6,2},{... | collective-permute-start | bytes 2064392 | tf_op jit(solution)/shard_map/ppermute | solution.py:24
  63.6 29.5 %collective-permute-start.1 = (bf16[2,168,512]{2,1,0:T(8,128)(2,1)S(1)}, bf16[2,168,512]{2,1,0:T(8,128)(2,1)S(1)}, u32[]{:S(2)}, u32[]{:S(2)}) collective-permute-start(bf16[2,168,512]{2,1,0:T(8,128)(2,1)S(1)} %bitcast.16), channel_id=1, source_target_pairs={{0,12},{4,0},{8,4},{12,8},{1,13},{5,1},{9,5},{13,9},{2,14},{6,2},{... | collective-permute-start | bytes 1032200 | tf_op jit(solution)/shard_map/ppermute | solution.py:24
  76.3 28.1 %collective-permute-start.11 = (bf16[2,168,512]{2,1,0:T(8,128)(2,1)S(1)}, bf16[2,168,512]{2,1,0:T(8,128)(2,1)}, u32[]{:S(2)}, u32[]{:S(2)}) collective-permute-start(bf16[2,168,512]{2,1,0:T(8,128)(2,1)S(1)} %collective-permute-done.8.refs_7_.refs_0_), channel_id=1, source_target_pairs={{0,8},{4,12},{8,0},{12,4},{1,9},{5,13},{9,1},{13,5},{2,10},{6,14},... | collective-permute-start | bytes 1032200 | tf_op jit(solution)/shard_map/ppermute | solution.py:24
  81.5 23.0 %collective-permute-start.10 = (bf16[2,168,512]{2,1,0:T(8,128)(2,1)S(1)}, bf16[2,168,512]{2,1,0:T(8,128)(2,1)}, u32[]{:S(2)}, u32[]{:S(2)}) collective-permute-start(bf16[2,168,512]{2,1,0:T(8,128)(2,1)S(1)} %collective-permute-done.8.refs_7_.refs_0_), channel_id=1, source_target_pairs={{0,4},{4,8},{8,12},{12,0},{1,5},{5,9},{9,13},{13,1},{2,6},{6,10},{... | collective-permute-start | bytes 1032200 | tf_op jit(solution)/shard_map/ppermute | solution.py:24
  85.2 0.8 copy-start.3
  86.0 18.5 %collective-permute-start.9 = (bf16[2,168,512]{2,1,0:T(8,128)(2,1)S(1)}, bf16[2,168,512]{2,1,0:T(8,128)(2,1)}, u32[]{:S(2)}, u32[]{:S(2)}) collective-permute-start(bf16[2,168,512]{2,1,0:T(8,128)(2,1)S(1)} %collective-permute-done.8.refs_7_.refs_0_), channel_id=1, source_target_pairs={{0,12},{4,0},{8,4},{12,8},{1,13},{5,1},{9,5},{13,9},{2,14},{6,2},{... | collective-permute-start | bytes 1032200 | tf_op jit(solution)/shard_map/ppermute | solution.py:24
  88.9 15.6 %collective-permute-start.12 = (bf16[2,168,512]{2,1,0:T(8,128)(2,1)}, bf16[2,168,512]{2,1,0:T(8,128)(2,1)}, u32[]{:S(2)}, u32[]{:S(2)}) collective-permute-start(bf16[2,168,512]{2,1,0:T(8,128)(2,1)} %slice.16), channel_id=1, source_target_pairs={{0,4},{4,8},{8,12},{12,0},{1,5},{5,9},{9,13},{13,1},{2,6},{6,10},{... | collective-permute-start | bytes 1032200 | tf_op jit(solution)/shard_map/ppermute | solution.py:24
  93.1 0.7 copy-start.6
  93.8 15.3 %collective-permute-start.13 = (bf16[2,168,512]{2,1,0:T(8,128)(2,1)}, bf16[2,168,512]{2,1,0:T(8,128)(2,1)}, u32[]{:S(2)}, u32[]{:S(2)}) collective-permute-start(bf16[2,168,512]{2,1,0:T(8,128)(2,1)} %slice.17), channel_id=1, source_target_pairs={{0,12},{4,0},{8,4},{12,8},{1,13},{5,1},{9,5},{13,9},{2,14},{6,2},{... | collective-permute-start | bytes 1032200 | tf_op jit(solution)/shard_map/ppermute | solution.py:24
  97.3 2.6 %copy-start = (bf16[16,2,168,512]{3,2,1,0:T(8,128)(2,1)S(1)}, bf16[16,2,168,512]{3,2,1,0:T(8,128)(2,1)}, u32[]{:S(2)}) copy-start(bf16[16,2,168,512]{3,2,1,0:T(8,128)(2,1)} %all-gather.2.cloned.1.call-done.weights_ref) | copy-start | bytes 16515076
  99.9 1.0 copy-start.4
  100.9 1.0 copy-start.7
  109.1 13.8 %copy-start.1 = (bf16[16,2,168,512]{3,2,1,0:T(8,128)(2,1)S(1)}, bf16[16,2,168,512]{3,2,1,0:T(8,128)(2,1)}, u32[]{:S(2)}) copy-start(bf16[16,2,168,512]{3,2,1,0:T(8,128)(2,1)} %all-gather.2.cloned.1.call-done.weights_ref) | copy-start | bytes 16515076
  111.8 15.2 %collective-permute-start.15 = (bf16[2,512,128]{2,1,0:T(8,128)(2,1)S(1)}, bf16[2,512,128]{2,1,0:T(8,128)(2,1)S(1)}, u32[]{:S(2)}, u32[]{:S(2)}) collective-permute-start(bf16[2,512,128]{2,1,0:T(8,128)(2,1)S(1)} %project.5.own_ref), channel_id=1, source_target_pairs={{0,16},{16,32},{32,48},{48,64},{64,80},{80,96},{96,112},{112,128},... | collective-permute-start | bytes 786440 | tf_op jit(solution)/shard_map/ppermute | solution.py:30
  113.7 17.1 %collective-permute-start.14 = (bf16[2,512,128]{2,1,0:T(8,128)(2,1)S(1)}, bf16[2,512,128]{2,1,0:T(8,128)(2,1)S(1)}, u32[]{:S(2)}, u32[]{:S(2)}) collective-permute-start(bf16[2,512,128]{2,1,0:T(8,128)(2,1)S(1)} %project.5.own_ref), channel_id=1, source_target_pairs={{0,32},{16,48},{32,64},{48,80},{64,96},{80,112},{96,128},{112,144}... | collective-permute-start | bytes 786440 | tf_op jit(solution)/shard_map/ppermute | solution.py:30
  122.9 7.9 %copy-start.9 = (bf16[512,256]{1,0:T(8,128)(2,1)S(1)}, bf16[512,256]{1,0:T(8,128)(2,1)}, u32[]{:S(2)}) copy-start(bf16[512,256]{1,0:T(8,128)(2,1)} %grad_ref.1) | copy-start | bytes 786436
  127.0 30.9 %copy-start.5 = (bf16[2,168,512]{2,1,0:T(8,128)(2,1)S(1)}, bf16[2,168,512]{2,1,0:T(8,128)(2,1)}, u32[]{:S(2)}) copy-start(bf16[2,168,512]{2,1,0:T(8,128)(2,1)} %copy-done.3) | copy-start | bytes 1032196
  127.0 30.9 %copy-start.8 = (bf16[2,168,512]{2,1,0:T(8,128)(2,1)S(1)}, bf16[2,168,512]{2,1,0:T(8,128)(2,1)}, u32[]{:S(2)}) copy-start(bf16[2,168,512]{2,1,0:T(8,128)(2,1)} %copy-done.6) | copy-start | bytes 1032196
  136.6 4.6 %collective-permute-start.16 = (bf16[2,512,128]{2,1,0:T(8,128)(2,1)S(1)}, bf16[2,512,128]{2,1,0:T(8,128)(2,1)S(1)}, u32[]{:S(2)}, u32[]{:S(2)}) collective-permute-start(bf16[2,512,128]{2,1,0:T(8,128)(2,1)S(1)} %get-tuple-element.9), channel_id=1, source_target_pairs={{16,0},{32,16},{48,32},{64,48},{80,64},{96,80},{112,96},{128,112},... | collective-permute-start | bytes 786440 | tf_op jit(solution)/shard_map/ppermute | solution.py:30
  137.9 20.0 %collective-permute-start.17 = (bf16[2,512,128]{2,1,0:T(8,128)(2,1)S(1)}, bf16[2,512,128]{2,1,0:T(8,128)(2,1)S(1)}, u32[]{:S(2)}, u32[]{:S(2)}) collective-permute-start(bf16[2,512,128]{2,1,0:T(8,128)(2,1)S(1)} %get-tuple-element.10), channel_id=1, source_target_pairs={{32,0},{48,16},{64,32},{80,48},{96,64},{112,80},{128,96},{144,112}... | collective-permute-start | bytes 786440 | tf_op jit(solution)/shard_map/ppermute | solution.py:30
  160.4 5.0 %collective-permute-start.18 = (bf16[16,168,256]{2,1,0:T(8,128)(2,1)S(1)}, bf16[16,168,256]{2,1,0:T(8,128)(2,1)S(1)}, u32[]{:S(2)}, u32[]{:S(2)}) collective-permute-start(bf16[16,168,256]{2,1,0:T(8,128)(2,1)S(1)} %weight_grad.3), channel_id=1, source_target_pairs={{0,16},{16,0},{1,17},{17,1},{2,18},{18,2},{3,19},{19,3},{4,20},{20... | collective-permute-start | bytes 4128776 | tf_op jit(solution)/shard_map/ppermute | solution.py:24
Sparse Core Ops, SparseCore 0:
  26.3 51.6 all-gather.1

commit v2 on v1

--- a/solution.py
+++ b/solution.py
@@ -127,79 +127,107 @@
         out_ref[:, head * HEAD_DIM : (head + 1) * HEAD_DIM] = queries.astype(jnp.bfloat16)
 
 
-def attention_kernel(low_ref, q_ref, far_ref, near_ref, own_ref, grad_ref, att_ref, *refs):
-    far_out, near_out, own_out, keys, values, acc = refs
+def attention_kernel(low_ref, q_ref, far_ref, near_ref, own_ref, grad_ref, *refs):
+    att_ref, probs_ref, dot_ref, far_out, near_out, own_out, keys, values, acc = refs
     tokens, width = q_ref.shape
     for number, ref in enumerate((far_ref, near_ref, own_ref)):
         keys[number * tokens : (number + 1) * tokens] = ref[0]
         values[number * tokens : (number + 1) * tokens] = ref[1]
     acc[...] = jnp.zeros_like(acc)
     span = 2 * tokens + BLOCK
-    heads = width // HEAD_DIM
-    for head in range(heads):
+    tiles = [(head, at) for head in range(width // HEAD_DIM) for at in range(0, tokens, BLOCK)]
+    for number, (head, at) in enumerate(tiles):
         cols = slice(head * HEAD_DIM, (head + 1) * HEAD_DIM)
-        for at in range(0, tokens, BLOCK):
-            rows = slice(at, at + BLOCK)
-            window = slice(at, at + span)
-            low = low_ref[:, rows]
-            key_at = lax.broadcasted_iota(jnp.int32, (span, BLOCK), 0) + at
-            query_at = lax.broadcasted_iota(jnp.int32, (span, BLOCK), 1) + (2 * tokens + at)
-            allowed = (key_at >= low) & (key_at <= query_at)
-            query = q_ref[rows, cols]
-            grad = grad_ref[rows, cols]
-            scores = lax.dot_general(
-                keys[window], query, CONTRACT_COLS, preferred_element_type=jnp.float32
-            )
-            scores = jnp.where(allowed, scores, -jnp.inf)
-            raw = jnp.exp(scores - jnp.max(scores, axis=0, keepdims=True))
-            probs = raw * (1.0 / jnp.sum(raw, axis=0, keepdims=True))
-            low_probs = probs.astype(jnp.bfloat16)
-            attended = lax.dot_general(
-                values[window], low_probs, CONTRACT_ROWS, preferred_element_type=jnp.float32
-            )
-            attended = attended.T.astype(jnp.bfloat16)
-            att_ref[rows, cols] = attended
-            product = grad.astype(jnp.float32) * attended.astype(jnp.float32)
-            out_dot = jnp.sum(product.T, axis=0, keepdims=True)
-            acc[1, window] += jnp.dot(low_probs, grad, preferred_element_type=jnp.float32)
-            prob_grad = lax.dot_general(
-                values[window], grad, CONTRACT_COLS, preferred_element_type=jnp.float32
-            )
-            score_grad = (probs * (prob_grad - out_dot)).astype(jnp.bfloat16)
-            acc[0, window] += jnp.dot(score_grad, query, preferred_element_type=jnp.float32)
-    far_out[...] = acc[:, :tokens].astype(jnp.bfloat16)
-    near_out[...] = acc[:, tokens : 2 * tokens].astype(jnp.bfloat16)
-    own_out[...] = acc[:, 2 * tokens :]
-
-
-def attention_call(low, queries, far, near, own, grads):
+        rows = slice(at, at + BLOCK)
+        window = slice(at, at + span)
+        low = low_ref[:, rows]
+        key_at = lax.broadcasted_iota(jnp.int32, (span, BLOCK), 0) + at
+        query_at = lax.broadcasted_iota(jnp.int32, (span, BLOCK), 1) + (2 * tokens + at)
+        allowed = (key_at >= low) & (key_at <= query_at)
+        grad = grad_ref[rows, cols]
+        scores = lax.dot_general(
+            keys[window], q_ref[rows, cols], CONTRACT_COLS, preferred_element_type=jnp.float32
+        )
+        scores = jnp.where(allowed, scores, -jnp.inf)
+        raw = jnp.exp(scores - jnp.max(scores, axis=0, keepdims=True))
+        probs = raw * (1.0 / jnp.sum(raw, axis=0, keepdims=True))
+        probs_ref[number] = probs
+        low_probs = probs.astype(jnp.bfloat16)
+        acc[window] += jnp.dot(low_probs, grad, preferred_element_type=jnp.float32)
+        attended = lax.dot_general(
+            values[window], low_probs, CONTRACT_ROWS, preferred_element_type=jnp.float32
+        )
+        attended = attended.T.astype(jnp.bfloat16)
+        att_ref[rows, cols] = attended
+        product = grad.astype(jnp.float32) * attended.astype(jnp.float32)
+        dot_ref[number] = jnp.sum(product.T, axis=0, keepdims=True)
+    far_out[...] = acc[:tokens].astype(jnp.bfloat16)
+    near_out[...] = acc[tokens : 2 * tokens].astype(jnp.bfloat16)
+    own_out[...] = acc[2 * tokens :]
+
+
+def key_grad_kernel(probs_ref, dot_ref, q_ref, far_ref, near_ref, own_ref, grad_ref, *refs):
+    far_out, near_out, own_out, values, acc = refs
+    tokens, width = q_ref.shape
+    for number, ref in enumerate((far_ref, near_ref, own_ref)):
+        values[number * tokens : (number + 1) * tokens] = ref[1]
+    acc[...] = jnp.zeros_like(acc)
+    span = 2 * tokens + BLOCK
+    tiles = [(head, at) for head in range(width // HEAD_DIM) for at in range(0, tokens, BLOCK)]
+    for number, (head, at) in enumerate(tiles):
+        cols = slice(head * HEAD_DIM, (head + 1) * HEAD_DIM)
+        rows = slice(at, at + BLOCK)
+        window = slice(at, at + span)
+        prob_grad = lax.dot_general(
+            values[window], grad_ref[rows, cols], CONTRACT_COLS, preferred_element_type=jnp.float32
+        )
+        score_grad = (probs_ref[number] * (prob_grad - dot_ref[number])).astype(jnp.bfloat16)
+        acc[window] += jnp.dot(score_grad, q_ref[rows, cols], preferred_element_type=jnp.float32)
+    far_out[...] = acc[:tokens].astype(jnp.bfloat16)
+    near_out[...] = acc[tokens : 2 * tokens].astype(jnp.bfloat16)
+    own_out[...] = acc[2 * tokens :]
+
+
+def attention_calls(low, queries, far, near, own, grads):
     tokens, width = queries.shape
     vmem = pl.BlockSpec(memory_space=pltpu.VMEM)
-    block = jax.ShapeDtypeStruct(own.shape, jnp.bfloat16)
-    pairs = tokens * (2 * tokens + BLOCK) * (width // HEAD_DIM)
-    return pl.pallas_call(
+    tiles = (width // HEAD_DIM) * (tokens // BLOCK)
+    span = 2 * tokens + BLOCK
+    part = jax.ShapeDtypeStruct((tokens, HEAD_DIM), jnp.bfloat16)
+    parts = (part, part, jax.ShapeDtypeStruct((tokens, HEAD_DIM), jnp.float32))
+    block = pltpu.VMEM((3 * tokens, HEAD_DIM), jnp.bfloat16)
+    total = pltpu.VMEM((3 * tokens, HEAD_DIM), jnp.float32)
+    pairs = tiles * span * BLOCK
+    attention, probs, dots, *value_parts = pl.pallas_call(
         attention_kernel,
         out_shape=(
             jax.ShapeDtypeStruct((tokens, width), jnp.bfloat16),
-            block,
-            block,
-            jax.ShapeDtypeStruct(own.shape, jnp.float32),
+            jax.ShapeDtypeStruct((tiles, span, BLOCK), jnp.float32),
+            jax.ShapeDtypeStruct((tiles, 1, BLOCK), jnp.float32),
+            *parts,
         ),
         in_specs=[vmem] * 6,
-        out_specs=(vmem,) * 4,
-        scratch_shapes=[
-            pltpu.VMEM((3 * tokens, HEAD_DIM), jnp.bfloat16),
-            pltpu.VMEM((3 * tokens, HEAD_DIM), jnp.bfloat16),
-            pltpu.VMEM((2, 3 * tokens, HEAD_DIM), jnp.float32),
-        ],
-        compiler_params=pltpu.CompilerParams(vmem_limit_bytes=10 << 20),
+        out_specs=(vmem,) * 6,
+        scratch_shapes=[block, block, total],
+        compiler_params=pltpu.CompilerParams(vmem_limit_bytes=14 << 20),
         cost_estimate=pl.CostEstimate(
-            flops=10 * pairs * HEAD_DIM,
-            bytes_accessed=4 * tokens * width * 4,
-            transcendentals=pairs,
+            flops=6 * pairs * HEAD_DIM, bytes_accessed=8 * tokens * width, transcendentals=pairs
         ),
         name="attention",
     )(low, queries, far, near, own, grads)
+    key_parts = pl.pallas_call(
+        key_grad_kernel,
+        out_shape=parts,
+        in_specs=[vmem] * 7,
+        out_specs=(vmem,) * 3,
+        scratch_shapes=[block, total],
+        compiler_params=pltpu.CompilerParams(vmem_limit_bytes=14 << 20),
+        cost_estimate=pl.CostEstimate(
+            flops=4 * pairs * HEAD_DIM, bytes_accessed=8 * tokens * width, transcendentals=0
+        ),
+        name="key_grad",
+    )(probs, dots, queries, far, near, own, grads)
+    return attention, key_parts, value_parts
 
 
 def project(kernel, out_shape, arrays, pieces, columns, place, weights, tables, begun=()):
@@ -223,15 +251,13 @@
     )(place, weights, *tables, *arrays, *begun)
 
 
-def weight_grad_kernel(
-    pieces, partner, place_ref, own_ref, near_ref, far_ref, cos_ref, sin_ref, *refs
-):
-    *arrays, out_ref, grads = refs
+def weight_grad_kernel(pieces, partner, place_ref, *refs):
+    parts, (cos_ref, sin_ref, *arrays, out_ref, grads) = refs[:6], refs[6:]
     core = place_ref[16]
     wanted = 1 - core if partner else core
     sums = [
-        own_ref[i] + near_ref[i].astype(jnp.float32) + far_ref[i].astype(jnp.float32)
-        for i in range(2)
+        own[...] + near[...].astype(jnp.float32) + far[...].astype(jnp.float32)
+        for own, near, far in (parts[:3], parts[3:])
     ]
     grads[:, :HEAD_DIM] = unturned(sums[0], cos_ref[...], sin_ref[...]).astype(jnp.bfloat16)
     grads[:, HEAD_DIM:] = sums[1].astype(jnp.bfloat16)
@@ -243,7 +269,7 @@
             out_ref[place_ref[x_step * 4 + y_step]] = term.astype(jnp.bfloat16)
 
 
-def weight_grad(arrays, pieces, place, own, near, far, tables, partner):
+def weight_grad(arrays, pieces, place, parts, tables, partner):
     rows, tokens = arrays[0].shape[1:]
     width = 2 * HEAD_DIM
     vmem = pl.BlockSpec(memory_space=pltpu.VMEM)
@@ -251,7 +277,7 @@
     return pl.pallas_call(
         functools.partial(weight_grad_kernel, pieces, partner),
         out_shape=jax.ShapeDtypeStruct((16, rows, width), jnp.bfloat16),
-        in_specs=[pl.BlockSpec(memory_space=pltpu.SMEM)] + [vmem] * (5 + len(arrays)),
+        in_specs=[pl.BlockSpec(memory_space=pltpu.SMEM)] + [vmem] * (8 + len(arrays)),
         out_specs=vmem,
         scratch_shapes=[pltpu.VMEM((tokens, width), jnp.bfloat16)],
         compiler_params=pltpu.CompilerParams(vmem_limit_bytes=10 << 20),
@@ -261,7 +287,7 @@
             transcendentals=0,
         ),
         name="weight_grad",
-    )(place, own, near, far, *tables, *arrays)
+    )(place, *parts, *tables, *arrays)
 
 
 def scattered_sum(kept, sent):
@@ -334,12 +360,16 @@
         weights,
         tables,
     )
-    attention, far_part, near_part, own_part = attention_call(
+    attention, key_parts, value_parts = attention_calls(
         low, queries, far, near, key_value, out_grad
     )
-    far_back, near_back = passed_along(far_part, -2), passed_along(near_part, -1)
+    back = []
+    for (far_part, near_part, own_part) in (value_parts, key_parts):
+        far_back = passed_along(far_part, -2)
+        near_back = passed_along(near_part, -1)
+        back.append((own_part, near_back, far_back))
     sent, kept = (
-        weight_grad(arrays, pieces, place, own_part, near_back, far_back, tables, partner)
+        weight_grad(arrays, pieces, place, back[1] + back[0], tables, partner)
         for partner in (True, False)
     )
     weight_grads = scattered_sum(kept, sent).astype(jnp.bfloat16)

time: 239 us -> 243 us (1.017)
  starting transfers between devices: 60.7 us -> 63.3 us
  waiting for transfers between devices: 62.3 us -> 59.7 us
    ppermute x4 -> x6, waiting for transfers between devices: 22.5 us -> 19.9 us  [passed_along(): return lax.ppermute(block, CTX, route)]
    ppermute x4 -> x6, starting transfers between devices: 13.7 us -> 16.3 us  [passed_along(): return lax.ppermute(block, CTX, route)]
    pallas_call x1 -> x2, Pallas kernels: 5.73 us -> 6.88 us  [the longest x1 5.25 us: attention_calls(): pl.pallas_call(attention_kernel, out_shape=(jax.ShapeDtypeStruct((tokens,...]
  transfers between devices with their start and end apart: 20 -> 22, of which waited for: 9 -> 9; matrix products, arithmetic and copies ran while one was open for 2% -> 2% of each run, Pallas kernels for 4% -> 4%
where the time goes in v2:
time: 243 us; the launch traced here: 241 us
  blocking collectives  66.8 us (27%)
  starting transfers between devices  63.3 us (26%)
  waiting for transfers between devices  59.7 us (25%)
  Pallas kernels  21.3 us (9%)
  between operations  14.5 us (6%)
  local copies, waits for them, and re-layouts  10.9 us (4%)
  other arithmetic  5 us (2%)
    all_to_all x1, blocking collectives, scattered_sum(): landed = lax.all_to_all(chip, ('z', 'far'), 0, 0, tiled=True)  66.8 us
    ppermute x15, starting transfers between devices, cycled(): lax.ppermute(value, axis, [(i, (i + step) % count) for i in range(count)])  47 us
    ppermute x15, waiting for transfers between devices, cycled(): lax.ppermute(value, axis, [(i, (i + step) % count) for i in range(count)])  39.8 us
    ppermute x6, waiting for transfers between devices, passed_along(): return lax.ppermute(block, CTX, route)  19.9 us
    ppermute x6, starting transfers between devices, passed_along(): return lax.ppermute(block, CTX, route)  16.3 us
    pallas_call x3, Pallas kernels, project(): pl.pallas_call(functools.partial(kernel, pieces, columns), out_shape=out_...  9.29 us
    unnamed x25, local copies, waits for them, and re-layouts  7.76 us
    pallas_call x1, Pallas kernels, attention_calls(): pl.pallas_call(attention_kernel, out_shape=(jax.ShapeDtypeStruct((tokens,...  5.25 us
  transfers between devices with their start and end apart: 22, of which 9 were waited for; matrix products, arithmetic and copies ran while one was open for 2% of the time, Pallas kernels for 4%

profile of v2, /device:TPU:22, one launch (start us, length us, event | category | flops | bytes accessed | tf_op | source)
XLA Modules:
  0.0 241.4 jit_solution(12145145046682458211)
XLA Ops:
  7.2 0.0 all-gather.2.cloned.1.call-start
  7.2 0.9 constant_dynamic-update-slice_fusion.2
  8.2 0.8 constant_dynamic-update-slice_fusion.1
  9.0 0.8 constant_dynamic-update-slice_fusion
  9.8 5.9 %collective-permute-start = (bf16[168,512]{1,0:T(8,128)(2,1)S(1)}, bf16[168,512]{1,0:T(8,128)(2,1)S(1)}, u32[]{:S(2)}, u32[]{:S(2)}) collective-permute-start(bf16[168,512]{1,0:T(8,128)(2,1)S(1)} %constant_dynamic-update-slice_fusion), channel_id=1, source_target_pairs={{0,32},{32,0},{1,33},{33,1},{2,34},{34,2},{3,35},{35,3},{4,36},{36... | collective-permute-start | bytes 516104 | tf_op jit(solution)/shard_map/ppermute | solution.py:24
  15.7 9.6 %collective-permute-done = bf16[168,512]{1,0:T(8,128)(2,1)S(1)} collective-permute-done((bf16[168,512]{1,0:T(8,128)(2,1)S(1)}, bf16[168,512]{1,0:T(8,128)(2,1)S(1)}, u32[]{:S(2)}, u32[]{:S(2)}) %collective-permute-start) | collective-permute-done | bytes 172064 | tf_op jit(solution)/shard_map/ppermute | solution.py:24
  25.3 0.8 maximum_select_fusion
  26.1 0.0 all-gather.2.cloned.1.call-update
  26.2 1.9 collective-permute-start.8
  28.1 3.8 %collective-permute-start.5 = (bf16[2,168,512]{2,1,0:T(8,128)(2,1)S(1)}, bf16[2,168,512]{2,1,0:T(8,128)(2,1)S(1)}, u32[]{:S(2)}, u32[]{:S(2)}) collective-permute-start(bf16[2,168,512]{2,1,0:T(8,128)(2,1)S(1)} %bitcast.12), channel_id=1, source_target_pairs={{0,3},{1,0},{2,1},{3,2},{4,7},{5,4},{6,5},{7,6},{8,11},{9,8},{10,9... | collective-permute-start | bytes 1032200 | tf_op jit(solution)/shard_map/ppermute | solution.py:24
  31.9 2.1 collective-permute-start.4
  34.0 3.3 %collective-permute-start.3 = (bf16[2,168,512]{2,1,0:T(8,128)(2,1)S(1)}, bf16[2,168,512]{2,1,0:T(8,128)(2,1)S(1)}, u32[]{:S(2)}, u32[]{:S(2)}) collective-permute-start(bf16[2,168,512]{2,1,0:T(8,128)(2,1)S(1)} %bitcast.14), channel_id=1, source_target_pairs={{0,8},{4,12},{8,0},{12,4},{1,9},{5,13},{9,1},{13,5},{2,10},{6,14},... | collective-permute-start | bytes 1032200 | tf_op jit(solution)/shard_map/ppermute | solution.py:24
  37.3 4.3 %collective-permute-start.2 = (bf16[2,168,512]{2,1,0:T(8,128)(2,1)S(1)}, bf16[2,168,512]{2,1,0:T(8,128)(2,1)}, u32[]{:S(2)}, u32[]{:S(2)}) collective-permute-start(bf16[2,168,512]{2,1,0:T(8,128)(2,1)S(1)} %bitcast.15), channel_id=1, source_target_pairs={{0,4},{4,8},{8,12},{12,0},{1,5},{5,9},{9,13},{13,1},{2,6},{6,10},{... | collective-permute-start | bytes 1032200 | tf_op jit(solution)/shard_map/ppermute | solution.py:24
  41.6 0.2 reduce-window.9
  41.8 0.1 select_reduce_fusion
  41.9 15.7 %collective-permute-done.4 = bf16[2,168,512]{2,1,0:T(8,128)(2,1)S(1)} collective-permute-done((bf16[2,168,512]{2,1,0:T(8,128)(2,1)S(1)}, bf16[2,168,512]{2,1,0:T(8,128)(2,1)S(1)}, u32[]{:S(2)}, u32[]{:S(2)}) %collective-permute-start.4) | collective-permute-done | bytes 344096 | tf_op jit(solution)/shard_map/ppermute | solution.py:24
  57.6 0.0 collective-permute-done.5
  57.7 2.4 collective-permute-start.7
  60.1 3.5 %collective-permute-start.6 = (bf16[4,168,512]{2,1,0:T(8,128)(2,1)S(1)}, bf16[4,168,512]{2,1,0:T(8,128)(2,1)S(1)}, u32[]{:S(2)}, u32[]{:S(2)}) collective-permute-start(bf16[4,168,512]{2,1,0:T(8,128)(2,1)S(1)} %constant_dynamic-update-slice_fusion.3.refs_4_.refs_12_), channel_id=1, source_target_pairs={{0,12},{4,0},{8,4},{12,8},{1,13},{5,1},{9,5},{13,9},{2,14},{6,2},{... | collective-permute-start | bytes 2064392 | tf_op jit(solution)/shard_map/ppermute | solution.py:24
  63.6 2.7 %collective-permute-start.1 = (bf16[2,168,512]{2,1,0:T(8,128)(2,1)S(1)}, bf16[2,168,512]{2,1,0:T(8,128)(2,1)S(1)}, u32[]{:S(2)}, u32[]{:S(2)}) collective-permute-start(bf16[2,168,512]{2,1,0:T(8,128)(2,1)S(1)} %bitcast.16), channel_id=1, source_target_pairs={{0,12},{4,0},{8,4},{12,8},{1,13},{5,1},{9,5},{13,9},{2,14},{6,2},{... | collective-permute-start | bytes 1032200 | tf_op jit(solution)/shard_map/ppermute | solution.py:24
  66.4 1.8 fusion
  68.2 8.2 %collective-permute-done.7.refs_6_.refs_14_ = bf16[4,168,512]{2,1,0:T(8,128)(2,1)S(1)} collective-permute-done((bf16[4,168,512]{2,1,0:T(8,128)(2,1)S(1)}, bf16[4,168,512]{2,1,0:T(8,128)(2,1)S(1)}, u32[]{:S(2)}, u32[]{:S(2)}) %collective-permute-start.7) | collective-permute-done | bytes 688160 | tf_op jit(solution)/shard_map/ppermute | solution.py:24
  76.4 3.3 %collective-permute-start.11 = (bf16[2,168,512]{2,1,0:T(8,128)(2,1)S(1)}, bf16[2,168,512]{2,1,0:T(8,128)(2,1)}, u32[]{:S(2)}, u32[]{:S(2)}) collective-permute-start(bf16[2,168,512]{2,1,0:T(8,128)(2,1)S(1)} %collective-permute-done.8.refs_7_.refs_0_.refs_15_), channel_id=1, source_target_pairs={{0,8},{4,12},{8,0},{12,4},{1,9},{5,13},{9,1},{13,5},{2,10},{6,14},... | collective-permute-start | bytes 1032200 | tf_op jit(solution)/shard_map/ppermute | solution.py:24
  79.7 0.8 slice.16
  80.4 1.1 collective-permute-done.6.refs_5_.refs_13_
  81.5 2.9 %collective-permute-start.10 = (bf16[2,168,512]{2,1,0:T(8,128)(2,1)S(1)}, bf16[2,168,512]{2,1,0:T(8,128)(2,1)}, u32[]{:S(2)}, u32[]{:S(2)}) collective-permute-start(bf16[2,168,512]{2,1,0:T(8,128)(2,1)S(1)} %collective-permute-done.8.refs_7_.refs_0_.refs_15_), channel_id=1, source_target_pairs={{0,4},{4,8},{8,12},{12,0},{1,5},{5,9},{9,13},{13,1},{2,6},{6,10},{... | collective-permute-start | bytes 1032200 | tf_op jit(solution)/shard_map/ppermute | solution.py:24
  84.5 0.8 slice.17
  85.2 0.8 copy-done.3
  86.0 2.9 %collective-permute-start.9 = (bf16[2,168,512]{2,1,0:T(8,128)(2,1)S(1)}, bf16[2,168,512]{2,1,0:T(8,128)(2,1)}, u32[]{:S(2)}, u32[]{:S(2)}) collective-permute-start(bf16[2,168,512]{2,1,0:T(8,128)(2,1)S(1)} %collective-permute-done.8.refs_7_.refs_0_.refs_15_), channel_id=1, source_target_pairs={{0,12},{4,0},{8,4},{12,8},{1,13},{5,1},{9,5},{13,9},{2,14},{6,2},{... | collective-permute-start | bytes 1032200 | tf_op jit(solution)/shard_map/ppermute | solution.py:24
  88.9 4.2 %collective-permute-start.12 = (bf16[2,168,512]{2,1,0:T(8,128)(2,1)}, bf16[2,168,512]{2,1,0:T(8,128)(2,1)}, u32[]{:S(2)}, u32[]{:S(2)}) collective-permute-start(bf16[2,168,512]{2,1,0:T(8,128)(2,1)} %slice.16), channel_id=1, source_target_pairs={{0,4},{4,8},{8,12},{12,0},{1,5},{5,9},{9,13},{13,1},{2,6},{6,10},{... | collective-permute-start | bytes 1032200 | tf_op jit(solution)/shard_map/ppermute | solution.py:24
  93.1 0.7 copy-done.6
  93.8 1.9 collective-permute-start.13
  95.7 0.1 broadcast_add_fusion
  95.8 0.1 add.112
  95.9 0.1 pad_add_fusion.place_ref
  96.0 1.3 pad_maximum_fusion
  97.3 0.0 all-gather.2.cloned.1.call-done.weights_ref
  97.3 2.6 %copy-done = bf16[16,2,168,512]{3,2,1,0:T(8,128)(2,1)S(1)} copy-done((bf16[16,2,168,512]{3,2,1,0:T(8,128)(2,1)S(1)}, bf16[16,2,168,512]{3,2,1,0:T(8,128)(2,1)}, u32[]{:S(2)}) %copy-start) | copy-done | bytes 5505048
  99.9 1.0 copy-done.4
  100.8 1.0 copy-done.7
  101.8 2.6 %project.4.refs_6_ = f32[512,256]{1,0:T(8,128)S(1)} custom-call(s32[18]{0:T(128)S(1)} %pad_add_fusion.place_ref, bf16[16,2,168,512]{3,2,1,0:T(8,128)(2,1)S(1)} %copy-done, f32[512,128]{1,0:T(8,128)S(1)} %get-tuple-element.28.cos_ref.refs_6_, f32[512,128]{1,0:T(8,128)S(1)} %get-tuple-element.29.sin_ref.refs_7_, bf16[2,168,512]{2,1,0:T(8,128)(2,1)S(1)} %bitcast.17, ...), custom_call_target="tpu_custom_call" | custom-call | flops 880803840 | bytes 5685248 | tf_op jit(solution)/shard_map/project/pallas_call | solution.py:238
  104.5 4.6 %collective-permute-done.13.refs_12_.refs_5_.refs_20_ = bf16[2,168,512]{2,1,0:T(8,128)(2,1)} collective-permute-done((bf16[2,168,512]{2,1,0:T(8,128)(2,1)}, bf16[2,168,512]{2,1,0:T(8,128)(2,1)}, u32[]{:S(2)}, u32[]{:S(2)}) %collective-permute-start.13) | collective-permute-done | bytes 344096 | tf_op jit(solution)/shard_map/ppermute | solution.py:24
  109.1 2.7 %project.5.own_ref = bf16[2,512,128]{2,1,0:T(8,128)(2,1)S(1)} custom-call(s32[18]{0:T(128)S(1)} %pad_add_fusion.place_ref, bf16[16,2,168,512]{3,2,1,0:T(8,128)(2,1)S(1)} %copy-done, f32[512,128]{1,0:T(8,128)S(1)} %get-tuple-element.28.cos_ref.refs_6_, f32[512,128]{1,0:T(8,128)S(1)} %get-tuple-element.29.sin_ref.refs_7_, ...), custom_call_target="tpu_custom_call" | custom-call | flops 528482304 | bytes 3620864 | tf_op jit(solution)/shard_map/project/pallas_call | solution.py:238
  111.8 1.9 collective-permute-start.15
  113.7 9.2 %collective-permute-start.14 = (bf16[2,512,128]{2,1,0:T(8,128)(2,1)S(1)}, bf16[2,512,128]{2,1,0:T(8,128)(2,1)S(1)}, u32[]{:S(2)}, u32[]{:S(2)}) collective-permute-start(bf16[2,512,128]{2,1,0:T(8,128)(2,1)S(1)} %project.5.own_ref), channel_id=1, source_target_pairs={{0,32},{16,48},{32,64},{48,80},{64,96},{80,112},{96,128},{112,144}... | collective-permute-start | bytes 786440 | tf_op jit(solution)/shard_map/ppermute | solution.py:30
  122.9 0.0 copy-start.9
  122.9 4.0 %project.3.q_ref = bf16[512,256]{1,0:T(8,128)(2,1)S(1)} custom-call(s32[18]{0:T(128)S(1)} %pad_add_fusion.place_ref, bf16[16,2,168,512]{3,2,1,0:T(8,128)(2,1)S(1)} %copy-done.1, f32[512,128]{1,0:T(8,128)S(1)} %get-tuple-element.28.cos_ref.refs_6_, f32[512,128]{1,0:T(8,128)S(1)} %get-tuple-element.29.sin_ref.refs_7_, bf16[2,168,512]{2,1,0:T(8,128)(2,1)S(1)} %bitcast.18, ...), custom_call_target="tpu_custom_call" | custom-call | flops 1409286144 | bytes 8781824 | tf_op jit(solution)/shard_map/project/pallas_call | solution.py:238
  127.0 3.9 %collective-permute-done.14.far_ref = bf16[2,512,128]{2,1,0:T(8,128)(2,1)S(1)} collective-permute-done((bf16[2,512,128]{2,1,0:T(8,128)(2,1)S(1)}, bf16[2,512,128]{2,1,0:T(8,128)(2,1)S(1)}, u32[]{:S(2)}, u32[]{:S(2)}) %collective-permute-start.14) | collective-permute-done | bytes 262176 | tf_op jit(solution)/shard_map/ppermute | solution.py:30
  130.8 5.2 %attention.1 = (bf16[512,256]{1,0:T(8,128)(2,1)}, f32[4,1280,256]{2,1,0:T(8,128)S(1)}, f32[4,1,256]{2,1,0:T(1,128)S(1)}, bf16[512,128]{1,0:T(8,128)(2,1)S(1)}, b...) custom-call(s32[1,512]{1,0:T(1,128)S(1)} %maximum_subtract_fusion.low_ref, bf16[512,256]{1,0:T(8,128)(2,1)S(1)} %project.3.q_ref, ...), custom_call_target="tpu_custom_call" | custom-call | flops 1006632960 | bytes 1048576 | tf_op jit(solution)/shard_map/attention/pallas_call | solution.py:201
  136.1 1.6 key_grad.1
  137.7 1.3 collective-permute-start.16
  139.0 1.3 collective-permute-start.17
  140.3 1.3 collective-permute-start.18
  141.6 1.3 collective-permute-start.19
  142.9 12.5 %collective-permute-done.17.refs_2_ = bf16[512,128]{1,0:T(8,128)(2,1)S(1)} collective-permute-done((bf16[512,128]{1,0:T(8,128)(2,1)S(1)}, bf16[512,128]{1,0:T(8,128)(2,1)S(1)}, u32[]{:S(2)}, u32[]{:S(2)}) %collective-permute-start.17) | collective-permute-done | bytes 131104 | tf_op jit(solution)/shard_map/ppermute | solution.py:30
  155.5 3.5 %collective-permute-done.19.refs_5_ = bf16[512,128]{1,0:T(8,128)(2,1)S(1)} collective-permute-done((bf16[512,128]{1,0:T(8,128)(2,1)S(1)}, bf16[512,128]{1,0:T(8,128)(2,1)S(1)}, u32[]{:S(2)}, u32[]{:S(2)}) %collective-permute-start.19) | collective-permute-done | bytes 131104 | tf_op jit(solution)/shard_map/ppermute | solution.py:30
  159.0 2.5 %weight_grad.3 = bf16[16,168,256]{2,1,0:T(8,128)(2,1)S(1)} custom-call(s32[18]{0:T(128)S(1)} %pad_add_fusion.place_ref, f32[512,128]{1,0:T(8,128)S(1)} %get-tuple-element.15.refs_0_, bf16[512,128]{1,0:T(8,128)(2,1)S(1)} %collective-permute-done.16.refs_1_, bf16[512,128]{1,0:T(8,128)(2,1)S(1)} %collective-permute-done.17.refs_2_, ...), custom_call_target="tpu_custom_call" | custom-call | flops 704643072 | bytes 4390912 | tf_op jit(solution)/shard_map/weight_grad/pallas_call | solution.py:277
  161.5 1.9 collective-permute-start.20
  163.4 2.6 %weight_grad.2 = bf16[16,168,256]{2,1,0:T(8,128)(2,1)S(1)} custom-call(s32[18]{0:T(128)S(1)} %pad_add_fusion.place_ref, f32[512,128]{1,0:T(8,128)S(1)} %get-tuple-element.15.refs_0_, bf16[512,128]{1,0:T(8,128)(2,1)S(1)} %collective-permute-done.16.refs_1_, bf16[512,128]{1,0:T(8,128)(2,1)S(1)} %collective-permute-done.17.refs_2_, ...), custom_call_target="tpu_custom_call" | custom-call | flops 704643072 | bytes 4390912 | tf_op jit(solution)/shard_map/weight_grad/pallas_call | solution.py:277
  166.0 0.5 collective-permute-done.20
  166.5 0.4 add_convert_fusion
  167.0 66.8 %all_to_all.5 = bf16[16,168,256]{2,1,0:T(8,128)(2,1)S(1)} all-to-all(bf16[16,168,256]{2,1,0:T(8,128)(2,1)S(1)} %add_convert_fusion), channel_id=1, replica_groups=mesh['z'=8,'far'=2,'core'=2,'x'=4,'y'=4] {'z','far'}, dimensions={0} | all-to-all | bytes 2752512 | tf_op jit(solution)/shard_map/all_to_all | solution.py:296
  233.8 0.2 reduce_sum.12
  233.9 0.6 fusion.4
  (35 shorter events, 0.2 us)
Async XLA Ops:
  7.2 19.0 %copy-start.2 = (bf16[512,336]{0,1:T(8,128)(2,1)S(1)}, bf16[512,336]{0,1:T(8,128)(2,1)}, u32[]{:S(2)}) copy-start(bf16[512,336]{0,1:T(8,128)(2,1)} %param.6) | copy-start | bytes 1032196
  7.2 34.4 %copy-start.10 = (s32[8]{0:T(128)S(1)}, s32[8]{0:T(128)}, u32[]{:S(2)}) copy-start(s32[8]{0:T(128)} %param.10) | copy-start | bytes 100
  7.2 90.1 %all-gather.2.cloned.1.call-start = ((), (), s32[]{:S(2)}) async-start(), calls=%async_computation.1 | async-start | bytes 5849088 | tf_op jit(solution)/shard_map/all_gather | solution.py:305
  9.8 15.6 %collective-permute-start = (bf16[168,512]{1,0:T(8,128)(2,1)S(1)}, bf16[168,512]{1,0:T(8,128)(2,1)S(1)}, u32[]{:S(2)}, u32[]{:S(2)}) collective-permute-start(bf16[168,512]{1,0:T(8,128)(2,1)S(1)} %constant_dynamic-update-slice_fusion), channel_id=1, source_target_pairs={{0,32},{32,0},{1,33},{33,1},{2,34},{34,2},{3,35},{35,3},{4,36},{36... | collective-permute-start | bytes 516104 | tf_op jit(solution)/shard_map/ppermute | solution.py:24
  26.2 37.4 %collective-permute-start.8 = (bf16[2,168,512]{2,1,0:T(8,128)(2,1)S(1)}, bf16[2,168,512]{2,1,0:T(8,128)(2,1)S(1)}, u32[]{:S(2)}, u32[]{:S(2)}) collective-permute-start(bf16[2,168,512]{2,1,0:T(8,128)(2,1)S(1)} %bitcast.11), channel_id=1, source_target_pairs={{0,2},{1,3},{2,0},{3,1},{4,6},{5,7},{6,4},{7,5},{8,10},{9,11},{10,... | collective-permute-start | bytes 1032200 | tf_op jit(solution)/shard_map/ppermute | solution.py:24
  28.1 29.6 %collective-permute-start.5 = (bf16[2,168,512]{2,1,0:T(8,128)(2,1)S(1)}, bf16[2,168,512]{2,1,0:T(8,128)(2,1)S(1)}, u32[]{:S(2)}, u32[]{:S(2)}) collective-permute-start(bf16[2,168,512]{2,1,0:T(8,128)(2,1)S(1)} %bitcast.12), channel_id=1, source_target_pairs={{0,3},{1,0},{2,1},{3,2},{4,7},{5,4},{6,5},{7,6},{8,11},{9,8},{10,9... | collective-permute-start | bytes 1032200 | tf_op jit(solution)/shard_map/ppermute | solution.py:24
  31.9 25.7 %collective-permute-start.4 = (bf16[2,168,512]{2,1,0:T(8,128)(2,1)S(1)}, bf16[2,168,512]{2,1,0:T(8,128)(2,1)S(1)}, u32[]{:S(2)}, u32[]{:S(2)}) collective-permute-start(bf16[2,168,512]{2,1,0:T(8,128)(2,1)S(1)} %bitcast.13), channel_id=1, source_target_pairs={{0,1},{1,2},{2,3},{3,0},{4,5},{5,6},{6,7},{7,4},{8,9},{9,10},{10,1... | collective-permute-start | bytes 1032200 | tf_op jit(solution)/shard_map/ppermute | solution.py:24
  34.0 51.3 %collective-permute-start.3 = (bf16[2,168,512]{2,1,0:T(8,128)(2,1)S(1)}, bf16[2,168,512]{2,1,0:T(8,128)(2,1)S(1)}, u32[]{:S(2)}, u32[]{:S(2)}) collective-permute-start(bf16[2,168,512]{2,1,0:T(8,128)(2,1)S(1)} %bitcast.14), channel_id=1, source_target_pairs={{0,8},{4,12},{8,0},{12,4},{1,9},{5,13},{9,1},{13,5},{2,10},{6,14},... | collective-permute-start | bytes 1032200 | tf_op jit(solution)/shard_map/ppermute | solution.py:24
  37.3 51.6 %collective-permute-start.2 = (bf16[2,168,512]{2,1,0:T(8,128)(2,1)S(1)}, bf16[2,168,512]{2,1,0:T(8,128)(2,1)}, u32[]{:S(2)}, u32[]{:S(2)}) collective-permute-start(bf16[2,168,512]{2,1,0:T(8,128)(2,1)S(1)} %bitcast.15), channel_id=1, source_target_pairs={{0,4},{4,8},{8,12},{12,0},{1,5},{5,9},{9,13},{13,1},{2,6},{6,10},{... | collective-permute-start | bytes 1032200 | tf_op jit(solution)/shard_map/ppermute | solution.py:24
  57.7 18.7 %collective-permute-start.7 = (bf16[4,168,512]{2,1,0:T(8,128)(2,1)S(1)}, bf16[4,168,512]{2,1,0:T(8,128)(2,1)S(1)}, u32[]{:S(2)}, u32[]{:S(2)}) collective-permute-start(bf16[4,168,512]{2,1,0:T(8,128)(2,1)S(1)} %constant_dynamic-update-slice_fusion.3.refs_4_.refs_12_), channel_id=1, source_target_pairs={{0,4},{4,8},{8,12},{12,0},{1,5},{5,9},{9,13},{13,1},{2,6},{6,10},{... | collective-permute-start | bytes 2064392 | tf_op jit(solution)/shard_map/ppermute | solution.py:24
  60.1 21.4 %collective-permute-start.6 = (bf16[4,168,512]{2,1,0:T(8,128)(2,1)S(1)}, bf16[4,168,512]{2,1,0:T(8,128)(2,1)S(1)}, u32[]{:S(2)}, u32[]{:S(2)}) collective-permute-start(bf16[4,168,512]{2,1,0:T(8,128)(2,1)S(1)} %constant_dynamic-update-slice_fusion.3.refs_4_.refs_12_), channel_id=1, source_target_pairs={{0,12},{4,0},{8,4},{12,8},{1,13},{5,1},{9,5},{13,9},{2,14},{6,2},{... | collective-permute-start | bytes 2064392 | tf_op jit(solution)/shard_map/ppermute | solution.py:24
  63.6 29.5 %collective-permute-start.1 = (bf16[2,168,512]{2,1,0:T(8,128)(2,1)S(1)}, bf16[2,168,512]{2,1,0:T(8,128)(2,1)S(1)}, u32[]{:S(2)}, u32[]{:S(2)}) collective-permute-start(bf16[2,168,512]{2,1,0:T(8,128)(2,1)S(1)} %bitcast.16), channel_id=1, source_target_pairs={{0,12},{4,0},{8,4},{12,8},{1,13},{5,1},{9,5},{13,9},{2,14},{6,2},{... | collective-permute-start | bytes 1032200 | tf_op jit(solution)/shard_map/ppermute | solution.py:24
  76.4 28.1 %collective-permute-start.11 = (bf16[2,168,512]{2,1,0:T(8,128)(2,1)S(1)}, bf16[2,168,512]{2,1,0:T(8,128)(2,1)}, u32[]{:S(2)}, u32[]{:S(2)}) collective-permute-start(bf16[2,168,512]{2,1,0:T(8,128)(2,1)S(1)} %collective-permute-done.8.refs_7_.refs_0_.refs_15_), channel_id=1, source_target_pairs={{0,8},{4,12},{8,0},{12,4},{1,9},{5,13},{9,1},{13,5},{2,10},{6,14},... | collective-permute-start | bytes 1032200 | tf_op jit(solution)/shard_map/ppermute | solution.py:24
  81.5 22.9 %collective-permute-start.10 = (bf16[2,168,512]{2,1,0:T(8,128)(2,1)S(1)}, bf16[2,168,512]{2,1,0:T(8,128)(2,1)}, u32[]{:S(2)}, u32[]{:S(2)}) collective-permute-start(bf16[2,168,512]{2,1,0:T(8,128)(2,1)S(1)} %collective-permute-done.8.refs_7_.refs_0_.refs_15_), channel_id=1, source_target_pairs={{0,4},{4,8},{8,12},{12,0},{1,5},{5,9},{9,13},{13,1},{2,6},{6,10},{... | collective-permute-start | bytes 1032200 | tf_op jit(solution)/shard_map/ppermute | solution.py:24
  85.2 0.8 copy-start.3
  86.0 18.4 %collective-permute-start.9 = (bf16[2,168,512]{2,1,0:T(8,128)(2,1)S(1)}, bf16[2,168,512]{2,1,0:T(8,128)(2,1)}, u32[]{:S(2)}, u32[]{:S(2)}) collective-permute-start(bf16[2,168,512]{2,1,0:T(8,128)(2,1)S(1)} %collective-permute-done.8.refs_7_.refs_0_.refs_15_), channel_id=1, source_target_pairs={{0,12},{4,0},{8,4},{12,8},{1,13},{5,1},{9,5},{13,9},{2,14},{6,2},{... | collective-permute-start | bytes 1032200 | tf_op jit(solution)/shard_map/ppermute | solution.py:24
  88.9 15.6 %collective-permute-start.12 = (bf16[2,168,512]{2,1,0:T(8,128)(2,1)}, bf16[2,168,512]{2,1,0:T(8,128)(2,1)}, u32[]{:S(2)}, u32[]{:S(2)}) collective-permute-start(bf16[2,168,512]{2,1,0:T(8,128)(2,1)} %slice.16), channel_id=1, source_target_pairs={{0,4},{4,8},{8,12},{12,0},{1,5},{5,9},{9,13},{13,1},{2,6},{6,10},{... | collective-permute-start | bytes 1032200 | tf_op jit(solution)/shard_map/ppermute | solution.py:24
  93.1 0.7 copy-start.6
  93.8 15.3 %collective-permute-start.13 = (bf16[2,168,512]{2,1,0:T(8,128)(2,1)}, bf16[2,168,512]{2,1,0:T(8,128)(2,1)}, u32[]{:S(2)}, u32[]{:S(2)}) collective-permute-start(bf16[2,168,512]{2,1,0:T(8,128)(2,1)} %slice.17), channel_id=1, source_target_pairs={{0,12},{4,0},{8,4},{12,8},{1,13},{5,1},{9,5},{13,9},{2,14},{6,2},{... | collective-permute-start | bytes 1032200 | tf_op jit(solution)/shard_map/ppermute | solution.py:24
  97.3 2.6 %copy-start = (bf16[16,2,168,512]{3,2,1,0:T(8,128)(2,1)S(1)}, bf16[16,2,168,512]{3,2,1,0:T(8,128)(2,1)}, u32[]{:S(2)}) copy-start(bf16[16,2,168,512]{3,2,1,0:T(8,128)(2,1)} %all-gather.2.cloned.1.call-done.weights_ref) | copy-start | bytes 16515076
  99.9 1.0 copy-start.4
  100.8 1.0 copy-start.7
  109.1 13.8 %copy-start.1 = (bf16[16,2,168,512]{3,2,1,0:T(8,128)(2,1)S(1)}, bf16[16,2,168,512]{3,2,1,0:T(8,128)(2,1)}, u32[]{:S(2)}) copy-start(bf16[16,2,168,512]{3,2,1,0:T(8,128)(2,1)} %all-gather.2.cloned.1.call-done.weights_ref) | copy-start | bytes 16515076
  111.8 15.2 %collective-permute-start.15 = (bf16[2,512,128]{2,1,0:T(8,128)(2,1)S(1)}, bf16[2,512,128]{2,1,0:T(8,128)(2,1)S(1)}, u32[]{:S(2)}, u32[]{:S(2)}) collective-permute-start(bf16[2,512,128]{2,1,0:T(8,128)(2,1)S(1)} %project.5.own_ref), channel_id=1, source_target_pairs={{0,16},{16,32},{32,48},{48,64},{64,80},{80,96},{96,112},{112,128},... | collective-permute-start | bytes 786440 | tf_op jit(solution)/shard_map/ppermute | solution.py:30
  113.7 17.1 %collective-permute-start.14 = (bf16[2,512,128]{2,1,0:T(8,128)(2,1)S(1)}, bf16[2,512,128]{2,1,0:T(8,128)(2,1)S(1)}, u32[]{:S(2)}, u32[]{:S(2)}) collective-permute-start(bf16[2,512,128]{2,1,0:T(8,128)(2,1)S(1)} %project.5.own_ref), channel_id=1, source_target_pairs={{0,32},{16,48},{32,64},{48,80},{64,96},{80,112},{96,128},{112,144}... | collective-permute-start | bytes 786440 | tf_op jit(solution)/shard_map/ppermute | solution.py:30
  122.9 7.9 %copy-start.9 = (bf16[512,256]{1,0:T(8,128)(2,1)S(1)}, bf16[512,256]{1,0:T(8,128)(2,1)}, u32[]{:S(2)}) copy-start(bf16[512,256]{1,0:T(8,128)(2,1)} %grad_ref.3) | copy-start | bytes 786436
  136.1 22.9 %copy-start.5 = (bf16[2,168,512]{2,1,0:T(8,128)(2,1)S(1)}, bf16[2,168,512]{2,1,0:T(8,128)(2,1)}, u32[]{:S(2)}) copy-start(bf16[2,168,512]{2,1,0:T(8,128)(2,1)} %copy-done.3) | copy-start | bytes 1032196
  136.1 22.9 %copy-start.8 = (bf16[2,168,512]{2,1,0:T(8,128)(2,1)S(1)}, bf16[2,168,512]{2,1,0:T(8,128)(2,1)}, u32[]{:S(2)}) copy-start(bf16[2,168,512]{2,1,0:T(8,128)(2,1)} %copy-done.6) | copy-start | bytes 1032196
  137.7 5.2 %collective-permute-start.16 = (bf16[512,128]{1,0:T(8,128)(2,1)S(1)}, bf16[512,128]{1,0:T(8,128)(2,1)S(1)}, u32[]{:S(2)}, u32[]{:S(2)}) collective-permute-start(bf16[512,128]{1,0:T(8,128)(2,1)S(1)} %get-tuple-element.16), channel_id=1, source_target_pairs={{16,0},{32,16},{48,32},{64,48},{80,64},{96,80},{112,96},{128,112},... | collective-permute-start | bytes 393224 | tf_op jit(solution)/shard_map/ppermute | solution.py:30
  139.0 16.5 %collective-permute-start.17 = (bf16[512,128]{1,0:T(8,128)(2,1)S(1)}, bf16[512,128]{1,0:T(8,128)(2,1)S(1)}, u32[]{:S(2)}, u32[]{:S(2)}) collective-permute-start(bf16[512,128]{1,0:T(8,128)(2,1)S(1)} %get-tuple-element.17), channel_id=1, source_target_pairs={{32,0},{48,16},{64,32},{80,48},{96,64},{112,80},{128,96},{144,112}... | collective-permute-start | bytes 393224 | tf_op jit(solution)/shard_map/ppermute | solution.py:30
  140.3 15.2 %collective-permute-start.18 = (bf16[512,128]{1,0:T(8,128)(2,1)S(1)}, bf16[512,128]{1,0:T(8,128)(2,1)S(1)}, u32[]{:S(2)}, u32[]{:S(2)}) collective-permute-start(bf16[512,128]{1,0:T(8,128)(2,1)S(1)} %get-tuple-element.19), channel_id=1, source_target_pairs={{16,0},{32,16},{48,32},{64,48},{80,64},{96,80},{112,96},{128,112},... | collective-permute-start | bytes 393224 | tf_op jit(solution)/shard_map/ppermute | solution.py:30
  141.6 17.3 %collective-permute-start.19 = (bf16[512,128]{1,0:T(8,128)(2,1)S(1)}, bf16[512,128]{1,0:T(8,128)(2,1)S(1)}, u32[]{:S(2)}, u32[]{:S(2)}) collective-permute-start(bf16[512,128]{1,0:T(8,128)(2,1)S(1)} %get-tuple-element.20), channel_id=1, source_target_pairs={{32,0},{48,16},{64,32},{80,48},{96,64},{112,80},{128,96},{144,112}... | collective-permute-start | bytes 393224 | tf_op jit(solution)/shard_map/ppermute | solution.py:30
  161.5 5.0 %collective-permute-start.20 = (bf16[16,168,256]{2,1,0:T(8,128)(2,1)S(1)}, bf16[16,168,256]{2,1,0:T(8,128)(2,1)S(1)}, u32[]{:S(2)}, u32[]{:S(2)}) collective-permute-start(bf16[16,168,256]{2,1,0:T(8,128)(2,1)S(1)} %weight_grad.3), channel_id=1, source_target_pairs={{0,16},{16,0},{1,17},{17,1},{2,18},{18,2},{3,19},{19,3},{4,20},{20... | collective-permute-start | bytes 4128776 | tf_op jit(solution)/shard_map/ppermute | solution.py:24
Sparse Core Ops, SparseCore 0:
  26.3 51.6 all-gather.1

commit v3 on v1

--- a/solution.py
+++ b/solution.py
@@ -230,7 +230,9 @@
     core = place_ref[16]
     wanted = 1 - core if partner else core
     sums = [
-        own_ref[i] + near_ref[i].astype(jnp.float32) + far_ref[i].astype(jnp.float32)
+        own_ref[i]
+        + jnp.where(core == 0, near_ref[i].astype(jnp.float32), 0.0)
+        + far_ref[i].astype(jnp.float32)
         for i in range(2)
     ]
     grads[:, :HEAD_DIM] = unturned(sums[0], cos_ref[...], sin_ref[...]).astype(jnp.bfloat16)
@@ -323,7 +325,9 @@
         tables,
         (begun,),
     )
-    far, near = passed_along(key_value, 2), passed_along(key_value, 1)
+    core = lax.axis_index("core")
+    far = passed_along(key_value, CORES)
+    near = cycled(jnp.where(core == 0, key_value, far), "core", 1)
     queries = project(
         functools.partial(query_kernel, scale=query_scale),
         jax.ShapeDtypeStruct((tok_rows, query_cols), jnp.bfloat16),
@@ -337,7 +341,9 @@
     attention, far_part, near_part, own_part = attention_call(
         low, queries, far, near, key_value, out_grad
     )
-    far_back, near_back = passed_along(far_part, -2), passed_along(near_part, -1)
+    near_back = cycled(near_part, "core", 1)
+    joined = far_part.astype(jnp.float32) + near_back.astype(jnp.float32)
+    far_back = passed_along(jnp.where(core == 0, far_part, joined.astype(jnp.bfloat16)), -CORES)
     sent, kept = (
         weight_grad(arrays, pieces, place, own_part, near_back, far_back, tables, partner)
         for partner in (True, False)

time: 239 us -> 244 us (1.021)
  local copies, waits for them, and re-layouts: 10.9 us -> 15.4 us
    unnamed x25 -> x29, local copies, waits for them, and re-layouts: 7.79 us -> 12.3 us
    ppermute x15 -> x17, starting transfers between devices: 47 us -> 51.5 us  [cycled(): lax.ppermute(value, axis, [(i, (i + step) % count) for i in range(count)])]
    ppermute x4 -> x2, waiting for transfers between devices: 22.5 us -> 19 us  [passed_along(): return lax.ppermute(block, CTX, route)]
    ppermute x4 -> x2, starting transfers between devices: 13.7 us -> 10.9 us  [passed_along(): return lax.ppermute(block, CTX, route)]
    ppermute x15 -> x17, waiting for transfers between devices: 39.8 us -> 41 us  [cycled(): lax.ppermute(value, axis, [(i, (i + step) % count) for i in range(count)])]
where the time goes in v3:
time: 244 us; the launch traced here: 243 us
  blocking collectives  64.6 us (26%)
  starting transfers between devices  62.4 us (26%)
  waiting for transfers between devices  60 us (25%)
  Pallas kernels  21 us (9%)
  local copies, waits for them, and re-layouts  15.4 us (6%)
  between operations  14.5 us (6%)
  other arithmetic  5.14 us (2%)
    all_to_all x1, blocking collectives, scattered_sum(): landed = lax.all_to_all(chip, ('z', 'far'), 0, 0, tiled=True)  64.6 us
    ppermute x17, starting transfers between devices, cycled(): lax.ppermute(value, axis, [(i, (i + step) % count) for i in range(count)])  51.5 us
    ppermute x17, waiting for transfers between devices, cycled(): lax.ppermute(value, axis, [(i, (i + step) % count) for i in range(count)])  41 us
    ppermute x2, waiting for transfers between devices, passed_along(): return lax.ppermute(block, CTX, route)  19 us
    unnamed x29, local copies, waits for them, and re-layouts  12.3 us
    ppermute x2, starting transfers between devices, passed_along(): return lax.ppermute(block, CTX, route)  10.9 us
    pallas_call x3, Pallas kernels, project(): pl.pallas_call(functools.partial(kernel, pieces, columns), out_shape=out_...  9.16 us
    pallas_call x1, Pallas kernels, attention_call(): pl.pallas_call(attention_kernel, out_shape=(jax.ShapeDtypeStruct((tokens,...  6.72 us
  transfers between devices with their start and end apart: 20, of which 9 were waited for; matrix products, arithmetic and copies ran while one was open for 2% of the time, Pallas kernels for 4%

profile of v3, /device:TPU:22, one launch (start us, length us, event | category | flops | bytes accessed | tf_op | source)
XLA Modules:
  0.0 243.0 jit_solution(2672405033379177178)
XLA Ops:
  7.2 0.0 all-gather.2.cloned.1.call-start
  7.2 0.9 constant_dynamic-update-slice_fusion.2
  8.2 0.8 constant_dynamic-update-slice_fusion.1
  9.0 0.8 constant_dynamic-update-slice_fusion
  9.8 5.9 %collective-permute-start = (bf16[168,512]{1,0:T(8,128)(2,1)S(1)}, bf16[168,512]{1,0:T(8,128)(2,1)S(1)}, u32[]{:S(2)}, u32[]{:S(2)}) collective-permute-start(bf16[168,512]{1,0:T(8,128)(2,1)S(1)} %constant_dynamic-update-slice_fusion), channel_id=1, source_target_pairs={{0,32},{32,0},{1,33},{33,1},{2,34},{34,2},{3,35},{35,3},{4,36},{36... | collective-permute-start | bytes 516104 | tf_op jit(solution)/shard_map/ppermute | solution.py:24
  15.7 9.6 %collective-permute-done = bf16[168,512]{1,0:T(8,128)(2,1)S(1)} collective-permute-done((bf16[168,512]{1,0:T(8,128)(2,1)S(1)}, bf16[168,512]{1,0:T(8,128)(2,1)S(1)}, u32[]{:S(2)}, u32[]{:S(2)}) %collective-permute-start) | collective-permute-done | bytes 172064 | tf_op jit(solution)/shard_map/ppermute | solution.py:24
  25.3 0.8 maximum_select_fusion
  26.1 0.0 all-gather.2.cloned.1.call-update
  26.2 1.9 collective-permute-start.8
  28.1 3.8 %collective-permute-start.5 = (bf16[2,168,512]{2,1,0:T(8,128)(2,1)S(1)}, bf16[2,168,512]{2,1,0:T(8,128)(2,1)S(1)}, u32[]{:S(2)}, u32[]{:S(2)}) collective-permute-start(bf16[2,168,512]{2,1,0:T(8,128)(2,1)S(1)} %bitcast.12), channel_id=1, source_target_pairs={{0,3},{1,0},{2,1},{3,2},{4,7},{5,4},{6,5},{7,6},{8,11},{9,8},{10,9... | collective-permute-start | bytes 1032200 | tf_op jit(solution)/shard_map/ppermute | solution.py:24
  31.9 2.1 collective-permute-start.4
  34.0 3.3 %collective-permute-start.3 = (bf16[2,168,512]{2,1,0:T(8,128)(2,1)S(1)}, bf16[2,168,512]{2,1,0:T(8,128)(2,1)S(1)}, u32[]{:S(2)}, u32[]{:S(2)}) collective-permute-start(bf16[2,168,512]{2,1,0:T(8,128)(2,1)S(1)} %bitcast.14), channel_id=1, source_target_pairs={{0,8},{4,12},{8,0},{12,4},{1,9},{5,13},{9,1},{13,5},{2,10},{6,14},... | collective-permute-start | bytes 1032200 | tf_op jit(solution)/shard_map/ppermute | solution.py:24
  37.3 4.3 %collective-permute-start.2 = (bf16[2,168,512]{2,1,0:T(8,128)(2,1)S(1)}, bf16[2,168,512]{2,1,0:T(8,128)(2,1)}, u32[]{:S(2)}, u32[]{:S(2)}) collective-permute-start(bf16[2,168,512]{2,1,0:T(8,128)(2,1)S(1)} %bitcast.15), channel_id=1, source_target_pairs={{0,4},{4,8},{8,12},{12,0},{1,5},{5,9},{9,13},{13,1},{2,6},{6,10},{... | collective-permute-start | bytes 1032200 | tf_op jit(solution)/shard_map/ppermute | solution.py:24
  41.6 0.2 reduce-window.9
  41.8 0.1 select_reduce_fusion
  41.9 15.7 %collective-permute-done.4 = bf16[2,168,512]{2,1,0:T(8,128)(2,1)S(1)} collective-permute-done((bf16[2,168,512]{2,1,0:T(8,128)(2,1)S(1)}, bf16[2,168,512]{2,1,0:T(8,128)(2,1)S(1)}, u32[]{:S(2)}, u32[]{:S(2)}) %collective-permute-start.4) | collective-permute-done | bytes 344096 | tf_op jit(solution)/shard_map/ppermute | solution.py:24
  57.7 0.0 collective-permute-done.5
  57.7 2.4 collective-permute-start.7
  60.1 3.5 %collective-permute-start.6 = (bf16[4,168,512]{2,1,0:T(8,128)(2,1)S(1)}, bf16[4,168,512]{2,1,0:T(8,128)(2,1)S(1)}, u32[]{:S(2)}, u32[]{:S(2)}) collective-permute-start(bf16[4,168,512]{2,1,0:T(8,128)(2,1)S(1)} %constant_dynamic-update-slice_fusion.3.refs_4_), channel_id=1, source_target_pairs={{0,12},{4,0},{8,4},{12,8},{1,13},{5,1},{9,5},{13,9},{2,14},{6,2},{... | collective-permute-start | bytes 2064392 | tf_op jit(solution)/shard_map/ppermute | solution.py:24
  63.6 2.7 %collective-permute-start.1 = (bf16[2,168,512]{2,1,0:T(8,128)(2,1)S(1)}, bf16[2,168,512]{2,1,0:T(8,128)(2,1)S(1)}, u32[]{:S(2)}, u32[]{:S(2)}) collective-permute-start(bf16[2,168,512]{2,1,0:T(8,128)(2,1)S(1)} %bitcast.16), channel_id=1, source_target_pairs={{0,12},{4,0},{8,4},{12,8},{1,13},{5,1},{9,5},{13,9},{2,14},{6,2},{... | collective-permute-start | bytes 1032200 | tf_op jit(solution)/shard_map/ppermute | solution.py:24
  66.4 1.8 fusion.1
  68.2 8.2 %collective-permute-done.7.refs_6_ = bf16[4,168,512]{2,1,0:T(8,128)(2,1)S(1)} collective-permute-done((bf16[4,168,512]{2,1,0:T(8,128)(2,1)S(1)}, bf16[4,168,512]{2,1,0:T(8,128)(2,1)S(1)}, u32[]{:S(2)}, u32[]{:S(2)}) %collective-permute-start.7) | collective-permute-done | bytes 688160 | tf_op jit(solution)/shard_map/ppermute | solution.py:24
  76.4 3.3 %collective-permute-start.11 = (bf16[2,168,512]{2,1,0:T(8,128)(2,1)S(1)}, bf16[2,168,512]{2,1,0:T(8,128)(2,1)}, u32[]{:S(2)}, u32[]{:S(2)}) collective-permute-start(bf16[2,168,512]{2,1,0:T(8,128)(2,1)S(1)} %collective-permute-done.8.refs_7_.refs_0_), channel_id=1, source_target_pairs={{0,8},{4,12},{8,0},{12,4},{1,9},{5,13},{9,1},{13,5},{2,10},{6,14},... | collective-permute-start | bytes 1032200 | tf_op jit(solution)/shard_map/ppermute | solution.py:24
  79.7 0.8 slice.16
  80.4 1.1 collective-permute-done.6.refs_5_
  81.5 2.9 %collective-permute-start.10 = (bf16[2,168,512]{2,1,0:T(8,128)(2,1)S(1)}, bf16[2,168,512]{2,1,0:T(8,128)(2,1)}, u32[]{:S(2)}, u32[]{:S(2)}) collective-permute-start(bf16[2,168,512]{2,1,0:T(8,128)(2,1)S(1)} %collective-permute-done.8.refs_7_.refs_0_), channel_id=1, source_target_pairs={{0,4},{4,8},{8,12},{12,0},{1,5},{5,9},{9,13},{13,1},{2,6},{6,10},{... | collective-permute-start | bytes 1032200 | tf_op jit(solution)/shard_map/ppermute | solution.py:24
  84.4 0.7 slice.17
  85.2 0.8 copy-done.3
  86.0 2.9 %collective-permute-start.9 = (bf16[2,168,512]{2,1,0:T(8,128)(2,1)S(1)}, bf16[2,168,512]{2,1,0:T(8,128)(2,1)}, u32[]{:S(2)}, u32[]{:S(2)}) collective-permute-start(bf16[2,168,512]{2,1,0:T(8,128)(2,1)S(1)} %collective-permute-done.8.refs_7_.refs_0_), channel_id=1, source_target_pairs={{0,12},{4,0},{8,4},{12,8},{1,13},{5,1},{9,5},{13,9},{2,14},{6,2},{... | collective-permute-start | bytes 1032200 | tf_op jit(solution)/shard_map/ppermute | solution.py:24
  88.9 4.2 %collective-permute-start.12 = (bf16[2,168,512]{2,1,0:T(8,128)(2,1)}, bf16[2,168,512]{2,1,0:T(8,128)(2,1)}, u32[]{:S(2)}, u32[]{:S(2)}) collective-permute-start(bf16[2,168,512]{2,1,0:T(8,128)(2,1)} %slice.16), channel_id=1, source_target_pairs={{0,4},{4,8},{8,12},{12,0},{1,5},{5,9},{9,13},{13,1},{2,6},{6,10},{... | collective-permute-start | bytes 1032200 | tf_op jit(solution)/shard_map/ppermute | solution.py:24
  93.1 0.8 copy-done.7
  93.8 1.9 collective-permute-start.13
  95.7 0.1 broadcast_add_fusion
  95.8 0.1 add.115
  95.9 0.1 pad_add_fusion.place_ref
  96.0 1.3 pad_maximum_fusion
  97.3 0.0 all-gather.2.cloned.1.call-done.weights_ref
  97.3 2.6 %copy-done = bf16[16,2,168,512]{3,2,1,0:T(8,128)(2,1)S(1)} copy-done((bf16[16,2,168,512]{3,2,1,0:T(8,128)(2,1)S(1)}, bf16[16,2,168,512]{3,2,1,0:T(8,128)(2,1)}, u32[]{:S(2)}) %copy-start) | copy-done | bytes 5505048
  99.9 1.0 copy-done.4
  100.9 1.0 copy-done.8
  101.8 2.6 %project.4.refs_6_ = f32[512,256]{1,0:T(8,128)S(1)} custom-call(s32[18]{0:T(128)S(1)} %pad_add_fusion.place_ref, bf16[16,2,168,512]{3,2,1,0:T(8,128)(2,1)S(1)} %copy-done, f32[512,128]{1,0:T(8,128)S(1)} %get-tuple-element.18.cos_ref, f32[512,128]{1,0:T(8,128)S(1)} %get-tuple-element.19.sin_ref, bf16[2,168,512]{2,1,0:T(8,128)(2,1)S(1)} %bitcast.17, ...), custom_call_target="tpu_custom_call" | custom-call | flops 880803840 | bytes 5685248 | tf_op jit(solution)/shard_map/project/pallas_call | solution.py:210
  104.5 4.6 %collective-permute-done.13.refs_12_.refs_5_ = bf16[2,168,512]{2,1,0:T(8,128)(2,1)} collective-permute-done((bf16[2,168,512]{2,1,0:T(8,128)(2,1)}, bf16[2,168,512]{2,1,0:T(8,128)(2,1)}, u32[]{:S(2)}, u32[]{:S(2)}) %collective-permute-start.13) | collective-permute-done | bytes 344096 | tf_op jit(solution)/shard_map/ppermute | solution.py:24
  109.1 2.5 %project.5.own_ref = bf16[2,512,128]{2,1,0:T(8,128)(2,1)S(1)} custom-call(s32[18]{0:T(128)S(1)} %pad_add_fusion.place_ref, bf16[16,2,168,512]{3,2,1,0:T(8,128)(2,1)S(1)} %copy-done, f32[512,128]{1,0:T(8,128)S(1)} %get-tuple-element.18.cos_ref, f32[512,128]{1,0:T(8,128)S(1)} %get-tuple-element.19.sin_ref, ...), custom_call_target="tpu_custom_call" | custom-call | flops 528482304 | bytes 3620864 | tf_op jit(solution)/shard_map/project/pallas_call | solution.py:210
  111.6 9.6 %collective-permute-start.14 = (bf16[2,512,128]{2,1,0:T(8,128)(2,1)S(1)}, bf16[2,512,128]{2,1,0:T(8,128)(2,1)}, u32[]{:S(2)}, u32[]{:S(2)}) collective-permute-start(bf16[2,512,128]{2,1,0:T(8,128)(2,1)S(1)} %project.5.own_ref), channel_id=1, source_target_pairs={{0,32},{16,48},{32,64},{48,80},{64,96},{80,112},{96,128},{112,144}... | collective-permute-start | bytes 786440 | tf_op jit(solution)/shard_map/ppermute | solution.py:30
  121.2 5.1 %collective-permute-done.14.far_ref = bf16[2,512,128]{2,1,0:T(8,128)(2,1)} collective-permute-done((bf16[2,512,128]{2,1,0:T(8,128)(2,1)S(1)}, bf16[2,512,128]{2,1,0:T(8,128)(2,1)}, u32[]{:S(2)}, u32[]{:S(2)}) %collective-permute-start.14) | collective-permute-done | bytes 262176 | tf_op jit(solution)/shard_map/ppermute | solution.py:30
  126.4 2.3 collective-permute-start.15
  128.7 2.6 %copy-done.1 = bf16[16,2,168,512]{3,2,1,0:T(8,128)(2,1)S(1)} copy-done((bf16[16,2,168,512]{3,2,1,0:T(8,128)(2,1)S(1)}, bf16[16,2,168,512]{3,2,1,0:T(8,128)(2,1)}, u32[]{:S(2)}) %copy-start.1) | copy-done | bytes 5505048
  131.2 1.0 copy-done.5
  132.2 1.0 copy-done.9
  133.2 4.1 %project.3.q_ref = bf16[512,256]{1,0:T(8,128)(2,1)S(1)} custom-call(s32[18]{0:T(128)S(1)} %pad_add_fusion.place_ref, bf16[16,2,168,512]{3,2,1,0:T(8,128)(2,1)S(1)} %copy-done.1, f32[512,128]{1,0:T(8,128)S(1)} %get-tuple-element.18.cos_ref, f32[512,128]{1,0:T(8,128)S(1)} %get-tuple-element.19.sin_ref, bf16[2,168,512]{2,1,0:T(8,128)(2,1)S(1)} %bitcast.18, ...), custom_call_target="tpu_custom_call" | custom-call | flops 1409286144 | bytes 8781824 | tf_op jit(solution)/shard_map/project/pallas_call | solution.py:210
  137.3 6.7 %attention.1 = (bf16[512,256]{1,0:T(8,128)(2,1)}, bf16[2,512,128]{2,1,0:T(8,128)(2,1)S(1)}, bf16[2,512,128]{2,1,0:T(8,128)(2,1)S(1)}, f32[2,512,128]{2,1,0:T(8,128)S(1)}) custom-call(s32[1,512]{1,0:T(1,128)S(1)} %maximum_subtract_fusion.low_ref, bf16[512,256]{1,0:T(8,128)(2,1)S(1)} %project.3.q_ref, bf16[2,512,128]{2,1,0:T(8,128)(2,1)} %collective-permute-done.14.far_ref, ...), custom_call_target="tpu_custom_call" | custom-call | flops 1677721600 | bytes 2097152 | tf_op jit(solution)/shard_map/attention/pallas_call | solution.py:180
  144.0 2.2 collective-permute-start.16
  146.3 1.2 collective-permute-done.16.near_ref
  147.4 0.1 fusion
  147.5 1.3 collective-permute-start.17
  148.8 13.9 %collective-permute-done.17.far_ref = bf16[2,512,128]{2,1,0:T(8,128)(2,1)S(1)} collective-permute-done((bf16[2,512,128]{2,1,0:T(8,128)(2,1)S(1)}, bf16[2,512,128]{2,1,0:T(8,128)(2,1)S(1)}, u32[]{:S(2)}, u32[]{:S(2)}) %collective-permute-start.17) | collective-permute-done | bytes 262176 | tf_op jit(solution)/shard_map/ppermute | solution.py:30
  162.7 2.6 %weight_grad.3 = bf16[16,168,256]{2,1,0:T(8,128)(2,1)S(1)} custom-call(s32[18]{0:T(128)S(1)} %pad_add_fusion.place_ref, f32[2,512,128]{2,1,0:T(8,128)S(1)} %get-tuple-element.8.own_ref, bf16[2,512,128]{2,1,0:T(8,128)(2,1)S(1)} %collective-permute-done.16.near_ref, bf16[2,512,128]{2,1,0:T(8,128)(2,1)S(1)} %collective-permute-done.17.far_ref, ...), custom_call_target="tpu_custom_call" | custom-call | flops 704643072 | bytes 4390912 | tf_op jit(solution)/shard_map/weight_grad/pallas_call | solution.py:253
  165.3 1.9 collective-permute-start.18
  167.2 2.6 %weight_grad.2 = bf16[16,168,256]{2,1,0:T(8,128)(2,1)S(1)} custom-call(s32[18]{0:T(128)S(1)} %pad_add_fusion.place_ref, f32[2,512,128]{2,1,0:T(8,128)S(1)} %get-tuple-element.8.own_ref, bf16[2,512,128]{2,1,0:T(8,128)(2,1)S(1)} %collective-permute-done.16.near_ref, bf16[2,512,128]{2,1,0:T(8,128)(2,1)S(1)} %collective-permute-done.17.far_ref, ...), custom_call_target="tpu_custom_call" | custom-call | flops 704643072 | bytes 4390912 | tf_op jit(solution)/shard_map/weight_grad/pallas_call | solution.py:253
  169.8 0.5 collective-permute-done.18
  170.3 0.4 add_convert_fusion
  170.7 64.6 %all_to_all.5 = bf16[16,168,256]{2,1,0:T(8,128)(2,1)S(1)} all-to-all(bf16[16,168,256]{2,1,0:T(8,128)(2,1)S(1)} %add_convert_fusion), channel_id=1, replica_groups=mesh['z'=8,'far'=2,'core'=2,'x'=4,'y'=4] {'z','far'}, dimensions={0} | all-to-all | bytes 2752512 | tf_op jit(solution)/shard_map/all_to_all | solution.py:272
  235.3 0.2 reduce_sum.12
  235.5 0.6 fusion.5
  (36 shorter events, 0.2 us)
Async XLA Ops:
  7.2 19.0 %copy-start.2 = (bf16[512,336]{0,1:T(8,128)(2,1)S(1)}, bf16[512,336]{0,1:T(8,128)(2,1)}, u32[]{:S(2)}) copy-start(bf16[512,336]{0,1:T(8,128)(2,1)} %param.6) | copy-start | bytes 1032196
  7.2 34.4 %copy-start.12 = (s32[8]{0:T(128)S(1)}, s32[8]{0:T(128)}, u32[]{:S(2)}) copy-start(s32[8]{0:T(128)} %param.10) | copy-start | bytes 100
  7.2 90.1 %all-gather.2.cloned.1.call-start = ((), (), s32[]{:S(2)}) async-start(), calls=%async_computation.1 | async-start | bytes 5849088 | tf_op jit(solution)/shard_map/all_gather | solution.py:281
  9.8 15.6 %collective-permute-start = (bf16[168,512]{1,0:T(8,128)(2,1)S(1)}, bf16[168,512]{1,0:T(8,128)(2,1)S(1)}, u32[]{:S(2)}, u32[]{:S(2)}) collective-permute-start(bf16[168,512]{1,0:T(8,128)(2,1)S(1)} %constant_dynamic-update-slice_fusion), channel_id=1, source_target_pairs={{0,32},{32,0},{1,33},{33,1},{2,34},{34,2},{3,35},{35,3},{4,36},{36... | collective-permute-start | bytes 516104 | tf_op jit(solution)/shard_map/ppermute | solution.py:24
  26.2 37.4 %collective-permute-start.8 = (bf16[2,168,512]{2,1,0:T(8,128)(2,1)S(1)}, bf16[2,168,512]{2,1,0:T(8,128)(2,1)S(1)}, u32[]{:S(2)}, u32[]{:S(2)}) collective-permute-start(bf16[2,168,512]{2,1,0:T(8,128)(2,1)S(1)} %bitcast.11), channel_id=1, source_target_pairs={{0,2},{1,3},{2,0},{3,1},{4,6},{5,7},{6,4},{7,5},{8,10},{9,11},{10,... | collective-permute-start | bytes 1032200 | tf_op jit(solution)/shard_map/ppermute | solution.py:24
  28.1 29.6 %collective-permute-start.5 = (bf16[2,168,512]{2,1,0:T(8,128)(2,1)S(1)}, bf16[2,168,512]{2,1,0:T(8,128)(2,1)S(1)}, u32[]{:S(2)}, u32[]{:S(2)}) collective-permute-start(bf16[2,168,512]{2,1,0:T(8,128)(2,1)S(1)} %bitcast.12), channel_id=1, source_target_pairs={{0,3},{1,0},{2,1},{3,2},{4,7},{5,4},{6,5},{7,6},{8,11},{9,8},{10,9... | collective-permute-start | bytes 1032200 | tf_op jit(solution)/shard_map/ppermute | solution.py:24
  31.9 25.7 %collective-permute-start.4 = (bf16[2,168,512]{2,1,0:T(8,128)(2,1)S(1)}, bf16[2,168,512]{2,1,0:T(8,128)(2,1)S(1)}, u32[]{:S(2)}, u32[]{:S(2)}) collective-permute-start(bf16[2,168,512]{2,1,0:T(8,128)(2,1)S(1)} %bitcast.13), channel_id=1, source_target_pairs={{0,1},{1,2},{2,3},{3,0},{4,5},{5,6},{6,7},{7,4},{8,9},{9,10},{10,1... | collective-permute-start | bytes 1032200 | tf_op jit(solution)/shard_map/ppermute | solution.py:24
  34.0 51.2 %collective-permute-start.3 = (bf16[2,168,512]{2,1,0:T(8,128)(2,1)S(1)}, bf16[2,168,512]{2,1,0:T(8,128)(2,1)S(1)}, u32[]{:S(2)}, u32[]{:S(2)}) collective-permute-start(bf16[2,168,512]{2,1,0:T(8,128)(2,1)S(1)} %bitcast.14), channel_id=1, source_target_pairs={{0,8},{4,12},{8,0},{12,4},{1,9},{5,13},{9,1},{13,5},{2,10},{6,14},... | collective-permute-start | bytes 1032200 | tf_op jit(solution)/shard_map/ppermute | solution.py:24
  37.3 51.6 %collective-permute-start.2 = (bf16[2,168,512]{2,1,0:T(8,128)(2,1)S(1)}, bf16[2,168,512]{2,1,0:T(8,128)(2,1)}, u32[]{:S(2)}, u32[]{:S(2)}) collective-permute-start(bf16[2,168,512]{2,1,0:T(8,128)(2,1)S(1)} %bitcast.15), channel_id=1, source_target_pairs={{0,4},{4,8},{8,12},{12,0},{1,5},{5,9},{9,13},{13,1},{2,6},{6,10},{... | collective-permute-start | bytes 1032200 | tf_op jit(solution)/shard_map/ppermute | solution.py:24
  57.7 18.7 %collective-permute-start.7 = (bf16[4,168,512]{2,1,0:T(8,128)(2,1)S(1)}, bf16[4,168,512]{2,1,0:T(8,128)(2,1)S(1)}, u32[]{:S(2)}, u32[]{:S(2)}) collective-permute-start(bf16[4,168,512]{2,1,0:T(8,128)(2,1)S(1)} %constant_dynamic-update-slice_fusion.3.refs_4_), channel_id=1, source_target_pairs={{0,4},{4,8},{8,12},{12,0},{1,5},{5,9},{9,13},{13,1},{2,6},{6,10},{... | collective-permute-start | bytes 2064392 | tf_op jit(solution)/shard_map/ppermute | solution.py:24
  60.1 21.4 %collective-permute-start.6 = (bf16[4,168,512]{2,1,0:T(8,128)(2,1)S(1)}, bf16[4,168,512]{2,1,0:T(8,128)(2,1)S(1)}, u32[]{:S(2)}, u32[]{:S(2)}) collective-permute-start(bf16[4,168,512]{2,1,0:T(8,128)(2,1)S(1)} %constant_dynamic-update-slice_fusion.3.refs_4_), channel_id=1, source_target_pairs={{0,12},{4,0},{8,4},{12,8},{1,13},{5,1},{9,5},{13,9},{2,14},{6,2},{... | collective-permute-start | bytes 2064392 | tf_op jit(solution)/shard_map/ppermute | solution.py:24
  63.6 29.4 %collective-permute-start.1 = (bf16[2,168,512]{2,1,0:T(8,128)(2,1)S(1)}, bf16[2,168,512]{2,1,0:T(8,128)(2,1)S(1)}, u32[]{:S(2)}, u32[]{:S(2)}) collective-permute-start(bf16[2,168,512]{2,1,0:T(8,128)(2,1)S(1)} %bitcast.16), channel_id=1, source_target_pairs={{0,12},{4,0},{8,4},{12,8},{1,13},{5,1},{9,5},{13,9},{2,14},{6,2},{... | collective-permute-start | bytes 1032200 | tf_op jit(solution)/shard_map/ppermute | solution.py:24
  76.4 28.1 %collective-permute-start.11 = (bf16[2,168,512]{2,1,0:T(8,128)(2,1)S(1)}, bf16[2,168,512]{2,1,0:T(8,128)(2,1)}, u32[]{:S(2)}, u32[]{:S(2)}) collective-permute-start(bf16[2,168,512]{2,1,0:T(8,128)(2,1)S(1)} %collective-permute-done.8.refs_7_.refs_0_), channel_id=1, source_target_pairs={{0,8},{4,12},{8,0},{12,4},{1,9},{5,13},{9,1},{13,5},{2,10},{6,14},... | collective-permute-start | bytes 1032200 | tf_op jit(solution)/shard_map/ppermute | solution.py:24
  81.5 22.9 %collective-permute-start.10 = (bf16[2,168,512]{2,1,0:T(8,128)(2,1)S(1)}, bf16[2,168,512]{2,1,0:T(8,128)(2,1)}, u32[]{:S(2)}, u32[]{:S(2)}) collective-permute-start(bf16[2,168,512]{2,1,0:T(8,128)(2,1)S(1)} %collective-permute-done.8.refs_7_.refs_0_), channel_id=1, source_target_pairs={{0,4},{4,8},{8,12},{12,0},{1,5},{5,9},{9,13},{13,1},{2,6},{6,10},{... | collective-permute-start | bytes 1032200 | tf_op jit(solution)/shard_map/ppermute | solution.py:24
  85.2 0.8 copy-start.3
  86.0 18.5 %collective-permute-start.9 = (bf16[2,168,512]{2,1,0:T(8,128)(2,1)S(1)}, bf16[2,168,512]{2,1,0:T(8,128)(2,1)}, u32[]{:S(2)}, u32[]{:S(2)}) collective-permute-start(bf16[2,168,512]{2,1,0:T(8,128)(2,1)S(1)} %collective-permute-done.8.refs_7_.refs_0_), channel_id=1, source_target_pairs={{0,12},{4,0},{8,4},{12,8},{1,13},{5,1},{9,5},{13,9},{2,14},{6,2},{... | collective-permute-start | bytes 1032200 | tf_op jit(solution)/shard_map/ppermute | solution.py:24
  88.9 15.6 %collective-permute-start.12 = (bf16[2,168,512]{2,1,0:T(8,128)(2,1)}, bf16[2,168,512]{2,1,0:T(8,128)(2,1)}, u32[]{:S(2)}, u32[]{:S(2)}) collective-permute-start(bf16[2,168,512]{2,1,0:T(8,128)(2,1)} %slice.16), channel_id=1, source_target_pairs={{0,4},{4,8},{8,12},{12,0},{1,5},{5,9},{9,13},{13,1},{2,6},{6,10},{... | collective-permute-start | bytes 1032200 | tf_op jit(solution)/shard_map/ppermute | solution.py:24
  93.1 0.8 copy-start.7
  93.8 15.3 %collective-permute-start.13 = (bf16[2,168,512]{2,1,0:T(8,128)(2,1)}, bf16[2,168,512]{2,1,0:T(8,128)(2,1)}, u32[]{:S(2)}, u32[]{:S(2)}) collective-permute-start(bf16[2,168,512]{2,1,0:T(8,128)(2,1)} %slice.17), channel_id=1, source_target_pairs={{0,12},{4,0},{8,4},{12,8},{1,13},{5,1},{9,5},{13,9},{2,14},{6,2},{... | collective-permute-start | bytes 1032200 | tf_op jit(solution)/shard_map/ppermute | solution.py:24
  97.3 2.6 %copy-start = (bf16[16,2,168,512]{3,2,1,0:T(8,128)(2,1)S(1)}, bf16[16,2,168,512]{3,2,1,0:T(8,128)(2,1)}, u32[]{:S(2)}) copy-start(bf16[16,2,168,512]{3,2,1,0:T(8,128)(2,1)} %all-gather.2.cloned.1.call-done.weights_ref) | copy-start | bytes 16515076
  99.9 1.0 copy-start.4
  100.9 1.0 copy-start.8
  111.6 14.7 %collective-permute-start.14 = (bf16[2,512,128]{2,1,0:T(8,128)(2,1)S(1)}, bf16[2,512,128]{2,1,0:T(8,128)(2,1)}, u32[]{:S(2)}, u32[]{:S(2)}) collective-permute-start(bf16[2,512,128]{2,1,0:T(8,128)(2,1)S(1)} %project.5.own_ref), channel_id=1, source_target_pairs={{0,32},{16,48},{32,64},{48,80},{64,96},{80,112},{96,128},{112,144}... | collective-permute-start | bytes 786440 | tf_op jit(solution)/shard_map/ppermute | solution.py:30
  126.4 10.9 %collective-permute-start.15 = (bf16[2,512,128]{2,1,0:T(8,128)(2,1)S(1)}, bf16[2,512,128]{2,1,0:T(8,128)(2,1)S(1)}, u32[]{:S(2)}, u32[]{:S(2)}) collective-permute-start(bf16[2,512,128]{2,1,0:T(8,128)(2,1)S(1)} %broadcast_select_fusion), channel_id=1, source_target_pairs={{0,16},{16,0},{1,17},{17,1},{2,18},{18,2},{3,19},{19,3},{4,20},{20... | collective-permute-start | bytes 786440 | tf_op jit(solution)/shard_map/ppermute | solution.py:24
  128.7 2.6 %copy-start.1 = (bf16[16,2,168,512]{3,2,1,0:T(8,128)(2,1)S(1)}, bf16[16,2,168,512]{3,2,1,0:T(8,128)(2,1)}, u32[]{:S(2)}) copy-start(bf16[16,2,168,512]{3,2,1,0:T(8,128)(2,1)} %all-gather.2.cloned.1.call-done.weights_ref) | copy-start | bytes 16515076
  131.2 1.0 copy-start.5
  132.2 1.0 copy-start.9
  133.2 4.1 %copy-start.11 = (bf16[512,256]{1,0:T(8,128)(2,1)S(1)}, bf16[512,256]{1,0:T(8,128)(2,1)}, u32[]{:S(2)}) copy-start(bf16[512,256]{1,0:T(8,128)(2,1)} %grad_ref.1) | copy-start | bytes 786436
  137.3 25.5 %copy-start.6 = (bf16[2,168,512]{2,1,0:T(8,128)(2,1)S(1)}, bf16[2,168,512]{2,1,0:T(8,128)(2,1)}, u32[]{:S(2)}) copy-start(bf16[2,168,512]{2,1,0:T(8,128)(2,1)} %copy-done.3) | copy-start | bytes 1032196
  137.3 25.5 %copy-start.10 = (bf16[2,168,512]{2,1,0:T(8,128)(2,1)S(1)}, bf16[2,168,512]{2,1,0:T(8,128)(2,1)}, u32[]{:S(2)}) copy-start(bf16[2,168,512]{2,1,0:T(8,128)(2,1)} %copy-done.7) | copy-start | bytes 1032196
  144.0 3.4 %collective-permute-start.16 = (bf16[2,512,128]{2,1,0:T(8,128)(2,1)S(1)}, bf16[2,512,128]{2,1,0:T(8,128)(2,1)S(1)}, u32[]{:S(2)}, u32[]{:S(2)}) collective-permute-start(bf16[2,512,128]{2,1,0:T(8,128)(2,1)S(1)} %get-tuple-element.9), channel_id=1, source_target_pairs={{0,16},{16,0},{1,17},{17,1},{2,18},{18,2},{3,19},{19,3},{4,20},{20... | collective-permute-start | bytes 786440 | tf_op jit(solution)/shard_map/ppermute | solution.py:24
  147.5 15.2 %collective-permute-start.17 = (bf16[2,512,128]{2,1,0:T(8,128)(2,1)S(1)}, bf16[2,512,128]{2,1,0:T(8,128)(2,1)S(1)}, u32[]{:S(2)}, u32[]{:S(2)}) collective-permute-start(bf16[2,512,128]{2,1,0:T(8,128)(2,1)S(1)} %fusion), channel_id=1, source_target_pairs={{32,0},{48,16},{64,32},{80,48},{96,64},{112,80},{128,96},{144,112}... | collective-permute-start | bytes 786440 | tf_op jit(solution)/shard_map/ppermute | solution.py:30
  165.3 5.0 %collective-permute-start.18 = (bf16[16,168,256]{2,1,0:T(8,128)(2,1)S(1)}, bf16[16,168,256]{2,1,0:T(8,128)(2,1)S(1)}, u32[]{:S(2)}, u32[]{:S(2)}) collective-permute-start(bf16[16,168,256]{2,1,0:T(8,128)(2,1)S(1)} %weight_grad.3), channel_id=1, source_target_pairs={{0,16},{16,0},{1,17},{17,1},{2,18},{18,2},{3,19},{19,3},{4,20},{20... | collective-permute-start | bytes 4128776 | tf_op jit(solution)/shard_map/ppermute | solution.py:24
Sparse Core Ops, SparseCore 0:
  26.3 51.6 all-gather.1

commit v4 on v3

--- a/solution.py
+++ b/solution.py
@@ -202,6 +202,30 @@
     )(low, queries, far, near, own, grads)
 
 
+def chosen_kernel(place_ref, first_ref, second_ref, out_ref):
+    out_ref[...] = jnp.where(place_ref[16] == 0, first_ref[...], second_ref[...])
+
+
+def joined_kernel(place_ref, far_ref, near_ref, out_ref):
+    near = jnp.where(place_ref[16] == 0, 0.0, near_ref[...].astype(jnp.float32))
+    out_ref[...] = (far_ref[...].astype(jnp.float32) + near).astype(jnp.bfloat16)
+
+
+def on_small_block(kernel, place, first, second):
+    vmem = pl.BlockSpec(memory_space=pltpu.VMEM)
+    return pl.pallas_call(
+        kernel,
+        out_shape=jax.ShapeDtypeStruct(first.shape, first.dtype),
+        in_specs=[pl.BlockSpec(memory_space=pltpu.SMEM), vmem, vmem],
+        out_specs=vmem,
+        compiler_params=pltpu.CompilerParams(vmem_limit_bytes=10 << 20),
+        cost_estimate=pl.CostEstimate(
+            flops=first.size, bytes_accessed=6 * first.size, transcendentals=0
+        ),
+        name="small_block",
+    )(place, first, second)
+
+
 def project(kernel, out_shape, arrays, pieces, columns, place, weights, tables, begun=()):
     tokens = arrays[0].shape[2]
     width = columns[1] - columns[0]
@@ -301,7 +325,7 @@
     query_start = start_of(query_index, starts)
     tables = rope_tables(query_index - query_start)
     low = jnp.maximum(query_start, query_index - (WINDOW - 1)) - (ctx_index - SPAN) * tok_rows
-    low = low.astype(jnp.int32)[None]
+    low, tables = lax.optimization_barrier((low.astype(jnp.int32)[None], tables))
 
     columns = (query_cols, query_cols + 2 * value_cols)
     begun = project(
@@ -325,9 +349,8 @@
         tables,
         (begun,),
     )
-    core = lax.axis_index("core")
     far = passed_along(key_value, CORES)
-    near = cycled(jnp.where(core == 0, key_value, far), "core", 1)
+    near = cycled(on_small_block(chosen_kernel, place, key_value, far), "core", 1)
     queries = project(
         functools.partial(query_kernel, scale=query_scale),
         jax.ShapeDtypeStruct((tok_rows, query_cols), jnp.bfloat16),
@@ -342,8 +365,7 @@
         low, queries, far, near, key_value, out_grad
     )
     near_back = cycled(near_part, "core", 1)
-    joined = far_part.astype(jnp.float32) + near_back.astype(jnp.float32)
-    far_back = passed_along(jnp.where(core == 0, far_part, joined.astype(jnp.bfloat16)), -CORES)
+    far_back = passed_along(on_small_block(joined_kernel, place, far_part, near_back), -CORES)
     sent, kept = (
         weight_grad(arrays, pieces, place, own_part, near_back, far_back, tables, partner)
         for partner in (True, False)

time: 244 us -> 237 us (0.971)
  local copies, waits for them, and re-layouts: 15.4 us -> 10.9 us
  blocking collectives: 64.6 us -> 62.1 us
    unnamed x29 -> x25, local copies, waits for them, and re-layouts: 12.3 us -> 7.8 us
    all_to_all x1, blocking collectives: 64.6 us -> 62.1 us  [scattered_sum(): landed = lax.all_to_all(chip, ('z', 'far'), 0, 0, tiled=True)]
where the time goes in v4:
time: 237 us; the launch traced here: 236 us
  blocking collectives  62.1 us (26%)
  starting transfers between devices  61.8 us (26%)
  waiting for transfers between devices  60.6 us (26%)
  Pallas kernels  21.4 us (9%)
  between operations  14.5 us (6%)
  local copies, waits for them, and re-layouts  10.9 us (5%)
  other arithmetic  5 us (2%)
    all_to_all x1, blocking collectives, scattered_sum(): landed = lax.all_to_all(chip, ('z', 'far'), 0, 0, tiled=True)  62.1 us
    ppermute x17, starting transfers between devices, cycled(): lax.ppermute(value, axis, [(i, (i + step) % count) for i in range(count)])  51.6 us
    ppermute x17, waiting for transfers between devices, cycled(): lax.ppermute(value, axis, [(i, (i + step) % count) for i in range(count)])  40.9 us
    ppermute x2, waiting for transfers between devices, passed_along(): return lax.ppermute(block, CTX, route)  19.7 us
    ppermute x2, starting transfers between devices, passed_along(): return lax.ppermute(block, CTX, route)  10.2 us
    pallas_call x3, Pallas kernels, project(): pl.pallas_call(functools.partial(kernel, pieces, columns), out_shape=out_...  9.3 us
    unnamed x25, local copies, waits for them, and re-layouts  7.8 us
    pallas_call x1, Pallas kernels, attention_call(): pl.pallas_call(attention_kernel, out_shape=(jax.ShapeDtypeStruct((tokens,...  5.73 us
  transfers between devices with their start and end apart: 20, of which 9 were waited for; matrix products, arithmetic and copies ran while one was open for 2% of the time, Pallas kernels for 4%

profile of v4, /device:TPU:22, one launch (start us, length us, event | category | flops | bytes accessed | tf_op | source)
XLA Modules:
  0.0 236.3 jit_solution(8424619755337461292)
XLA Ops:
  7.2 0.0 all-gather.2.cloned.1.call-start
  7.2 0.9 constant_dynamic-update-slice_fusion.2
  8.2 0.8 constant_dynamic-update-slice_fusion.1
  9.0 0.8 constant_dynamic-update-slice_fusion
  9.8 5.9 %collective-permute-start = (bf16[168,512]{1,0:T(8,128)(2,1)S(1)}, bf16[168,512]{1,0:T(8,128)(2,1)S(1)}, u32[]{:S(2)}, u32[]{:S(2)}) collective-permute-start(bf16[168,512]{1,0:T(8,128)(2,1)S(1)} %constant_dynamic-update-slice_fusion), channel_id=1, source_target_pairs={{0,32},{32,0},{1,33},{33,1},{2,34},{34,2},{3,35},{35,3},{4,36},{36... | collective-permute-start | bytes 516104 | tf_op jit(solution)/shard_map/ppermute | solution.py:24
  15.7 9.6 %collective-permute-done = bf16[168,512]{1,0:T(8,128)(2,1)S(1)} collective-permute-done((bf16[168,512]{1,0:T(8,128)(2,1)S(1)}, bf16[168,512]{1,0:T(8,128)(2,1)S(1)}, u32[]{:S(2)}, u32[]{:S(2)}) %collective-permute-start) | collective-permute-done | bytes 172064 | tf_op jit(solution)/shard_map/ppermute | solution.py:24
  25.3 0.8 maximum_select_fusion
  26.1 0.0 all-gather.2.cloned.1.call-update
  26.2 1.9 collective-permute-start.8
  28.1 3.8 %collective-permute-start.5 = (bf16[2,168,512]{2,1,0:T(8,128)(2,1)S(1)}, bf16[2,168,512]{2,1,0:T(8,128)(2,1)S(1)}, u32[]{:S(2)}, u32[]{:S(2)}) collective-permute-start(bf16[2,168,512]{2,1,0:T(8,128)(2,1)S(1)} %bitcast.12), channel_id=1, source_target_pairs={{0,3},{1,0},{2,1},{3,2},{4,7},{5,4},{6,5},{7,6},{8,11},{9,8},{10,9... | collective-permute-start | bytes 1032200 | tf_op jit(solution)/shard_map/ppermute | solution.py:24
  31.9 2.1 collective-permute-start.4
  34.0 3.3 %collective-permute-start.3 = (bf16[2,168,512]{2,1,0:T(8,128)(2,1)S(1)}, bf16[2,168,512]{2,1,0:T(8,128)(2,1)S(1)}, u32[]{:S(2)}, u32[]{:S(2)}) collective-permute-start(bf16[2,168,512]{2,1,0:T(8,128)(2,1)S(1)} %bitcast.14), channel_id=1, source_target_pairs={{0,8},{4,12},{8,0},{12,4},{1,9},{5,13},{9,1},{13,5},{2,10},{6,14},... | collective-permute-start | bytes 1032200 | tf_op jit(solution)/shard_map/ppermute | solution.py:24
  37.3 4.3 %collective-permute-start.2 = (bf16[2,168,512]{2,1,0:T(8,128)(2,1)S(1)}, bf16[2,168,512]{2,1,0:T(8,128)(2,1)}, u32[]{:S(2)}, u32[]{:S(2)}) collective-permute-start(bf16[2,168,512]{2,1,0:T(8,128)(2,1)S(1)} %bitcast.15), channel_id=1, source_target_pairs={{0,4},{4,8},{8,12},{12,0},{1,5},{5,9},{9,13},{13,1},{2,6},{6,10},{... | collective-permute-start | bytes 1032200 | tf_op jit(solution)/shard_map/ppermute | solution.py:24
  41.6 0.2 reduce-window.9
  41.8 0.1 select_reduce_fusion
  41.9 15.7 %collective-permute-done.4 = bf16[2,168,512]{2,1,0:T(8,128)(2,1)S(1)} collective-permute-done((bf16[2,168,512]{2,1,0:T(8,128)(2,1)S(1)}, bf16[2,168,512]{2,1,0:T(8,128)(2,1)S(1)}, u32[]{:S(2)}, u32[]{:S(2)}) %collective-permute-start.4) | collective-permute-done | bytes 344096 | tf_op jit(solution)/shard_map/ppermute | solution.py:24
  57.7 2.4 %collective-permute-start.7 = (bf16[4,168,512]{2,1,0:T(8,128)(2,1)S(1)}, bf16[4,168,512]{2,1,0:T(8,128)(2,1)S(1)}, u32[]{:S(2)}, u32[]{:S(2)}) collective-permute-start(bf16[4,168,512]{2,1,0:T(8,128)(2,1)S(1)} %constant_dynamic-update-slice_fusion.3.refs_4_), channel_id=1, source_target_pairs={{0,4},{4,8},{8,12},{12,0},{1,5},{5,9},{9,13},{13,1},{2,6},{6,10},{... | collective-permute-start | bytes 2064392 | tf_op jit(solution)/shard_map/ppermute | solution.py:24
  60.1 3.5 %collective-permute-start.6 = (bf16[4,168,512]{2,1,0:T(8,128)(2,1)S(1)}, bf16[4,168,512]{2,1,0:T(8,128)(2,1)S(1)}, u32[]{:S(2)}, u32[]{:S(2)}) collective-permute-start(bf16[4,168,512]{2,1,0:T(8,128)(2,1)S(1)} %constant_dynamic-update-slice_fusion.3.refs_4_), channel_id=1, source_target_pairs={{0,12},{4,0},{8,4},{12,8},{1,13},{5,1},{9,5},{13,9},{2,14},{6,2},{... | collective-permute-start | bytes 2064392 | tf_op jit(solution)/shard_map/ppermute | solution.py:24
  63.6 2.7 %collective-permute-start.1 = (bf16[2,168,512]{2,1,0:T(8,128)(2,1)S(1)}, bf16[2,168,512]{2,1,0:T(8,128)(2,1)S(1)}, u32[]{:S(2)}, u32[]{:S(2)}) collective-permute-start(bf16[2,168,512]{2,1,0:T(8,128)(2,1)S(1)} %bitcast.16), channel_id=1, source_target_pairs={{0,12},{4,0},{8,4},{12,8},{1,13},{5,1},{9,5},{13,9},{2,14},{6,2},{... | collective-permute-start | bytes 1032200 | tf_op jit(solution)/shard_map/ppermute | solution.py:24
  66.4 1.8 fusion
  68.2 8.2 %collective-permute-done.7.refs_6_ = bf16[4,168,512]{2,1,0:T(8,128)(2,1)S(1)} collective-permute-done((bf16[4,168,512]{2,1,0:T(8,128)(2,1)S(1)}, bf16[4,168,512]{2,1,0:T(8,128)(2,1)S(1)}, u32[]{:S(2)}, u32[]{:S(2)}) %collective-permute-start.7) | collective-permute-done | bytes 688160 | tf_op jit(solution)/shard_map/ppermute | solution.py:24
  76.3 3.3 %collective-permute-start.11 = (bf16[2,168,512]{2,1,0:T(8,128)(2,1)S(1)}, bf16[2,168,512]{2,1,0:T(8,128)(2,1)}, u32[]{:S(2)}, u32[]{:S(2)}) collective-permute-start(bf16[2,168,512]{2,1,0:T(8,128)(2,1)S(1)} %collective-permute-done.8.refs_7_.refs_0_), channel_id=1, source_target_pairs={{0,8},{4,12},{8,0},{12,4},{1,9},{5,13},{9,1},{13,5},{2,10},{6,14},... | collective-permute-start | bytes 1032200 | tf_op jit(solution)/shard_map/ppermute | solution.py:24
  79.7 0.8 slice.16
  80.4 1.1 collective-permute-done.6.refs_5_
  81.5 2.9 %collective-permute-start.10 = (bf16[2,168,512]{2,1,0:T(8,128)(2,1)S(1)}, bf16[2,168,512]{2,1,0:T(8,128)(2,1)}, u32[]{:S(2)}, u32[]{:S(2)}) collective-permute-start(bf16[2,168,512]{2,1,0:T(8,128)(2,1)S(1)} %collective-permute-done.8.refs_7_.refs_0_), channel_id=1, source_target_pairs={{0,4},{4,8},{8,12},{12,0},{1,5},{5,9},{9,13},{13,1},{2,6},{6,10},{... | collective-permute-start | bytes 1032200 | tf_op jit(solution)/shard_map/ppermute | solution.py:24
  84.4 0.8 slice.17
  85.2 0.0 collective-permute-done.3.refs_3_
  85.2 0.8 copy-done.3
  86.0 2.9 %collective-permute-start.9 = (bf16[2,168,512]{2,1,0:T(8,128)(2,1)S(1)}, bf16[2,168,512]{2,1,0:T(8,128)(2,1)}, u32[]{:S(2)}, u32[]{:S(2)}) collective-permute-start(bf16[2,168,512]{2,1,0:T(8,128)(2,1)S(1)} %collective-permute-done.8.refs_7_.refs_0_), channel_id=1, source_target_pairs={{0,12},{4,0},{8,4},{12,8},{1,13},{5,1},{9,5},{13,9},{2,14},{6,2},{... | collective-permute-start | bytes 1032200 | tf_op jit(solution)/shard_map/ppermute | solution.py:24
  88.9 0.0 collective-permute-done.2.refs_2_
  88.9 4.2 %collective-permute-start.12 = (bf16[2,168,512]{2,1,0:T(8,128)(2,1)}, bf16[2,168,512]{2,1,0:T(8,128)(2,1)}, u32[]{:S(2)}, u32[]{:S(2)}) collective-permute-start(bf16[2,168,512]{2,1,0:T(8,128)(2,1)} %slice.16), channel_id=1, source_target_pairs={{0,4},{4,8},{8,12},{12,0},{1,5},{5,9},{9,13},{13,1},{2,6},{6,10},{... | collective-permute-start | bytes 1032200 | tf_op jit(solution)/shard_map/ppermute | solution.py:24
  93.1 0.0 collective-permute-done.1.refs_1_
  93.1 0.7 copy-done.6
  93.8 1.9 collective-permute-start.13
  95.7 0.1 broadcast_add_fusion
  95.8 0.1 add.112
  95.9 1.3 pad_maximum_fusion
  97.2 0.1 pad_add_fusion.place_ref
  97.3 2.6 %copy-done = bf16[16,2,168,512]{3,2,1,0:T(8,128)(2,1)S(1)} copy-done((bf16[16,2,168,512]{3,2,1,0:T(8,128)(2,1)S(1)}, bf16[16,2,168,512]{3,2,1,0:T(8,128)(2,1)}, u32[]{:S(2)}) %copy-start) | copy-done | bytes 5505048
  99.9 1.0 copy-done.4
  100.8 1.0 copy-done.7
  101.8 2.6 %project.4.refs_6_ = f32[512,256]{1,0:T(8,128)S(1)} custom-call(s32[18]{0:T(128)S(1)} %pad_add_fusion.place_ref, bf16[16,2,168,512]{3,2,1,0:T(8,128)(2,1)S(1)} %copy-done, f32[512,128]{1,0:T(8,128)S(1)} %get-tuple-element.11.cos_ref, f32[512,128]{1,0:T(8,128)S(1)} %get-tuple-element.12.sin_ref, bf16[2,168,512]{2,1,0:T(8,128)(2,1)S(1)} %bitcast.17, ...), custom_call_target="tpu_custom_call" | custom-call | flops 880803840 | bytes 5685248 | tf_op jit(solution)/shard_map/project/pallas_call | solution.py:234
  104.5 4.6 %collective-permute-done.13.refs_12_.refs_5_ = bf16[2,168,512]{2,1,0:T(8,128)(2,1)} collective-permute-done((bf16[2,168,512]{2,1,0:T(8,128)(2,1)}, bf16[2,168,512]{2,1,0:T(8,128)(2,1)}, u32[]{:S(2)}, u32[]{:S(2)}) %collective-permute-start.13) | collective-permute-done | bytes 344096 | tf_op jit(solution)/shard_map/ppermute | solution.py:24
  109.1 2.7 %project.5.first_ref.own_ref = bf16[2,512,128]{2,1,0:T(8,128)(2,1)S(1)} custom-call(s32[18]{0:T(128)S(1)} %pad_add_fusion.place_ref, bf16[16,2,168,512]{3,2,1,0:T(8,128)(2,1)S(1)} %copy-done, f32[512,128]{1,0:T(8,128)S(1)} %get-tuple-element.11.cos_ref, f32[512,128]{1,0:T(8,128)S(1)} %get-tuple-element.12.sin_ref, ...), custom_call_target="tpu_custom_call" | custom-call | flops 528482304 | bytes 3620864 | tf_op jit(solution)/shard_map/project/pallas_call | solution.py:234
  111.8 8.9 %collective-permute-start.14 = (bf16[2,512,128]{2,1,0:T(8,128)(2,1)S(1)}, bf16[2,512,128]{2,1,0:T(8,128)(2,1)S(1)}, u32[]{:S(2)}, u32[]{:S(2)}) collective-permute-start(bf16[2,512,128]{2,1,0:T(8,128)(2,1)S(1)} %project.5.first_ref.own_ref), channel_id=1, source_target_pairs={{0,32},{16,48},{32,64},{48,80},{64,96},{80,112},{96,128},{112,144}... | collective-permute-start | bytes 786440 | tf_op jit(solution)/shard_map/ppermute | solution.py:30
  120.7 5.8 %collective-permute-done.14.second_ref.far_ref = bf16[2,512,128]{2,1,0:T(8,128)(2,1)S(1)} collective-permute-done((bf16[2,512,128]{2,1,0:T(8,128)(2,1)S(1)}, bf16[2,512,128]{2,1,0:T(8,128)(2,1)S(1)}, u32[]{:S(2)}, u32[]{:S(2)}) %collective-permute-start.14) | collective-permute-done | bytes 262176 | tf_op jit(solution)/shard_map/ppermute | solution.py:30
  126.5 0.6 small_block.2
  127.1 0.0 copy-start.9
  127.1 2.2 collective-permute-start.15
  129.3 4.0 %project.3.q_ref = bf16[512,256]{1,0:T(8,128)(2,1)S(1)} custom-call(s32[18]{0:T(128)S(1)} %pad_add_fusion.place_ref, bf16[16,2,168,512]{3,2,1,0:T(8,128)(2,1)S(1)} %copy-done.1, f32[512,128]{1,0:T(8,128)S(1)} %get-tuple-element.11.cos_ref, f32[512,128]{1,0:T(8,128)S(1)} %get-tuple-element.12.sin_ref, bf16[2,168,512]{2,1,0:T(8,128)(2,1)S(1)} %bitcast.18, ...), custom_call_target="tpu_custom_call" | custom-call | flops 1409286144 | bytes 8781824 | tf_op jit(solution)/shard_map/project/pallas_call | solution.py:234
  133.4 5.7 %attention.1 = (bf16[512,256]{1,0:T(8,128)(2,1)}, bf16[2,512,128]{2,1,0:T(8,128)(2,1)S(1)}, bf16[2,512,128]{2,1,0:T(8,128)(2,1)S(1)}, f32[2,512,128]{2,1,0:T(8,128)S(1)}) custom-call(s32[1,512]{1,0:T(1,128)S(1)} %maximum_subtract_fusion.low_ref, bf16[512,256]{1,0:T(8,128)(2,1)S(1)} %project.3.q_ref, ...), custom_call_target="tpu_custom_call" | custom-call | flops 1677721600 | bytes 2097152 | tf_op jit(solution)/shard_map/attention/pallas_call | solution.py:180
  139.2 2.4 %collective-permute-start.16 = (bf16[2,512,128]{2,1,0:T(8,128)(2,1)S(1)}, bf16[2,512,128]{2,1,0:T(8,128)(2,1)S(1)}, u32[]{:S(2)}, u32[]{:S(2)}) collective-permute-start(bf16[2,512,128]{2,1,0:T(8,128)(2,1)S(1)} %get-tuple-element.15), channel_id=1, source_target_pairs={{0,16},{16,0},{1,17},{17,1},{2,18},{18,2},{3,19},{19,3},{4,20},{20... | collective-permute-start | bytes 786440 | tf_op jit(solution)/shard_map/ppermute | solution.py:24
  141.6 1.1 collective-permute-done.16.near_ref
  142.7 0.6 small_block.3
  143.3 1.3 collective-permute-start.17
  144.6 13.8 %collective-permute-done.17.far_ref = bf16[2,512,128]{2,1,0:T(8,128)(2,1)S(1)} collective-permute-done((bf16[2,512,128]{2,1,0:T(8,128)(2,1)S(1)}, bf16[2,512,128]{2,1,0:T(8,128)(2,1)S(1)}, u32[]{:S(2)}, u32[]{:S(2)}) %collective-permute-start.17) | collective-permute-done | bytes 262176 | tf_op jit(solution)/shard_map/ppermute | solution.py:30
  158.5 2.6 %weight_grad.3 = bf16[16,168,256]{2,1,0:T(8,128)(2,1)S(1)} custom-call(s32[18]{0:T(128)S(1)} %pad_add_fusion.place_ref, f32[2,512,128]{2,1,0:T(8,128)S(1)} %get-tuple-element.14.own_ref, bf16[2,512,128]{2,1,0:T(8,128)(2,1)S(1)} %collective-permute-done.16.near_ref, bf16[2,512,128]{2,1,0:T(8,128)(2,1)S(1)} %collective-permute-done.17.far_ref, ...), custom_call_target="tpu_custom_call" | custom-call | flops 704643072 | bytes 4390912 | tf_op jit(solution)/shard_map/weight_grad/pallas_call | solution.py:277
  161.0 1.9 collective-permute-start.18
  163.0 2.6 %weight_grad.2 = bf16[16,168,256]{2,1,0:T(8,128)(2,1)S(1)} custom-call(s32[18]{0:T(128)S(1)} %pad_add_fusion.place_ref, f32[2,512,128]{2,1,0:T(8,128)S(1)} %get-tuple-element.14.own_ref, bf16[2,512,128]{2,1,0:T(8,128)(2,1)S(1)} %collective-permute-done.16.near_ref, bf16[2,512,128]{2,1,0:T(8,128)(2,1)S(1)} %collective-permute-done.17.far_ref, ...), custom_call_target="tpu_custom_call" | custom-call | flops 704643072 | bytes 4390912 | tf_op jit(solution)/shard_map/weight_grad/pallas_call | solution.py:277
  165.5 0.5 collective-permute-done.18
  166.1 0.4 add_convert_fusion
  166.5 62.1 %all_to_all.5 = bf16[16,168,256]{2,1,0:T(8,128)(2,1)S(1)} all-to-all(bf16[16,168,256]{2,1,0:T(8,128)(2,1)S(1)} %add_convert_fusion), channel_id=1, replica_groups=mesh['z'=8,'far'=2,'core'=2,'x'=4,'y'=4] {'z','far'}, dimensions={0} | all-to-all | bytes 2752512 | tf_op jit(solution)/shard_map/all_to_all | solution.py:296
  228.6 0.2 reduce_sum.12
  228.8 0.6 fusion.4
  (32 shorter events, 0.2 us)
Async XLA Ops:
  7.2 19.0 %copy-start.2 = (bf16[512,336]{0,1:T(8,128)(2,1)S(1)}, bf16[512,336]{0,1:T(8,128)(2,1)}, u32[]{:S(2)}) copy-start(bf16[512,336]{0,1:T(8,128)(2,1)} %param.6) | copy-start | bytes 1032196
  7.2 34.4 %copy-start.10 = (s32[8]{0:T(128)S(1)}, s32[8]{0:T(128)}, u32[]{:S(2)}) copy-start(s32[8]{0:T(128)} %param.10) | copy-start | bytes 100
  7.2 90.1 %all-gather.2.cloned.1.call-start = ((), (), s32[]{:S(2)}) async-start(), calls=%async_computation.1 | async-start | bytes 5849088 | tf_op jit(solution)/shard_map/all_gather | solution.py:305
  9.8 15.6 %collective-permute-start = (bf16[168,512]{1,0:T(8,128)(2,1)S(1)}, bf16[168,512]{1,0:T(8,128)(2,1)S(1)}, u32[]{:S(2)}, u32[]{:S(2)}) collective-permute-start(bf16[168,512]{1,0:T(8,128)(2,1)S(1)} %constant_dynamic-update-slice_fusion), channel_id=1, source_target_pairs={{0,32},{32,0},{1,33},{33,1},{2,34},{34,2},{3,35},{35,3},{4,36},{36... | collective-permute-start | bytes 516104 | tf_op jit(solution)/shard_map/ppermute | solution.py:24
  26.2 37.4 %collective-permute-start.8 = (bf16[2,168,512]{2,1,0:T(8,128)(2,1)S(1)}, bf16[2,168,512]{2,1,0:T(8,128)(2,1)S(1)}, u32[]{:S(2)}, u32[]{:S(2)}) collective-permute-start(bf16[2,168,512]{2,1,0:T(8,128)(2,1)S(1)} %bitcast.11), channel_id=1, source_target_pairs={{0,2},{1,3},{2,0},{3,1},{4,6},{5,7},{6,4},{7,5},{8,10},{9,11},{10,... | collective-permute-start | bytes 1032200 | tf_op jit(solution)/shard_map/ppermute | solution.py:24
  28.1 29.6 %collective-permute-start.5 = (bf16[2,168,512]{2,1,0:T(8,128)(2,1)S(1)}, bf16[2,168,512]{2,1,0:T(8,128)(2,1)S(1)}, u32[]{:S(2)}, u32[]{:S(2)}) collective-permute-start(bf16[2,168,512]{2,1,0:T(8,128)(2,1)S(1)} %bitcast.12), channel_id=1, source_target_pairs={{0,3},{1,0},{2,1},{3,2},{4,7},{5,4},{6,5},{7,6},{8,11},{9,8},{10,9... | collective-permute-start | bytes 1032200 | tf_op jit(solution)/shard_map/ppermute | solution.py:24
  31.9 25.7 %collective-permute-start.4 = (bf16[2,168,512]{2,1,0:T(8,128)(2,1)S(1)}, bf16[2,168,512]{2,1,0:T(8,128)(2,1)S(1)}, u32[]{:S(2)}, u32[]{:S(2)}) collective-permute-start(bf16[2,168,512]{2,1,0:T(8,128)(2,1)S(1)} %bitcast.13), channel_id=1, source_target_pairs={{0,1},{1,2},{2,3},{3,0},{4,5},{5,6},{6,7},{7,4},{8,9},{9,10},{10,1... | collective-permute-start | bytes 1032200 | tf_op jit(solution)/shard_map/ppermute | solution.py:24
  34.0 51.3 %collective-permute-start.3 = (bf16[2,168,512]{2,1,0:T(8,128)(2,1)S(1)}, bf16[2,168,512]{2,1,0:T(8,128)(2,1)S(1)}, u32[]{:S(2)}, u32[]{:S(2)}) collective-permute-start(bf16[2,168,512]{2,1,0:T(8,128)(2,1)S(1)} %bitcast.14), channel_id=1, source_target_pairs={{0,8},{4,12},{8,0},{12,4},{1,9},{5,13},{9,1},{13,5},{2,10},{6,14},... | collective-permute-start | bytes 1032200 | tf_op jit(solution)/shard_map/ppermute | solution.py:24
  37.3 51.6 %collective-permute-start.2 = (bf16[2,168,512]{2,1,0:T(8,128)(2,1)S(1)}, bf16[2,168,512]{2,1,0:T(8,128)(2,1)}, u32[]{:S(2)}, u32[]{:S(2)}) collective-permute-start(bf16[2,168,512]{2,1,0:T(8,128)(2,1)S(1)} %bitcast.15), channel_id=1, source_target_pairs={{0,4},{4,8},{8,12},{12,0},{1,5},{5,9},{9,13},{13,1},{2,6},{6,10},{... | collective-permute-start | bytes 1032200 | tf_op jit(solution)/shard_map/ppermute | solution.py:24
  57.7 18.7 %collective-permute-start.7 = (bf16[4,168,512]{2,1,0:T(8,128)(2,1)S(1)}, bf16[4,168,512]{2,1,0:T(8,128)(2,1)S(1)}, u32[]{:S(2)}, u32[]{:S(2)}) collective-permute-start(bf16[4,168,512]{2,1,0:T(8,128)(2,1)S(1)} %constant_dynamic-update-slice_fusion.3.refs_4_), channel_id=1, source_target_pairs={{0,4},{4,8},{8,12},{12,0},{1,5},{5,9},{9,13},{13,1},{2,6},{6,10},{... | collective-permute-start | bytes 2064392 | tf_op jit(solution)/shard_map/ppermute | solution.py:24
  60.1 21.4 %collective-permute-start.6 = (bf16[4,168,512]{2,1,0:T(8,128)(2,1)S(1)}, bf16[4,168,512]{2,1,0:T(8,128)(2,1)S(1)}, u32[]{:S(2)}, u32[]{:S(2)}) collective-permute-start(bf16[4,168,512]{2,1,0:T(8,128)(2,1)S(1)} %constant_dynamic-update-slice_fusion.3.refs_4_), channel_id=1, source_target_pairs={{0,12},{4,0},{8,4},{12,8},{1,13},{5,1},{9,5},{13,9},{2,14},{6,2},{... | collective-permute-start | bytes 2064392 | tf_op jit(solution)/shard_map/ppermute | solution.py:24
  63.6 29.5 %collective-permute-start.1 = (bf16[2,168,512]{2,1,0:T(8,128)(2,1)S(1)}, bf16[2,168,512]{2,1,0:T(8,128)(2,1)S(1)}, u32[]{:S(2)}, u32[]{:S(2)}) collective-permute-start(bf16[2,168,512]{2,1,0:T(8,128)(2,1)S(1)} %bitcast.16), channel_id=1, source_target_pairs={{0,12},{4,0},{8,4},{12,8},{1,13},{5,1},{9,5},{13,9},{2,14},{6,2},{... | collective-permute-start | bytes 1032200 | tf_op jit(solution)/shard_map/ppermute | solution.py:24
  76.3 28.1 %collective-permute-start.11 = (bf16[2,168,512]{2,1,0:T(8,128)(2,1)S(1)}, bf16[2,168,512]{2,1,0:T(8,128)(2,1)}, u32[]{:S(2)}, u32[]{:S(2)}) collective-permute-start(bf16[2,168,512]{2,1,0:T(8,128)(2,1)S(1)} %collective-permute-done.8.refs_7_.refs_0_), channel_id=1, source_target_pairs={{0,8},{4,12},{8,0},{12,4},{1,9},{5,13},{9,1},{13,5},{2,10},{6,14},... | collective-permute-start | bytes 1032200 | tf_op jit(solution)/shard_map/ppermute | solution.py:24
  81.5 22.9 %collective-permute-start.10 = (bf16[2,168,512]{2,1,0:T(8,128)(2,1)S(1)}, bf16[2,168,512]{2,1,0:T(8,128)(2,1)}, u32[]{:S(2)}, u32[]{:S(2)}) collective-permute-start(bf16[2,168,512]{2,1,0:T(8,128)(2,1)S(1)} %collective-permute-done.8.refs_7_.refs_0_), channel_id=1, source_target_pairs={{0,4},{4,8},{8,12},{12,0},{1,5},{5,9},{9,13},{13,1},{2,6},{6,10},{... | collective-permute-start | bytes 1032200 | tf_op jit(solution)/shard_map/ppermute | solution.py:24
  85.2 0.8 copy-start.3
  86.0 18.4 %collective-permute-start.9 = (bf16[2,168,512]{2,1,0:T(8,128)(2,1)S(1)}, bf16[2,168,512]{2,1,0:T(8,128)(2,1)}, u32[]{:S(2)}, u32[]{:S(2)}) collective-permute-start(bf16[2,168,512]{2,1,0:T(8,128)(2,1)S(1)} %collective-permute-done.8.refs_7_.refs_0_), channel_id=1, source_target_pairs={{0,12},{4,0},{8,4},{12,8},{1,13},{5,1},{9,5},{13,9},{2,14},{6,2},{... | collective-permute-start | bytes 1032200 | tf_op jit(solution)/shard_map/ppermute | solution.py:24
  88.9 15.5 %collective-permute-start.12 = (bf16[2,168,512]{2,1,0:T(8,128)(2,1)}, bf16[2,168,512]{2,1,0:T(8,128)(2,1)}, u32[]{:S(2)}, u32[]{:S(2)}) collective-permute-start(bf16[2,168,512]{2,1,0:T(8,128)(2,1)} %slice.16), channel_id=1, source_target_pairs={{0,4},{4,8},{8,12},{12,0},{1,5},{5,9},{9,13},{13,1},{2,6},{6,10},{... | collective-permute-start | bytes 1032200 | tf_op jit(solution)/shard_map/ppermute | solution.py:24
  93.1 0.7 copy-start.6
  93.8 15.3 %collective-permute-start.13 = (bf16[2,168,512]{2,1,0:T(8,128)(2,1)}, bf16[2,168,512]{2,1,0:T(8,128)(2,1)}, u32[]{:S(2)}, u32[]{:S(2)}) collective-permute-start(bf16[2,168,512]{2,1,0:T(8,128)(2,1)} %slice.17), channel_id=1, source_target_pairs={{0,12},{4,0},{8,4},{12,8},{1,13},{5,1},{9,5},{13,9},{2,14},{6,2},{... | collective-permute-start | bytes 1032200 | tf_op jit(solution)/shard_map/ppermute | solution.py:24
  97.3 2.6 %copy-start = (bf16[16,2,168,512]{3,2,1,0:T(8,128)(2,1)S(1)}, bf16[16,2,168,512]{3,2,1,0:T(8,128)(2,1)}, u32[]{:S(2)}) copy-start(bf16[16,2,168,512]{3,2,1,0:T(8,128)(2,1)} %all-gather.2.cloned.1.call-done.weights_ref) | copy-start | bytes 16515076
  99.9 1.0 copy-start.4
  100.8 1.0 copy-start.7
  109.1 20.3 %copy-start.1 = (bf16[16,2,168,512]{3,2,1,0:T(8,128)(2,1)S(1)}, bf16[16,2,168,512]{3,2,1,0:T(8,128)(2,1)}, u32[]{:S(2)}) copy-start(bf16[16,2,168,512]{3,2,1,0:T(8,128)(2,1)} %all-gather.2.cloned.1.call-done.weights_ref) | copy-start | bytes 16515076
  111.8 14.7 %collective-permute-start.14 = (bf16[2,512,128]{2,1,0:T(8,128)(2,1)S(1)}, bf16[2,512,128]{2,1,0:T(8,128)(2,1)S(1)}, u32[]{:S(2)}, u32[]{:S(2)}) collective-permute-start(bf16[2,512,128]{2,1,0:T(8,128)(2,1)S(1)} %project.5.first_ref.own_ref), channel_id=1, source_target_pairs={{0,32},{16,48},{32,64},{48,80},{64,96},{80,112},{96,128},{112,144}... | collective-permute-start | bytes 786440 | tf_op jit(solution)/shard_map/ppermute | solution.py:30
  127.1 6.3 %copy-start.9 = (bf16[512,256]{1,0:T(8,128)(2,1)S(1)}, bf16[512,256]{1,0:T(8,128)(2,1)}, u32[]{:S(2)}) copy-start(bf16[512,256]{1,0:T(8,128)(2,1)} %grad_ref.1) | copy-start | bytes 786436
  127.1 6.3 %collective-permute-start.15 = (bf16[2,512,128]{2,1,0:T(8,128)(2,1)S(1)}, bf16[2,512,128]{2,1,0:T(8,128)(2,1)S(1)}, u32[]{:S(2)}, u32[]{:S(2)}) collective-permute-start(bf16[2,512,128]{2,1,0:T(8,128)(2,1)S(1)} %small_block.2), channel_id=1, source_target_pairs={{0,16},{16,0},{1,17},{17,1},{2,18},{18,2},{3,19},{19,3},{4,20},{20... | collective-permute-start | bytes 786440 | tf_op jit(solution)/shard_map/ppermute | solution.py:24
  133.4 25.1 %copy-start.5 = (bf16[2,168,512]{2,1,0:T(8,128)(2,1)S(1)}, bf16[2,168,512]{2,1,0:T(8,128)(2,1)}, u32[]{:S(2)}) copy-start(bf16[2,168,512]{2,1,0:T(8,128)(2,1)} %copy-done.3) | copy-start | bytes 1032196
  133.4 25.1 %copy-start.8 = (bf16[2,168,512]{2,1,0:T(8,128)(2,1)S(1)}, bf16[2,168,512]{2,1,0:T(8,128)(2,1)}, u32[]{:S(2)}) copy-start(bf16[2,168,512]{2,1,0:T(8,128)(2,1)} %copy-done.6) | copy-start | bytes 1032196
  139.2 3.5 %collective-permute-start.16 = (bf16[2,512,128]{2,1,0:T(8,128)(2,1)S(1)}, bf16[2,512,128]{2,1,0:T(8,128)(2,1)S(1)}, u32[]{:S(2)}, u32[]{:S(2)}) collective-permute-start(bf16[2,512,128]{2,1,0:T(8,128)(2,1)S(1)} %get-tuple-element.15), channel_id=1, source_target_pairs={{0,16},{16,0},{1,17},{17,1},{2,18},{18,2},{3,19},{19,3},{4,20},{20... | collective-permute-start | bytes 786440 | tf_op jit(solution)/shard_map/ppermute | solution.py:24
  143.3 15.1 %collective-permute-start.17 = (bf16[2,512,128]{2,1,0:T(8,128)(2,1)S(1)}, bf16[2,512,128]{2,1,0:T(8,128)(2,1)S(1)}, u32[]{:S(2)}, u32[]{:S(2)}) collective-permute-start(bf16[2,512,128]{2,1,0:T(8,128)(2,1)S(1)} %small_block.3), channel_id=1, source_target_pairs={{32,0},{48,16},{64,32},{80,48},{96,64},{112,80},{128,96},{144,112}... | collective-permute-start | bytes 786440 | tf_op jit(solution)/shard_map/ppermute | solution.py:30
  161.0 5.0 %collective-permute-start.18 = (bf16[16,168,256]{2,1,0:T(8,128)(2,1)S(1)}, bf16[16,168,256]{2,1,0:T(8,128)(2,1)S(1)}, u32[]{:S(2)}, u32[]{:S(2)}) collective-permute-start(bf16[16,168,256]{2,1,0:T(8,128)(2,1)S(1)} %weight_grad.3), channel_id=1, source_target_pairs={{0,16},{16,0},{1,17},{17,1},{2,18},{18,2},{3,19},{19,3},{4,20},{20... | collective-permute-start | bytes 4128776 | tf_op jit(solution)/shard_map/ppermute | solution.py:24
Sparse Core Ops, SparseCore 0:
  26.3 51.6 all-gather.1
